TPU v7x, 512 devices: a whole 4x4x16 slice. The times are simulated.
512 devices in a mesh: sec: 8 (over x, core), xy: 64 (over y, z).
Axes of the slice: x: 4, y: 4, z: 16, core: 2. Of those that a mesh axis runs over, the one named last changes fastest.
Arguments:
- source: bfloat16 [8, 32768, 1024], P('sec', 'xy'), may hold values from -6 to 6
- coarse: int32 [8, 2, 128], P('sec', None, 'xy'), may hold values from -1 to 1, as said below
- fraction: float32 [8, 2, 128], P('sec', None, 'xy'), may hold values from 0.25 to 0.75
- kernel_one: float32 [3, 3, 3], replicated, may hold values from -1.25 to 1.25
- kernel_two: float32 [3, 3, 3], replicated, may hold values from -1.25 to 1.25
Outputs:
- denoised: bfloat16 [8, 1024, 32768], P(None, 'xy', 'sec')
Inputs may be any that keep to these rules, and one draw needn't show every extreme that they name: Destination block (r, c) reads source block (r + coarse[z, 0, b], c + coarse[z, 1, b]); c + coarse[z, 1, b] always lies in 0 to 1. Among the 2 blocks of one block row of a section, at most one has a row offset of -1 and at most one has +1.
All inputs are finite; a program needn't handle non-finite values.
Results may differ from a plain program's by a relative error of at most 0.003.
The roundings to bfloat16 on the way count: a program that leaves them out, or rounds other values in their place, can miss the bound.
Values may be sent and summed in bfloat16 or wider, within the bound.
No kernel may reach another device: no remote copies, remote signals or barrier semaphores. Data moves between devices by JAX's collectives and lax.ppermute only.
A program may use at most 128 MiB of HBM per device.

v0:
```python
import jax
import jax.numpy as jnp
from jax import lax
from jax.sharding import PartitionSpec as P


def from_behind(value, axis, steps):
    count = lax.axis_size(axis)
    first, last = (max(0, -steps), min(count, count - steps))
    return lax.ppermute(value, axis, [(source, source + steps) for source in range(first, last)])


def with_halo(x, sides, width):
    for axis, dim in sides:
        size, length = (lax.axis_size(axis), x.shape[dim])
        up = [(i, (i + 1) % size) for i in range(size - 1)]
        down = [(j, i) for i, j in up]
        last = lax.slice_in_dim(x, length - width, length, axis=dim)
        first = lax.slice_in_dim(x, 0, width, axis=dim)
        before = lax.ppermute(last, axis, up)
        after = lax.ppermute(first, axis, down)
        x = jnp.concatenate([before, x, after], axis=dim)
    return x


def interpolation(shift, edge):
    row_index = lax.broadcasted_iota(jnp.int32, (edge, edge), 0)
    col_index = lax.broadcasted_iota(jnp.int32, (edge, edge), 1)
    offset = col_index - row_index
    amount = shift[..., None, None]
    w_before = ((-0.5 * amount + 1.0) * amount - 0.5) * amount
    w_center = (1.5 * amount - 2.5) * amount * amount + 1.0
    w_after = ((-1.5 * amount + 2.0) * amount + 0.5) * amount
    w_beyond = (0.5 * amount - 0.5) * amount * amount
    matrix = jnp.where(offset == -1, w_before, 0.0) + jnp.where(offset == 0, w_center, 0.0)
    matrix = matrix + jnp.where(offset == 1, w_after, 0.0) + jnp.where(offset == 2, w_beyond, 0.0)
    return matrix.astype(jnp.bfloat16)


def pad_sections(volume):
    return jnp.pad(volume, ((1, 1), (0, 0), (0, 0)))


def stencil(padded, kernel, depth, cols_out, rows_out):
    running = jnp.zeros((depth, cols_out, rows_out), jnp.float32)
    for tap_z in range(3):
        for tap_x in range(3):
            for tap_y in range(3):
                window = padded[
                    tap_z : tap_z + depth, tap_x : tap_x + cols_out, tap_y : tap_y + rows_out
                ]
                running = running + kernel[tap_z, tap_x, tap_y] * window
    return running


def body(source, coarse, fraction, kernel_one, kernel_two):
    sections_dev, edge, width = source.shape
    columns = width // edge
    row_shift = coarse[:, 0, :]
    col_shift = coarse[:, 1, :]
    target = lax.broadcasted_iota(jnp.int32, (sections_dev, columns, columns), 1)
    anchor = lax.broadcasted_iota(jnp.int32, (sections_dev, columns, columns), 2)
    from_above = from_behind(source, "xy", 1)
    from_below = from_behind(source, "xy", -1)
    stacked = jnp.stack([from_above, source, from_below]).reshape(
        3, sections_dev, edge, columns, edge
    )
    level = lax.broadcasted_iota(jnp.int32, (3, sections_dev, columns, columns), 0)
    choose = (row_shift[None, :, :, None] + 1 == level) & (
        target[None] + col_shift[None, :, :, None] == anchor[None]
    )
    picked = jnp.einsum(
        "ksnm,ksimj->snij", choose.astype(jnp.bfloat16), stacked, preferred_element_type=jnp.float32
    ).astype(jnp.bfloat16)
    row_matrix = interpolation(fraction[:, 0, :], edge)
    col_matrix = interpolation(fraction[:, 1, :], edge)
    rows_warped = jnp.einsum(
        "snij,snjk->snik", row_matrix, picked, preferred_element_type=jnp.float32
    ).astype(jnp.bfloat16)
    warped = jnp.einsum(
        "sncj,snrj->sncr", col_matrix, rows_warped, preferred_element_type=jnp.float32
    ).astype(jnp.bfloat16)
    aligned_strip = warped.reshape(sections_dev, width, edge)
    group_data = lax.all_to_all(
        lax.all_to_all(aligned_strip, "xy", split_axis=1, concat_axis=2, tiled=True),
        "sec",
        split_axis=2,
        concat_axis=0,
        tiled=True,
    )
    sections_all, group_cols, group_rows = group_data.shape
    rim_one = with_halo(group_data, (("sec", 2), ("xy", 1)), 1)
    first_pass = jnp.maximum(
        stencil(
            pad_sections(rim_one.astype(jnp.float32)),
            kernel_one,
            sections_all,
            group_cols,
            group_rows,
        ),
        0.0,
    ).astype(jnp.bfloat16)
    rim_two = with_halo(first_pass, (("sec", 2), ("xy", 1)), 1)
    second = stencil(
        pad_sections(rim_two.astype(jnp.float32)), kernel_two, sections_all, group_cols, group_rows
    )
    return (second + group_data.astype(jnp.float32)).astype(jnp.bfloat16)


def solution(mesh):
    placed = (P("sec", "xy", None), P("sec", None, "xy"), P("sec", None, "xy"), P(), P())
    return jax.shard_map(
        body, mesh=mesh, in_specs=placed, out_specs=P(None, "xy", "sec"), check_vma=False
    )
```

profile of v0, /device:TPU:24, one launch (start us, length us, event | category | flops | bytes accessed | tf_op | source)
XLA Modules:
  0.0 501.6 jit_solution(17445958585612541648)
XLA Ops:
  0.0 3.9 collective-permute-start
  4.0 9.7 %collective-permute-start.1 = (bf16[1,512,1024]{2,1,0:T(8,128)(2,1)}, bf16[1,512,1024]{2,1,0:T(8,128)(2,1)S(1)}, u32[]{:S(2)}, u32[]{:S(2)}) collective-permute-start(bf16[1,512,1024]{2,1,0:T(8,128)(2,1)} %param.5), channel_id=1, source_target_pairs={{1,0},{2,1},{3,2},{4,3},{5,4},{6,5},{7,6},{8,7},{9,8},{10,9},{11,1... | collective-permute-start | bytes 3145736 | tf_op jit(solution)/shard_map/ppermute | solution.py:10
  13.6 0.9 fusion.109
  14.5 1.8 stack.13
  16.4 1.0 fusion.111
  17.3 0.0 copy-done.8
  17.3 0.1 iota_compare_fusion.1
  17.4 0.1 fusion.122
  17.5 0.0 copy-done.7
  17.5 17.6 %collective-permute-done = bf16[1,512,1024]{2,1,0:T(8,128)(2,1)S(1)} collective-permute-done((bf16[1,512,1024]{2,1,0:T(8,128)(2,1)}, bf16[1,512,1024]{2,1,0:T(8,128)(2,1)S(1)}, u32[]{:S(2)}, u32[]{:S(2)}) %collective-permute-start) | collective-permute-done | bytes 1048608 | tf_op jit(solution)/shard_map/ppermute | solution.py:10
  35.1 1.6 stack.12
  36.6 0.0 collective-permute-done.1
  36.6 0.8 stack.14
  37.5 8.0 %bitcast_convert_fusion = bf16[2,512,512]{2,0,1:T(2,128)(2,1)} fusion(bf16[1,1,512,2,512]{4,3,0,2,1:T(2,128)(2,1)S(1)} %stack.14, bf16[1,1,512,2,512]{4,3,0,2,1:T(2,128)(2,1)S(1)} %stack.13, bf16[1,1,512,2,512]{4,3,0,2,1:T(2,128)(2,1)} %stack.12, pred[3,2,2]{2,0,1:T(4,128)(4,1)S(1)} %fusion.122), kind=kOutput, calls=%fused_computation.148 | convolution fusion | flops 16252928 | bytes 4194316 | tf_op jit(solution)/shard_map/ksnm,ksimj->snij/dot_general | solution.py:72
  45.4 0.0 copy-done.3
  45.5 3.9 convolution_convert_fusion
  49.4 1.6 copy.28
  51.0 0.5 broadcast.323
  51.5 7.0 %reduce = bf16[1024,512]{1,0:T(8,128)(2,1)S(1)} reduce(bf16[1024,1,512]{2,1,0:T(2,128)(2,1)S(1)} %bitcast.173, bf16[]{:T(256)} %broadcast.323), dimensions={1}, to_apply=%bitcast.165.reduce_sub_computation | reduce | bytes 2097154
  58.6 0.8 reshape.317
  59.4 64.8 %all_to_all.36 = bf16[64,2,4096]{2,1,0:T(2,128)(2,1)S(1)} all-to-all(bf16[64,2,4096]{2,1,0:T(2,128)(2,1)S(1)} %reshape.317), channel_id=1, replica_groups=mesh['sec'=8,'xy'=64] {'xy'}, dimensions={0} | all-to-all | bytes 2097152 | tf_op jit(solution)/shard_map/all_to_all | solution.py:85
  124.1 1.0 reshape.318
  125.2 0.3 copy.19
  125.5 0.1 copy.20
  125.5 25.0 %copy.15 = bf16[1,16,32768]{1,0,2:T(2,128)(2,1)} copy(bf16[1,16,32768]{2,1,0:T(8,128)(2,1)S(1)} %bitcast.175) | data formatting | bytes 2097152 | tf_op jit(solution)/shard_map/all_to_all | solution.py:85
  150.5 179.2 %reduce.1 = bf16[32768,16]{1,0:T(8,128)(2,1)} reduce(bf16[32768,1,16]{2,1,0:T(2,128)(2,1)} %bitcast.168, bf16[]{:T(256)} %broadcast.323), dimensions={1}, to_apply=%bitcast.162.reduce_sub_computation | reduce | bytes 2097154
  329.7 10.4 %reshape.319 = bf16[8,2,32768]{2,1,0:T(2,128)(2,1)S(1)} reshape(bf16[32768,16]{1,0:T(8,128)(2,1)} %reduce.1) | data formatting | bytes 2097152
  340.1 20.2 %all_to_all.37 = bf16[8,2,32768]{2,1,0:T(2,128)(2,1)S(1)} all-to-all(bf16[8,2,32768]{2,1,0:T(2,128)(2,1)S(1)} %reshape.319), channel_id=1, replica_groups=mesh['sec'=8,'xy'=64] {'sec'}, dimensions={0} | all-to-all | bytes 2097152 | tf_op jit(solution)/shard_map/all_to_all | solution.py:84
  360.3 12.2 %reshape.320 = bf16[32768,1,16]{2,1,0:T(2,128)(2,1)} reshape(bf16[8,2,32768]{2,1,0:T(2,128)(2,1)S(1)} %all_to_all.37) | data formatting | bytes 2097152
  372.5 29.6 %copy.16 = bf16[1,16,32768]{2,1,0:T(8,128)(2,1)S(1)} copy(bf16[1,16,32768]{1,0,2:T(2,128)(2,1)} %bitcast.169) | data formatting | bytes 2097152 | tf_op jit(solution)/shard_map/all_to_all | solution.py:84
  402.2 0.0 copy-start.5
  402.2 0.6 copy.21
  402.8 0.1 bitcast_bitcast_fusion
  402.9 0.1 fusion.143
  403.0 1.4 collective-permute-start.2
  404.3 1.3 collective-permute-start.3
  405.7 0.7 fusion.146
  406.4 0.0 collective-permute-done.2
  406.4 1.8 collective-permute-done.3
  408.2 1.6 concatenate.13
  409.8 3.5 collective-permute-start.4
  413.3 4.7 collective-permute-start.5
  418.0 0.7 fusion.147
  418.7 0.0 collective-permute-done.4
  418.7 0.0 copy-done
  418.7 0.9 collective-permute-done.5
  419.6 1.4 maximum_convert_fusion
  421.1 0.0 copy-start.6
  421.1 27.6 %fusion.43 = bf16[8,16,4096]{2,0,1:T(8,128)(2,1)} fusion(f32[8,18,4098]{2,0,1:T(8,128)S(1)} %maximum_convert_fusion, f32[]{:T(128)} %bitcast.41, f32[]{:T(128)} %bitcast.40, f32[]{:T(128)} %bitcast.39, f32[]{:T(128)} %bitcast.38, f32[]{:T(128)} %bitcast.37, f32[]{:T(128)} %bitcast.36, f32[]{:T(128)} %bitcast.35, f32[]{:T(128)} %bitcast.34, f32[]{:T(128)} %bitcast.33, ...), kind=kLoop, calls=%fused_computation.80 | loop fusion | flops 28835840 | bytes 22356076 | tf_op jit(solution)/shard_map/convert_element_type | solution.py:102
  448.7 0.9 fusion.142
  449.5 3.4 collective-permute-start.6
  452.9 1.3 collective-permute-start.7
  454.2 0.7 fusion.144
  455.0 0.0 collective-permute-done.6
  455.0 1.7 collective-permute-done.7
  456.7 2.9 concatenate.15
  459.6 2.7 collective-permute-start.8
  462.3 5.6 %collective-permute-start.9 = (bf16[8,1,4098]{2,0,1:T(8,128)(2,1)S(1)}, bf16[8,1,4098]{2,0,1:T(8,128)(2,1)S(1)}, u32[]{:S(2)}, u32[]{:S(2)}) collective-permute-start(bf16[8,1,4098]{2,0,1:T(8,128)(2,1)S(1)} %get-tuple-element.6), channel_id=1, source_target_pairs={{1,0},{2,1},{3,2},{4,3},{5,4},{6,5},{7,6},{8,7},{9,8},{10,9},{11,1... | collective-permute-start | bytes 196712 | tf_op jit(solution)/shard_map/ppermute | solution.py:21
  467.9 0.7 fusion.145
  468.6 0.0 collective-permute-done.8
  468.6 1.2 collective-permute-done.9
  469.8 1.4 maximum_convert_fusion.1
  471.2 27.6 %fusion.89 = bf16[8,16,4096]{2,0,1:T(8,128)(2,1)} fusion(f32[8,18,4098]{2,0,1:T(8,128)S(1)} %maximum_convert_fusion.1, f32[]{:T(128)} %bitcast.67, f32[]{:T(128)} %bitcast.66, f32[]{:T(128)} %bitcast.65, f32[]{:T(128)} %bitcast.64, f32[]{:T(128)} %bitcast.63, f32[]{:T(128)} %bitcast.62, f32[]{:T(128)} %bitcast.61, f32[]{:T(128)} %bitcast.60, f32[]{:T(128)} %bitcast.59, ...), kind=kLoop, calls=%fused_computation.126 | loop fusion | flops 29360128 | bytes 23404652 | tf_op jit(solution)/shard_map/convert_element_type | solution.py:107
  498.9 2.8 copy.17
  (16 shorter events, 0.1 us)
Async XLA Ops:
  0.0 17.3 %copy-start.8 = (s32[1,2,2]{2,1,0:T(2,128)S(1)}, s32[1,2,2]{2,1,0:T(2,128)}, u32[]{:S(2)}) copy-start(s32[1,2,2]{2,1,0:T(2,128)} %param.6) | copy-start | bytes 52
  0.0 17.5 %copy-start.7 = (f32[1,2,2]{2,1,0:T(2,128)S(1)}, f32[1,2,2]{2,1,0:T(2,128)}, u32[]{:S(2)}) copy-start(f32[1,2,2]{2,1,0:T(2,128)} %param.7) | copy-start | bytes 52
  0.0 35.1 %collective-permute-start = (bf16[1,512,1024]{2,1,0:T(8,128)(2,1)}, bf16[1,512,1024]{2,1,0:T(8,128)(2,1)S(1)}, u32[]{:S(2)}, u32[]{:S(2)}) collective-permute-start(bf16[1,512,1024]{2,1,0:T(8,128)(2,1)} %param.5), channel_id=1, source_target_pairs={{0,1},{1,2},{2,3},{3,4},{4,5},{5,6},{6,7},{7,8},{8,9},{9,10},{10,1... | collective-permute-start | bytes 3145736 | tf_op jit(solution)/shard_map/ppermute | solution.py:10
  4.0 32.7 %collective-permute-start.1 = (bf16[1,512,1024]{2,1,0:T(8,128)(2,1)}, bf16[1,512,1024]{2,1,0:T(8,128)(2,1)S(1)}, u32[]{:S(2)}, u32[]{:S(2)}) collective-permute-start(bf16[1,512,1024]{2,1,0:T(8,128)(2,1)} %param.5), channel_id=1, source_target_pairs={{1,0},{2,1},{3,2},{4,3},{5,4},{6,5},{7,6},{8,7},{9,8},{10,9},{11,1... | collective-permute-start | bytes 3145736 | tf_op jit(solution)/shard_map/ppermute | solution.py:10
  37.4 8.0 %copy-start.2 = (pred[512,512]{1,0:T(8,128)(4,1)S(1)}, pred[512,512]{1,0:T(8,128)(4,1)}, u32[]{:S(2)}) copy-start(pred[512,512]{1,0:T(8,128)(4,1)} %get-tuple-element.78) | copy-start | bytes 786436
  37.4 8.0 %copy-start.3 = (pred[512,512]{1,0:T(8,128)(4,1)S(1)}, pred[512,512]{1,0:T(8,128)(4,1)}, u32[]{:S(2)}) copy-start(pred[512,512]{1,0:T(8,128)(4,1)} %get-tuple-element.79) | copy-start | bytes 786436
  37.4 8.0 %copy-start.4 = (pred[512,512]{1,0:T(8,128)(4,1)S(1)}, pred[512,512]{1,0:T(8,128)(4,1)}, u32[]{:S(2)}) copy-start(pred[512,512]{1,0:T(8,128)(4,1)} %get-tuple-element.80) | copy-start | bytes 786436
  402.2 3.5 copy-start.5
  403.0 3.4 collective-permute-start.2
  404.3 3.8 collective-permute-start.3
  409.7 8.9 %copy-start = (bf16[8,16,4098]{2,0,1:T(8,128)(2,1)}, bf16[8,16,4098]{2,0,1:T(8,128)(2,1)S(1)}, u32[]{:S(2)}) copy-start(bf16[8,16,4098]{2,0,1:T(8,128)(2,1)S(1)} %concatenate.13) | copy-start | bytes 3147268
  409.8 8.9 %collective-permute-start.4 = (bf16[8,1,4098]{2,0,1:T(8,128)(2,1)S(1)}, bf16[8,1,4098]{2,0,1:T(8,128)(2,1)S(1)}, u32[]{:S(2)}, u32[]{:S(2)}) collective-permute-start(bf16[8,1,4098]{2,0,1:T(8,128)(2,1)S(1)} %get-tuple-element.7), channel_id=1, source_target_pairs={{0,1},{1,2},{2,3},{3,4},{4,5},{5,6},{6,7},{7,8},{8,9},{9,10},{10,1... | collective-permute-start | bytes 196712 | tf_op jit(solution)/shard_map/ppermute | solution.py:20
  413.3 6.4 %collective-permute-start.5 = (bf16[8,1,4098]{2,0,1:T(8,128)(2,1)S(1)}, bf16[8,1,4098]{2,0,1:T(8,128)(2,1)S(1)}, u32[]{:S(2)}, u32[]{:S(2)}) collective-permute-start(bf16[8,1,4098]{2,0,1:T(8,128)(2,1)S(1)} %get-tuple-element.8), channel_id=1, source_target_pairs={{1,0},{2,1},{3,2},{4,3},{5,4},{6,5},{7,6},{8,7},{9,8},{10,9},{11,1... | collective-permute-start | bytes 196712 | tf_op jit(solution)/shard_map/ppermute | solution.py:21
  421.1 33.1 %copy-start.6 = (f32[3,3,3]{2,1,0:T(4,128)S(1)}, f32[3,3,3]{2,1,0:T(4,128)}, u32[]{:S(2)}) copy-start(f32[3,3,3]{2,1,0:T(4,128)} %param.9) | copy-start | bytes 328
  449.5 5.4 %collective-permute-start.6 = (bf16[8,16,1]{2,0,1:T(8,128)(2,1)S(1)}, bf16[8,16,1]{2,0,1:T(8,128)(2,1)S(1)}, u32[]{:S(2)}, u32[]{:S(2)}) collective-permute-start(bf16[8,16,1]{2,0,1:T(8,128)(2,1)S(1)} %get-tuple-element.10), channel_id=1, source_target_pairs={{0,64},{64,128},{128,192},{192,256},{256,320},{320,384},{384,448},... | collective-permute-start | bytes 776 | tf_op jit(solution)/shard_map/ppermute | solution.py:20
  452.9 3.7 collective-permute-start.7
  459.5 9.0 %copy-start.1 = (bf16[8,16,4098]{2,0,1:T(8,128)(2,1)}, bf16[8,16,4098]{2,0,1:T(8,128)(2,1)S(1)}, u32[]{:S(2)}) copy-start(bf16[8,16,4098]{2,0,1:T(8,128)(2,1)S(1)} %concatenate.15) | copy-start | bytes 3147268
  459.6 9.0 %collective-permute-start.8 = (bf16[8,1,4098]{2,0,1:T(8,128)(2,1)S(1)}, bf16[8,1,4098]{2,0,1:T(8,128)(2,1)S(1)}, u32[]{:S(2)}, u32[]{:S(2)}) collective-permute-start(bf16[8,1,4098]{2,0,1:T(8,128)(2,1)S(1)} %get-tuple-element.5), channel_id=1, source_target_pairs={{0,1},{1,2},{2,3},{3,4},{4,5},{5,6},{6,7},{7,8},{8,9},{9,10},{10,1... | collective-permute-start | bytes 196712 | tf_op jit(solution)/shard_map/ppermute | solution.py:20
  462.3 7.5 %collective-permute-start.9 = (bf16[8,1,4098]{2,0,1:T(8,128)(2,1)S(1)}, bf16[8,1,4098]{2,0,1:T(8,128)(2,1)S(1)}, u32[]{:S(2)}, u32[]{:S(2)}) collective-permute-start(bf16[8,1,4098]{2,0,1:T(8,128)(2,1)S(1)} %get-tuple-element.6), channel_id=1, source_target_pairs={{1,0},{2,1},{3,2},{4,3},{5,4},{6,5},{7,6},{8,7},{9,8},{10,9},{11,1... | collective-permute-start | bytes 196712 | tf_op jit(solution)/shard_map/ppermute | solution.py:21
where the time goes:
time: 506 us; the launch traced here: 502 us
  other arithmetic  246 us (49%)
  local copies, waits for them, and re-layouts  97.5 us (19%)
  blocking collectives  84.9 us (17%)
  starting transfers between devices  37.5 us (7%)
  waiting for transfers between devices  23.2 us (5%)
  matrix products  11.9 us (2%)
    unnamed x2, other arithmetic  186 us
    all_to_all x1, blocking collectives, body(): lax.all_to_all(aligned_strip, 'xy', split_axis=1, concat_axis=2, tiled=True)  64.8 us
    all_to_all x2, local copies, waits for them, and re-layouts, body(): lax.all_to_all(lax.all_to_all(aligned_strip, 'xy', split_axis=1, concat_a...  29.7 us
    convert_element_type x1, other arithmetic, body(): return (second + group_data.astype(jnp.float32)).astype(jnp.bfloat16)  27.6 us
    convert_element_type x1, other arithmetic, body(): first_pass = jnp.maximum(stencil(pad_sections(rim_one.astype(jnp.float32)...  27.6 us
    unnamed x25, local copies, waits for them, and re-layouts  25.9 us
    all_to_all x2, local copies, waits for them, and re-layouts, body(): lax.all_to_all(aligned_strip, 'xy', split_axis=1, concat_axis=2, tiled=True)  25.1 us
    all_to_all x1, blocking collectives, body(): lax.all_to_all(lax.all_to_all(aligned_strip, 'xy', split_axis=1, concat_a...  20.2 us
  transfers between devices with their start and end apart: 10, of which 5 were waited for; matrix products, arithmetic and copies ran while one was open for 2% of the time, Pallas kernels for 0%

commit v1 on v0

v1 whole, which is shorter than its diff:
```python
import jax
import jax.numpy as jnp
from jax import lax
from jax.experimental import pallas as pl
from jax.experimental.pallas import tpu as pltpu
from jax.sharding import PartitionSpec as P

LANES = 128
HALO = 2
VMEM = pl.BlockSpec(memory_space=pltpu.VMEM)
SMEM = pl.BlockSpec(memory_space=pltpu.SMEM)


def shift_pairs(count, steps):
    first, last = (max(0, -steps), min(count, count - steps))
    return [(source, source + steps) for source in range(first, last)]


def from_behind(value, axis, steps):
    return lax.ppermute(value, axis, shift_pairs(lax.axis_size(axis), steps))


def interpolation(amount, edge):
    row_index = lax.broadcasted_iota(jnp.int32, (edge, edge), 0)
    col_index = lax.broadcasted_iota(jnp.int32, (edge, edge), 1)
    offset = col_index - row_index
    w_before = ((-0.5 * amount + 1.0) * amount - 0.5) * amount
    w_center = (1.5 * amount - 2.5) * amount * amount + 1.0
    w_after = ((-1.5 * amount + 2.0) * amount + 0.5) * amount
    w_beyond = (0.5 * amount - 0.5) * amount * amount
    matrix = jnp.where(offset == -1, w_before, 0.0)
    matrix = jnp.where(offset == 0, w_center, matrix)
    matrix = jnp.where(offset == 1, w_after, matrix)
    return jnp.where(offset == 2, w_beyond, matrix)


def matrices_body(fraction_ref, out_ref):
    _, kinds, columns = fraction_ref.shape
    edge = out_ref.shape[-1]
    for kind in range(kinds):
        for block in range(columns):
            out_ref[kind, block] = interpolation(fraction_ref[0, kind, block], edge).astype(jnp.bfloat16)


def warp_body(coarse_ref, source_ref, above_ref, below_ref, matrix_ref, out_ref):
    _, edge, width = source_ref.shape
    columns = width // edge
    groups = out_ref.shape[0] // columns
    chunks, cols = out_ref.shape[1], out_ref.shape[2]
    for block in range(columns):
        down = coarse_ref[0, 0, block]
        anchor = block + coarse_ref[0, 1, block]
        picked = source_ref[0, :, 0:edge]
        for column in range(1, columns):
            picked = jnp.where(anchor == column, source_ref[0, :, column * edge : (column + 1) * edge], picked)
        picked = jnp.where(down < 0, above_ref[0], picked)
        picked = jnp.where(down > 0, below_ref[0], picked)
        rows_warped = jnp.dot(
            matrix_ref[0, block], picked, preferred_element_type=jnp.float32
        ).astype(jnp.bfloat16)
        warped = lax.dot_general(
            matrix_ref[1, block], rows_warped, (((1,), (1,)), ((), ())), preferred_element_type=jnp.float32
        ).astype(jnp.bfloat16)
        warped = warped.reshape(groups, cols, edge)
        for chunk in range(chunks):
            out_ref[block * groups : (block + 1) * groups, chunk] = warped[
                :, :, chunk * LANES : (chunk + 1) * LANES
            ]


def section_column(index, sections, cols, halo):
    main = sections * cols
    side = sections * halo
    in_main = index < main
    in_left = index < main + side
    left = index - main
    right = index - main - side
    section = jnp.where(in_main, index // cols, jnp.where(in_left, left // halo, right // halo))
    column = jnp.where(in_main, index % cols, jnp.where(in_left, left % halo - halo, right % halo + cols))
    return section, column


def stencil_matrix(kernel_ref, out_ref, sections, cols, halo_out, halo_in):
    _, _, rows_out, rows_in = out_ref.shape
    shape = (rows_out, rows_in)
    out_index = lax.broadcasted_iota(jnp.int32, shape, 0)
    in_index = lax.broadcasted_iota(jnp.int32, shape, 1)
    out_sec, out_col = section_column(out_index, sections, cols, halo_out) if halo_out else (out_index // cols, out_index % cols)
    in_sec, in_col = section_column(in_index, sections, cols, halo_in)
    delta_sec = in_sec - out_sec + 1
    delta_col = in_col - out_col + 1
    delta = jnp.where((delta_col >= 0) & (delta_col < 3), delta_sec * 3 + delta_col, -1)
    for tap_y in range(3):
        value = jnp.zeros(shape, jnp.float32)
        for tap_z in range(3):
            for tap_x in range(3):
                value = jnp.where(delta == tap_z * 3 + tap_x, kernel_ref[tap_z, tap_x, tap_y], value)
        high = value.astype(jnp.bfloat16)
        out_ref[tap_y, 0] = high
        out_ref[tap_y, 1] = (value - high.astype(jnp.float32)).astype(jnp.bfloat16)


def stencils_body(sections, cols, one_ref, two_ref, first_ref, second_ref):
    stencil_matrix(one_ref, first_ref, sections, cols, 1, HALO)
    stencil_matrix(two_ref, second_ref, sections, cols, 0, 1)


def edges_body(data_ref, first_ref, last_ref):
    sections, chunks, cols, lanes = data_ref.shape
    side = sections * HALO
    shape = (side, sections * cols)
    index = lax.broadcasted_iota(jnp.int32, shape, 0)
    source = lax.broadcasted_iota(jnp.int32, shape, 1)
    head = index // HALO * cols + index % HALO
    take_first = jnp.where(source == head, 1.0, 0.0).astype(jnp.bfloat16)
    take_last = jnp.where(source == head + cols - HALO, 1.0, 0.0).astype(jnp.bfloat16)
    for chunk in range(chunks):
        block = data_ref[:, chunk].reshape(sections * cols, lanes)
        where = slice(chunk * lanes, (chunk + 1) * lanes)
        first_ref[:, where] = jnp.dot(take_first, block, preferred_element_type=jnp.float32).astype(jnp.bfloat16)
        last_ref[:, where] = jnp.dot(take_last, block, preferred_element_type=jnp.float32).astype(jnp.bfloat16)


def shifted_sum(matrix_ref, volume):
    def tap(index):
        high = jnp.dot(matrix_ref[index, 0], volume, preferred_element_type=jnp.float32)
        return high + jnp.dot(matrix_ref[index, 1], volume, preferred_element_type=jnp.float32)

    size = volume.shape[1]
    return pltpu.roll(tap(0), 1, 1) + tap(1) + pltpu.roll(tap(2), size - 1, 1)


def denoise_body(place_ref, first_ref, second_ref, data_ref, left_ref, right_ref, out_ref, volume_ref, pass_ref):
    sections, chunks, cols, lanes = data_ref.shape
    main = sections * cols
    side = sections * HALO
    for chunk in range(chunks):
        volume_ref[0:main, chunk * lanes : (chunk + 1) * lanes] = data_ref[:, chunk].reshape(main, lanes)
    volume_ref[main : main + side, :] = left_ref[...]
    volume_ref[main + side : main + 2 * side, :] = right_ref[...]
    length = chunks * lanes
    passed = jnp.maximum(shifted_sum(first_ref, volume_ref[...]), 0.0)
    row = lax.broadcasted_iota(jnp.int32, passed.shape, 0)
    lane = lax.broadcasted_iota(jnp.int32, passed.shape, 1)
    gone = (row >= main) & (row < main + sections) & (place_ref[0] > 0)
    gone = gone | ((row >= main + sections) & (place_ref[1] > 0))
    gone = gone | ((lane < lanes) & (place_ref[2] > 0))
    gone = gone | ((lane >= length - lanes) & (place_ref[3] > 0))
    pass_ref[...] = jnp.where(gone, 0.0, passed).astype(jnp.bfloat16)
    second = shifted_sum(second_ref, pass_ref[...])
    total = second + volume_ref[0:main, :].astype(jnp.float32)
    out_ref[...] = total[:, lanes : length - lanes].astype(jnp.bfloat16).reshape(sections, cols, length - 2 * lanes)


def body(source, coarse, fraction, kernel_one, kernel_two):
    _, edge, width = source.shape
    columns = width // edge
    n_xy, n_sec = lax.axis_size("xy"), lax.axis_size("sec")
    cols = width // n_xy
    chunks = edge // LANES
    bf16 = jnp.bfloat16

    down, anchor = coarse[0, 0], coarse[0, 1] + jnp.arange(columns, dtype=jnp.int32)
    want_above = jnp.sum(jnp.where(down < 0, anchor, 0)).reshape(1, 1)
    want_below = jnp.sum(jnp.where(down > 0, anchor, 0)).reshape(1, 1)
    for_below = from_behind(want_above, "xy", -1)
    for_above = from_behind(want_below, "xy", 1)

    def choose(column):
        block = source[:, :, 0:edge]
        for index in range(1, columns):
            block = jnp.where(column == index, source[:, :, index * edge : (index + 1) * edge], block)
        return block

    above = from_behind(choose(for_below[0, 0]), "xy", 1)
    below = from_behind(choose(for_above[0, 0]), "xy", -1)

    matrix = pl.pallas_call(
        matrices_body,
        out_shape=jax.ShapeDtypeStruct((2, columns, edge, edge), bf16),
        in_specs=[SMEM],
        out_specs=VMEM,
        name="matrices",
    )(fraction)
    main, side = n_sec * cols, n_sec * HALO
    rows_in, rows_mid = main + 2 * side, main + 2 * n_sec
    first, second = pl.pallas_call(
        lambda *refs: stencils_body(n_sec, cols, *refs),
        out_shape=(
            jax.ShapeDtypeStruct((3, 2, rows_mid, rows_in), bf16),
            jax.ShapeDtypeStruct((3, 2, main, rows_mid), bf16),
        ),
        in_specs=[SMEM, SMEM],
        out_specs=(VMEM, VMEM),
        name="stencils",
    )(kernel_one, kernel_two)

    strip = pl.pallas_call(
        warp_body,
        out_shape=jax.ShapeDtypeStruct((n_xy, chunks, cols, LANES), bf16),
        in_specs=[SMEM, VMEM, VMEM, VMEM, VMEM],
        out_specs=VMEM,
        name="warp",
    )(coarse, source, above, below, matrix)

    mine = lax.all_to_all(strip, "xy", split_axis=0, concat_axis=0, tiled=True)
    per_sec = n_xy * chunks // n_sec
    mine = jnp.pad(mine.reshape(n_xy * chunks, cols, LANES), ((1, 1), (0, 0), (0, 0)))
    spread = jnp.stack([mine[index * per_sec : (index + 1) * per_sec + 2] for index in range(n_sec)])
    data = lax.all_to_all(spread, "sec", split_axis=0, concat_axis=0, tiled=True)

    length = (per_sec + 2) * LANES
    firsts, lasts = pl.pallas_call(
        edges_body,
        out_shape=(jax.ShapeDtypeStruct((side, length), bf16),) * 2,
        in_specs=[VMEM],
        out_specs=(VMEM, VMEM),
        name="edges",
    )(data)
    left = from_behind(lasts, "xy", 1)
    right = from_behind(firsts, "xy", -1)

    at_xy, at_sec = lax.axis_index("xy"), lax.axis_index("sec")
    place = jnp.stack([at_xy == 0, at_xy == n_xy - 1, at_sec == 0, at_sec == n_sec - 1]).astype(jnp.int32)
    return pl.pallas_call(
        denoise_body,
        out_shape=jax.ShapeDtypeStruct((n_sec, cols, per_sec * LANES), bf16),
        in_specs=[SMEM, VMEM, VMEM, VMEM, VMEM, VMEM],
        out_specs=VMEM,
        scratch_shapes=[pltpu.VMEM((rows_in, length), bf16), pltpu.VMEM((rows_mid, length), bf16)],
        name="denoise",
    )(place, first, second, data, left, right)


def solution(mesh):
    placed = (P("sec", "xy", None), P("sec", None, "xy"), P("sec", None, "xy"), P(), P())
    return jax.shard_map(
        body, mesh=mesh, in_specs=placed, out_specs=P(None, "xy", "sec"), check_vma=False
    )
```

time: 506 us -> 149 us (0.29)
  other arithmetic: 246 us -> 3.41 us
  local copies, waits for them, and re-layouts: 97.5 us -> 1.61 us
  Pallas kernels: 0 us -> 19.3 us
  waiting for transfers between devices: 23.2 us -> 9.35 us
  matrix products: 11.9 us -> 0 us
  starting transfers between devices: 37.5 us -> 29.6 us
    unnamed x2 -> x0, other arithmetic: 186 us -> none
    convert_element_type x4 -> x1, other arithmetic: 58.1 us -> 0.67 us  [body(): jnp.stack([at_xy == 0, at_xy == n_xy - 1, at_sec == 0, at_sec == n_sec - 1])]
    all_to_all x4 -> x0, local copies, waits for them, and re-layouts: 54.8 us -> none  [the longest x2 29.7 us: body(): lax.all_to_all(lax.all_to_all(aligned_strip, 'xy', split_axis=1, concat_a...]
    unnamed x25 -> x15, local copies, waits for them, and re-layouts: 25.9 us -> 1.59 us
    pallas_call x0 -> x5, Pallas kernels: none -> 19.3 us  [the longest x1 7.2 us: body(): pl.pallas_call(denoise_body, out_shape=jax.ShapeDtypeStruct((n_sec, cols,...]
    ppermute x10 -> x6, waiting for transfers between devices: 23.2 us -> 9.35 us  [from_behind(): return lax.ppermute(value, axis, shift_pairs(lax.axis_size(axis), steps))]
    dot_general x2 -> x0, matrix products: 11.9 us -> none  [the longest x1 7.98 us: body(): jnp.einsum('ksnm,ksimj->snij', choose.astype(jnp.bfloat16), stacked, pref...]
    ppermute x10 -> x6, starting transfers between devices: 37.5 us -> 29.6 us  [from_behind(): return lax.ppermute(value, axis, shift_pairs(lax.axis_size(axis), steps))]
  transfers between devices with their start and end apart: 10 -> 6, of which waited for: 5 -> 4; matrix products, arithmetic and copies ran while one was open for 2% -> 0% of each run, Pallas kernels for 0% -> 3%
where the time goes in v1:
time: 149 us; the launch traced here: 148 us
  blocking collectives  83.4 us (56%)
  starting transfers between devices  29.6 us (20%)
  Pallas kernels  19.3 us (13%)
  waiting for transfers between devices  9.35 us (6%)
  other arithmetic  3.41 us (2%)
  local copies, waits for them, and re-layouts  1.61 us (1%)
    all_to_all x1, blocking collectives, body(): mine = lax.all_to_all(strip, 'xy', split_axis=0, concat_axis=0, tiled=True)  62.4 us
    ppermute x6, starting transfers between devices, from_behind(): return lax.ppermute(value, axis, shift_pairs(lax.axis_size(axis), steps))  29.6 us
    all_to_all x1, blocking collectives, body(): lax.all_to_all(spread, 'sec', split_axis=0, concat_axis=0, tiled=True)  21 us
    ppermute x6, waiting for transfers between devices, from_behind(): return lax.ppermute(value, axis, shift_pairs(lax.axis_size(axis), steps))  9.35 us
    pallas_call x1, Pallas kernels, body(): pl.pallas_call(denoise_body, out_shape=jax.ShapeDtypeStruct((n_sec, cols,...  7.2 us
    pallas_call x1, Pallas kernels, body(): pl.pallas_call(warp_body, out_shape=jax.ShapeDtypeStruct((n_xy, chunks, c...  4.66 us
  transfers between devices with their start and end apart: 6, of which 4 were waited for; matrix products, arithmetic and copies ran while one was open for 0% of the time, Pallas kernels for 3%

profile of v1, /device:TPU:24, one launch (start us, length us, event | category | flops | bytes accessed | tf_op | source)
XLA Modules:
  0.0 148.0 jit_solution(9325906984299696762)
XLA Ops:
  0.0 1.5 fusion.11
  1.5 3.8 %collective-permute-start.2 = (s32[1,1]{1,0:T(1,128)}, s32[1,1]{1,0:T(1,128)}, u32[]{:S(2)}, u32[]{:S(2)}) collective-permute-start(s32[1,1]{1,0:T(1,128)} %bitcast.9), channel_id=1, source_target_pairs={{0,1},{1,2},{2,3},{3,4},{4,5},{5,6},{6,7},{7,8},{8,9},{9,10},{10,1... | collective-permute-start | bytes 20 | tf_op jit(solution)/shard_map/ppermute | solution.py:20
  5.3 9.7 %collective-permute-start = (s32[1,1]{1,0:T(1,128)}, s32[1,1]{1,0:T(1,128)}, u32[]{:S(2)}, u32[]{:S(2)}) collective-permute-start(s32[1,1]{1,0:T(1,128)} %bitcast.6), channel_id=1, source_target_pairs={{1,0},{2,1},{3,2},{4,3},{5,4},{6,5},{7,6},{8,7},{9,8},{10,9},{11,1... | collective-permute-start | bytes 20 | tf_op jit(solution)/shard_map/ppermute | solution.py:20
  15.0 0.0 collective-permute-done.2
  15.6 0.7 collective-permute-done
  16.9 1.3 broadcast_select_fusion
  18.2 1.9 %collective-permute-start.1 = (bf16[1,512,512]{2,1,0:T(8,128)(2,1)S(1)}, bf16[1,512,512]{2,1,0:T(8,128)(2,1)S(1)}, u32[]{:S(2)}, u32[]{:S(2)}) collective-permute-start(bf16[1,512,512]{2,1,0:T(8,128)(2,1)S(1)} %get-tuple-element.16), channel_id=1, source_target_pairs={{0,1},{1,2},{2,3},{3,4},{4,5},{5,6},{6,7},{7,8},{8,9},{9,10},{10,1... | collective-permute-start | bytes 1572872 | tf_op jit(solution)/shard_map/ppermute | solution.py:20
  20.1 6.2 %collective-permute-start.3 = (bf16[1,512,512]{2,1,0:T(8,128)(2,1)S(1)}, bf16[1,512,512]{2,1,0:T(8,128)(2,1)S(1)}, u32[]{:S(2)}, u32[]{:S(2)}) collective-permute-start(bf16[1,512,512]{2,1,0:T(8,128)(2,1)S(1)} %get-tuple-element.15), channel_id=1, source_target_pairs={{1,0},{2,1},{3,2},{4,3},{5,4},{6,5},{7,6},{8,7},{9,8},{10,9},{11,1... | collective-permute-start | bytes 1572872 | tf_op jit(solution)/shard_map/ppermute | solution.py:20
  26.4 2.5 %matrices.1.matrix_ref = bf16[2,2,512,512]{3,2,1,0:T(8,128)(2,1)} custom-call(f32[1,2,2]{2,1,0:T(2,128)} %fraction_ref.1), custom_call_target="tpu_custom_call" | custom-call | tf_op jit(solution)/shard_map/matrices/pallas_call | solution.py:178
  28.8 6.7 %collective-permute-done.1.above_ref = bf16[1,512,512]{2,1,0:T(8,128)(2,1)S(1)} collective-permute-done((bf16[1,512,512]{2,1,0:T(8,128)(2,1)S(1)}, bf16[1,512,512]{2,1,0:T(8,128)(2,1)S(1)}, u32[]{:S(2)}, u32[]{:S(2)}) %collective-permute-start.1) | collective-permute-done | bytes 524320 | tf_op jit(solution)/shard_map/ppermute | solution.py:20
  35.5 0.0 copy-start
  35.5 1.2 collective-permute-done.3.below_ref
  36.7 0.0 copy-done
  36.7 0.0 copy-start.1
  36.7 0.8 copy-done.1
  37.5 4.7 %warp.1 = bf16[64,4,16,128]{3,2,1,0:T(8,128)(2,1)} custom-call(s32[1,2,2]{2,1,0:T(2,128)} %coarse_ref.1, bf16[1,512,1024]{2,1,0:T(8,128)(2,1)} %source_ref.1, bf16[1,512,512]{2,1,0:T(8,128)(2,1)} %copy-done, bf16[1,512,512]{2,1,0:T(8,128)(2,1)} %copy-done.1, bf16[2,2,512,512]{3,2,1,0:T(8,128)(2,1)} %matrices.1.matrix_ref), custom_call_target="tpu_custom_call" | custom-call | tf_op jit(solution)/shard_map/warp/pallas_call | solution.py:198
  42.2 62.4 %all_to_all.10 = bf16[64,4,16,128]{3,2,1,0:T(8,128)(2,1)S(1)} all-to-all(bf16[64,4,16,128]{3,2,1,0:T(8,128)(2,1)} %warp.1), channel_id=1, replica_groups=mesh['sec'=8,'xy'=64] {'xy'}, dimensions={0} | all-to-all | bytes 2097152 | tf_op jit(solution)/shard_map/all_to_all | solution.py:206
  104.7 21.0 %all_to_all.11.data_ref = bf16[8,34,16,128]{3,2,1,0:T(8,128)(2,1)} all-to-all(bf16[8,34,16,128]{3,2,1,0:T(8,128)(2,1)S(1)} %fusion.3), channel_id=1, replica_groups=mesh['sec'=8,'xy'=64] {'sec'}, dimensions={0} | all-to-all | bytes 2228224 | tf_op jit(solution)/shard_map/all_to_all | solution.py:210
  125.8 2.7 %edges.1 = (bf16[16,4352]{1,0:T(8,128)(2,1)}, bf16[16,4352]{1,0:T(8,128)(2,1)}) custom-call(bf16[8,34,16,128]{3,2,1,0:T(8,128)(2,1)} %all_to_all.11.data_ref), custom_call_target="tpu_custom_call" | custom-call | tf_op jit(solution)/shard_map/edges/pallas_call | solution.py:213
  128.4 4.6 %collective-permute-start.4 = (bf16[16,4352]{1,0:T(8,128)(2,1)}, bf16[16,4352]{1,0:T(8,128)(2,1)S(1)}, u32[]{:S(2)}, u32[]{:S(2)}) collective-permute-start(bf16[16,4352]{1,0:T(8,128)(2,1)} %get-tuple-element.11), channel_id=1, source_target_pairs={{0,1},{1,2},{2,3},{3,4},{4,5},{5,6},{6,7},{7,8},{8,9},{9,10},{10,1... | collective-permute-start | bytes 417800 | tf_op jit(solution)/shard_map/ppermute | solution.py:20
  133.0 3.4 %collective-permute-start.5 = (bf16[16,4352]{1,0:T(8,128)(2,1)}, bf16[16,4352]{1,0:T(8,128)(2,1)S(1)}, u32[]{:S(2)}, u32[]{:S(2)}) collective-permute-start(bf16[16,4352]{1,0:T(8,128)(2,1)} %get-tuple-element.12), channel_id=1, source_target_pairs={{1,0},{2,1},{3,2},{4,3},{5,4},{6,5},{7,6},{8,7},{9,8},{10,9},{11,1... | collective-permute-start | bytes 417800 | tf_op jit(solution)/shard_map/ppermute | solution.py:20
  136.4 2.3 %stencils.1 = (bf16[3,2,144,160]{3,2,1,0:T(8,128)(2,1)}, bf16[3,2,128,144]{3,2,1,0:T(8,128)(2,1)}) custom-call(f32[3,3,3]{2,1,0:T(4,128)} %refs_0_.1, f32[3,3,3]{2,1,0:T(4,128)} %refs_1_.1), custom_call_target="tpu_custom_call" | custom-call | tf_op jit(solution)/shard_map/stencils/pallas_call | solution.py:187
  138.7 0.7 add_convert_fusion.place_ref
  139.3 0.0 collective-permute-done.4.left_ref
  139.3 0.0 copy-start.2
  139.3 0.8 collective-permute-done.5.right_ref
  140.1 0.0 copy-start.3
  140.1 0.0 copy-done.2
  140.1 0.6 copy-done.3
  140.8 7.2 %denoise.1 = bf16[8,16,4096]{2,1,0:T(8,128)(2,1)} custom-call(s32[4]{0:T(128)} %add_convert_fusion.place_ref, bf16[3,2,144,160]{3,2,1,0:T(8,128)(2,1)} %get-tuple-element.9.first_ref, bf16[3,2,128,144]{3,2,1,0:T(8,128)(2,1)} %get-tuple-element.10.second_ref, bf16[8,34,16,128]{3,2,1,0:T(8,128)(2,1)} %all_to_all.11.data_ref, bf16[16,4352]{1,0:T(8,128)(2,1)} %copy-done.2, ...), custom_call_target="tpu_custom_call" | custom-call | tf_op jit(solution)/shard_map/denoise/pallas_call | solution.py:225
  (8 shorter events, 0.2 us)
Async XLA Ops:
  1.5 13.5 %collective-permute-start.2 = (s32[1,1]{1,0:T(1,128)}, s32[1,1]{1,0:T(1,128)}, u32[]{:S(2)}, u32[]{:S(2)}) collective-permute-start(s32[1,1]{1,0:T(1,128)} %bitcast.9), channel_id=1, source_target_pairs={{0,1},{1,2},{2,3},{3,4},{4,5},{5,6},{6,7},{7,8},{8,9},{9,10},{10,1... | collective-permute-start | bytes 20 | tf_op jit(solution)/shard_map/ppermute | solution.py:20
  5.3 11.0 %collective-permute-start = (s32[1,1]{1,0:T(1,128)}, s32[1,1]{1,0:T(1,128)}, u32[]{:S(2)}, u32[]{:S(2)}) collective-permute-start(s32[1,1]{1,0:T(1,128)} %bitcast.6), channel_id=1, source_target_pairs={{1,0},{2,1},{3,2},{4,3},{5,4},{6,5},{7,6},{8,7},{9,8},{10,9},{11,1... | collective-permute-start | bytes 20 | tf_op jit(solution)/shard_map/ppermute | solution.py:20
  18.2 17.3 %collective-permute-start.1 = (bf16[1,512,512]{2,1,0:T(8,128)(2,1)S(1)}, bf16[1,512,512]{2,1,0:T(8,128)(2,1)S(1)}, u32[]{:S(2)}, u32[]{:S(2)}) collective-permute-start(bf16[1,512,512]{2,1,0:T(8,128)(2,1)S(1)} %get-tuple-element.16), channel_id=1, source_target_pairs={{0,1},{1,2},{2,3},{3,4},{4,5},{5,6},{6,7},{7,8},{8,9},{9,10},{10,1... | collective-permute-start | bytes 1572872 | tf_op jit(solution)/shard_map/ppermute | solution.py:20
  20.1 16.5 %collective-permute-start.3 = (bf16[1,512,512]{2,1,0:T(8,128)(2,1)S(1)}, bf16[1,512,512]{2,1,0:T(8,128)(2,1)S(1)}, u32[]{:S(2)}, u32[]{:S(2)}) collective-permute-start(bf16[1,512,512]{2,1,0:T(8,128)(2,1)S(1)} %get-tuple-element.15), channel_id=1, source_target_pairs={{1,0},{2,1},{3,2},{4,3},{5,4},{6,5},{7,6},{8,7},{9,8},{10,9},{11,1... | collective-permute-start | bytes 1572872 | tf_op jit(solution)/shard_map/ppermute | solution.py:20
  35.5 1.2 copy-start
  36.7 0.8 copy-start.1
  128.4 10.9 %collective-permute-start.4 = (bf16[16,4352]{1,0:T(8,128)(2,1)}, bf16[16,4352]{1,0:T(8,128)(2,1)S(1)}, u32[]{:S(2)}, u32[]{:S(2)}) collective-permute-start(bf16[16,4352]{1,0:T(8,128)(2,1)} %get-tuple-element.11), channel_id=1, source_target_pairs={{0,1},{1,2},{2,3},{3,4},{4,5},{5,6},{6,7},{7,8},{8,9},{9,10},{10,1... | collective-permute-start | bytes 417800 | tf_op jit(solution)/shard_map/ppermute | solution.py:20
  133.0 7.2 %collective-permute-start.5 = (bf16[16,4352]{1,0:T(8,128)(2,1)}, bf16[16,4352]{1,0:T(8,128)(2,1)S(1)}, u32[]{:S(2)}, u32[]{:S(2)}) collective-permute-start(bf16[16,4352]{1,0:T(8,128)(2,1)} %get-tuple-element.12), channel_id=1, source_target_pairs={{1,0},{2,1},{3,2},{4,3},{5,4},{6,5},{7,6},{8,7},{9,8},{10,9},{11,1... | collective-permute-start | bytes 417800 | tf_op jit(solution)/shard_map/ppermute | solution.py:20
  139.3 0.8 copy-start.2
  140.1 0.7 copy-start.3

commit v2 on v1

v2 whole, which is shorter than its diff:
```python
import numpy as np
import jax
import jax.numpy as jnp
from jax import lax
from jax.experimental import pallas as pl
from jax.experimental.pallas import tpu as pltpu
from jax.sharding import PartitionSpec as P

LANES = 128
HALO = 2
BF16 = jnp.bfloat16
F32 = jnp.float32
VMEM = pl.BlockSpec(memory_space=pltpu.VMEM)
SMEM = pl.BlockSpec(memory_space=pltpu.SMEM)


def call(body, outs, ins, name, mib, scratch=()):
    return pl.pallas_call(
        body,
        out_shape=outs,
        in_specs=ins,
        out_specs=jax.tree.map(lambda _: VMEM, outs),
        scratch_shapes=scratch,
        compiler_params=pltpu.CompilerParams(vmem_limit_bytes=mib << 20),
        name=name,
    )


def shaped(*shape):
    return jax.ShapeDtypeStruct(shape, BF16)


def dot(left, right):
    return jnp.dot(left, right, preferred_element_type=F32)


def shift_pairs(count, steps):
    first, last = (max(0, -steps), min(count, count - steps))
    return [(source, source + steps) for source in range(first, last)]


def from_behind(value, axis, steps):
    return lax.ppermute(value, axis, shift_pairs(lax.axis_size(axis), steps))


def interpolation(amount, edge):
    row_index = lax.broadcasted_iota(jnp.int32, (edge, edge), 0)
    col_index = lax.broadcasted_iota(jnp.int32, (edge, edge), 1)
    offset = col_index - row_index
    w_before = ((-0.5 * amount + 1.0) * amount - 0.5) * amount
    w_center = (1.5 * amount - 2.5) * amount * amount + 1.0
    w_after = ((-1.5 * amount + 2.0) * amount + 0.5) * amount
    w_beyond = (0.5 * amount - 0.5) * amount * amount
    matrix = jnp.where(offset == -1, w_before, 0.0)
    matrix = jnp.where(offset == 0, w_center, matrix)
    matrix = jnp.where(offset == 1, w_after, matrix)
    return jnp.where(offset == 2, w_beyond, matrix)


def matrices_body(fraction_ref, out_ref):
    _, kinds, columns = fraction_ref.shape
    edge = out_ref.shape[-1]
    for kind in range(kinds):
        for block in range(columns):
            out_ref[kind, block] = interpolation(fraction_ref[0, kind, block], edge).astype(BF16)


def warp_body(coarse_ref, source_ref, above_ref, below_ref, matrix_ref, out_ref):
    _, edge, width = source_ref.shape
    columns = width // edge
    groups = out_ref.shape[0] // columns
    chunks, cols = out_ref.shape[1], out_ref.shape[2]
    for block in range(columns):
        down = coarse_ref[0, 0, block]
        anchor = block + coarse_ref[0, 1, block]
        picked = source_ref[0, :, 0:edge]
        for column in range(1, columns):
            picked = jnp.where(anchor == column, source_ref[0, :, column * edge : (column + 1) * edge], picked)
        picked = jnp.where(down < 0, above_ref[0], picked)
        picked = jnp.where(down > 0, below_ref[0], picked)
        rows_warped = dot(matrix_ref[0, block], picked).astype(BF16)
        warped = lax.dot_general(
            matrix_ref[1, block], rows_warped, (((1,), (1,)), ((), ())), preferred_element_type=F32
        ).astype(BF16)
        warped = warped.reshape(groups, cols, edge)
        for chunk in range(chunks):
            out_ref[block * groups : (block + 1) * groups, chunk] = warped[
                :, :, chunk * LANES : (chunk + 1) * LANES
            ]


def tap_index(out_pixels, in_pixels):
    out_sec, out_col = np.array(out_pixels).T[:, :, None]
    in_sec, in_col = np.array(in_pixels).T[:, None, :]
    tap_z, tap_x = in_sec - out_sec + 1, in_col - out_col + 1
    linked = (tap_z >= 0) & (tap_z < 3) & (tap_x >= 0) & (tap_x < 3)
    return np.where(linked, tap_z * 3 + tap_x, -1).astype(np.int32)


def stencil_matrix(index, kernel_ref, out_ref):
    rows, width = index.shape
    for tap_y in range(3):
        value = jnp.zeros((rows, width), F32)
        for tap in range(9):
            value = jnp.where(index == tap, kernel_ref[tap // 3, tap % 3, tap_y], value)
        high = value.astype(BF16)
        low = (value - high.astype(F32)).astype(BF16)
        out_ref[tap_y * rows : (tap_y + 1) * rows, :] = jnp.concatenate([high, low], axis=1)


def stencils_body(one_ref, two_ref, *refs):
    indices, outs = refs[:4], refs[4:]
    for place, (index_ref, out_ref) in enumerate(zip(indices, outs)):
        stencil_matrix(index_ref[...], one_ref if place % 2 == 0 else two_ref, out_ref)


def edges_body(pad, data_ref, first_ref, last_ref):
    parts, chunks, cols, lanes = data_ref.shape
    shape = (pad, chunks * cols)
    index = lax.broadcasted_iota(jnp.int32, shape, 0)
    source = lax.broadcasted_iota(jnp.int32, shape, 1)
    head = index // HALO * cols + index % HALO
    used = index < chunks * HALO
    take_first = jnp.where(used & (source == head), 1.0, 0.0).astype(BF16)
    take_last = jnp.where(used & (source == head + cols - HALO), 1.0, 0.0).astype(BF16)
    take = jnp.concatenate([take_first, take_last], axis=0)
    for part in range(parts):
        rim = dot(take, data_ref[part].reshape(chunks * cols, lanes)).astype(BF16)
        first_ref[part] = rim[:pad]
        last_ref[part] = rim[pad:]


def shifted_sum(matrix_ref, volume, rows):
    size = volume.shape[1]
    before = dot(matrix_ref[0:rows], volume)
    here = dot(matrix_ref[rows : 2 * rows], volume)
    after = dot(matrix_ref[2 * rows : 3 * rows], volume)
    return pltpu.roll(before, 1, 1) + here + pltpu.roll(after, size - 1, 1)


def outside(place_ref, shape, lanes):
    lane = lax.broadcasted_iota(jnp.int32, shape, 1)
    gone = (lane < lanes) & (place_ref[2] > 0)
    return gone | ((lane >= shape[1] - lanes) & (place_ref[3] > 0))


def interior_body(place_ref, first_ref, second_ref, rim_ref, data_ref, out_ref, passed_ref, aligned_ref, volume_ref, pass_ref):
    sections, chunks, cols, lanes = data_ref.shape
    main = sections * cols
    length = chunks * lanes
    for chunk in range(chunks):
        block = data_ref[:, chunk].reshape(main, lanes)
        volume_ref[0:main, chunk * lanes : (chunk + 1) * lanes] = block
        volume_ref[main : 2 * main, chunk * lanes : (chunk + 1) * lanes] = block
    volume = volume_ref[...]
    aligned_ref[...] = dot(rim_ref[...], volume[0:main]).astype(BF16)
    rows = first_ref.shape[0] // 3
    passed = jnp.maximum(shifted_sum(first_ref, volume, rows), 0.0)
    passed = jnp.where(outside(place_ref, passed.shape, lanes), 0.0, passed).astype(BF16)
    passed_ref[...] = passed[0 : passed_ref.shape[0]]
    pass_ref[0:rows] = passed
    pass_ref[rows : 2 * rows] = passed
    second = shifted_sum(second_ref, pass_ref[...], main)
    total = (second + volume_ref[0:main, :].astype(F32))[:, lanes : length - lanes]
    column = lax.broadcasted_iota(jnp.int32, total.shape, 0) % cols
    inside = (column >= HALO) & (column < cols - HALO)
    out_ref[...] = jnp.where(inside, total, 0.0).astype(BF16).reshape(out_ref.shape)


def rim_body(place_ref, first_ref, second_ref, put_ref, halo_ref, passed_ref, aligned_ref, inner_ref, out_ref, volume_ref, pass_ref):
    sections, sides, pad, lanes = halo_ref.shape
    rim, length = aligned_ref.shape
    chunks = length // lanes
    side = sections * HALO
    shape = (chunks * side, sections * pad)
    index = lax.broadcasted_iota(jnp.int32, shape, 0)
    source = lax.broadcasted_iota(jnp.int32, shape, 1)
    wanted = (index % side) // HALO * pad + index // side * HALO + index % HALO
    gather = jnp.where(source == wanted, 1.0, 0.0).astype(BF16)
    high = rim + sides * side
    volume_ref[0:rim] = aligned_ref[...]
    volume_ref[high : high + rim] = aligned_ref[...]
    for which in range(sides):
        halo = dot(gather, halo_ref[:, which].reshape(sections * pad, lanes)).astype(BF16)
        for chunk in range(chunks):
            where = slice(chunk * lanes, (chunk + 1) * lanes)
            block = halo[chunk * side : (chunk + 1) * side]
            start = rim + which * side
            volume_ref[start : start + side, where] = block
            volume_ref[high + start : high + start + side, where] = block
    rows = first_ref.shape[0] // 3
    passed = jnp.maximum(shifted_sum(first_ref, volume_ref[...], rows), 0.0)
    row = lax.broadcasted_iota(jnp.int32, passed.shape, 0)
    gone = outside(place_ref, passed.shape, lanes)
    gone = gone | ((row < sections) & (place_ref[0] > 0))
    gone = gone | ((row >= rows - sections) & (place_ref[1] > 0))
    passed = jnp.where(gone, 0.0, passed).astype(BF16)
    inner = passed_ref.shape[0]
    for start in (0, inner + rows):
        pass_ref[start : start + inner] = passed_ref[...]
        pass_ref[start + inner : start + inner + rows] = passed
    second = shifted_sum(second_ref, pass_ref[...], rim)
    total = (second + aligned_ref[...].astype(F32))[:, lanes : length - lanes].astype(BF16)
    placed = dot(put_ref[...], total)
    inner_out = inner_ref[...].reshape(placed.shape).astype(F32)
    out_ref[...] = (placed + inner_out).astype(BF16).reshape(out_ref.shape)


def one_hot(out_pixels, in_pixels):
    match = [[pixel == other for other in in_pixels] for pixel in out_pixels]
    return jnp.asarray(np.array(match, np.float32), BF16)


def body(source, coarse, fraction, kernel_one, kernel_two):
    _, edge, width = source.shape
    columns = width // edge
    n_xy, n_sec = lax.axis_size("xy"), lax.axis_size("sec")
    cols = width // n_xy
    chunks = edge // LANES

    down, anchor = coarse[0, 0], coarse[0, 1] + jnp.arange(columns, dtype=jnp.int32)
    want_above = jnp.sum(jnp.where(down < 0, anchor, 0)).reshape(1, 1)
    want_below = jnp.sum(jnp.where(down > 0, anchor, 0)).reshape(1, 1)
    for_below = from_behind(want_above, "xy", -1)
    for_above = from_behind(want_below, "xy", 1)

    def choose(column):
        block = source[:, :, 0:edge]
        for index in range(1, columns):
            block = jnp.where(column == index, source[:, :, index * edge : (index + 1) * edge], block)
        return block

    above = from_behind(choose(for_below[0, 0]), "xy", 1)
    below = from_behind(choose(for_above[0, 0]), "xy", -1)

    matrix = call(matrices_body, shaped(2, columns, edge, edge), [SMEM], "matrices", 16)(fraction)

    def pixels(*columns_taken):
        return [(section, column) for section in range(n_sec) for column in columns_taken]

    def by_column(*columns_taken):
        return [(section, column) for column in columns_taken for section in range(n_sec)]

    last = cols - 1
    natural = pixels(*range(cols))
    near = pixels(1, 2, last - 2, last - 1)
    rim = pixels(0, 1, last - 1, last)
    inner_pass = near + pixels(*range(3, last - 2))
    rim_in = rim + pixels(-2, -1) + pixels(last + 1, last + 2)
    rim_pass = by_column(-1, 0, last, last + 1)
    inner_out = [(s, c) if HALO <= c < cols - HALO else (-9, -9) for s, c in natural]
    indices = [
        tap_index(inner_pass, natural),
        tap_index(inner_out, inner_pass),
        tap_index(rim_pass, rim_in),
        tap_index(rim, near + rim_pass),
    ]
    stencils = call(
        stencils_body,
        tuple(shaped(3 * index.shape[0], 2 * index.shape[1]) for index in indices),
        [SMEM, SMEM] + [VMEM] * 4,
        "stencils",
        8,
    )(kernel_one, kernel_two, *map(jnp.asarray, indices))

    at_xy, at_sec = lax.axis_index("xy"), lax.axis_index("sec")
    place = jnp.stack([at_xy == 0, at_xy == n_xy - 1, at_sec == 0, at_sec == n_sec - 1]).astype(jnp.int32)
    above, below, matrix, stencils, place = lax.optimization_barrier((above, below, matrix, stencils, place))

    strip = call(warp_body, shaped(n_xy, chunks, cols, LANES), [SMEM] + [VMEM] * 4, "warp", 16)(
        coarse, source, above, below, matrix
    )
    mine = lax.all_to_all(strip, "xy", split_axis=0, concat_axis=0, tiled=True)
    per_sec = n_xy * chunks // n_sec
    mine = jnp.pad(mine.reshape(n_xy * chunks, cols, LANES), ((1, 1), (0, 0), (0, 0)))
    spread = jnp.stack([mine[index * per_sec : (index + 1) * per_sec + 2] for index in range(n_sec)])
    data = lax.all_to_all(spread, "sec", split_axis=0, concat_axis=0, tiled=True)

    pad = -(-(per_sec + 2) * HALO // 16) * 16
    firsts, lasts = call(
        lambda *refs: edges_body(pad, *refs), (shaped(n_sec, pad, LANES),) * 2, [VMEM], "edges", 8
    )(spread)
    sides = jnp.stack([from_behind(lasts, "xy", 1), from_behind(firsts, "xy", -1)], axis=1)
    halo = lax.all_to_all(sides, "sec", split_axis=0, concat_axis=0, tiled=True)

    length = (per_sec + 2) * LANES
    out = shaped(n_sec, cols, per_sec * LANES)
    inner, passed, aligned = call(
        interior_body,
        (out, shaped(len(near), length), shaped(len(rim), length)),
        [SMEM] + [VMEM] * 4,
        "interior",
        32,
        [pltpu.VMEM((2 * len(natural), length), BF16), pltpu.VMEM((2 * len(inner_pass), length), BF16)],
    )(place, stencils[0], stencils[1], one_hot(rim, natural), data)
    return call(
        rim_body,
        out,
        [SMEM] + [VMEM] * 7,
        "rim",
        32,
        [pltpu.VMEM((2 * len(rim_in), length), BF16), pltpu.VMEM((2 * (len(near) + len(rim_pass)), length), BF16)],
    )(place, stencils[2], stencils[3], one_hot(natural, rim), halo, passed, aligned, inner)


def solution(mesh):
    placed = (P("sec", "xy", None), P("sec", None, "xy"), P("sec", None, "xy"), P(), P())
    return jax.shard_map(
        body, mesh=mesh, in_specs=placed, out_specs=P(None, "xy", "sec"), check_vma=False
    )
```

time: 149 us -> 145 us (0.973)
  blocking collectives: 83.4 us -> 59 us
  waiting for transfers between devices: 9.35 us -> 23.5 us
  starting transfers between devices: 29.6 us -> 38 us
  Pallas kernels: 19.3 us -> 12.9 us
  local copies, waits for them, and re-layouts: 1.61 us -> 5.39 us
    all_to_all x1 -> x0, blocking collectives: 21 us -> none  [body(): lax.all_to_all(spread, 'sec', split_axis=0, concat_axis=0, tiled=True)]
    ppermute x6, waiting for transfers between devices: 9.35 us -> 17.9 us  [from_behind(): return lax.ppermute(value, axis, shift_pairs(lax.axis_size(axis), steps))]
    all_to_all x0 -> x2, starting transfers between devices: none -> 8.15 us  [the longest x1 4.3 us: body(): lax.all_to_all(spread, 'sec', split_axis=0, concat_axis=0, tiled=True)]
    pallas_call x5 -> x6, Pallas kernels: 19.3 us -> 12.9 us  [the longest x1 3.51 us: body(): call(rim_body, out, [SMEM] + [VMEM] * 7, 'rim', 32, [pltpu.VMEM((2 * len(...]
    all_to_all x0 -> x2, waiting for transfers between devices: none -> 5.52 us  [the longest x1 4.79 us: body(): halo = lax.all_to_all(sides, 'sec', split_axis=0, concat_axis=0, tiled=True)]
    all_to_all x1, blocking collectives: 62.4 us -> 59 us  [body(): mine = lax.all_to_all(strip, 'xy', split_axis=0, concat_axis=0, tiled=True)]
    unnamed x15 -> x29, local copies, waits for them, and re-layouts: 1.59 us -> 4.72 us
  transfers between devices with their start and end apart: 6 -> 8, of which waited for: 4 -> 7; matrix products, arithmetic and copies ran while one was open for 0% -> 1% of each run, Pallas kernels for 3% -> 5%
where the time goes in v2:
time: 145 us; the launch traced here: 144 us
  blocking collectives  59 us (41%)
  starting transfers between devices  38 us (26%)
  waiting for transfers between devices  23.5 us (16%)
  Pallas kernels  12.9 us (9%)
  local copies, waits for them, and re-layouts  5.39 us (4%)
  other arithmetic  3.51 us (2%)
  between operations  1.51 us (1%)
    all_to_all x1, blocking collectives, body(): mine = lax.all_to_all(strip, 'xy', split_axis=0, concat_axis=0, tiled=True)  59 us
    ppermute x6, starting transfers between devices, from_behind(): return lax.ppermute(value, axis, shift_pairs(lax.axis_size(axis), steps))  29.9 us
    ppermute x6, waiting for transfers between devices, from_behind(): return lax.ppermute(value, axis, shift_pairs(lax.axis_size(axis), steps))  17.9 us
    all_to_all x1, waiting for transfers between devices, body(): halo = lax.all_to_all(sides, 'sec', split_axis=0, concat_axis=0, tiled=True)  4.79 us
    unnamed x29, local copies, waits for them, and re-layouts  4.72 us
    all_to_all x1, starting transfers between devices, body(): lax.all_to_all(spread, 'sec', split_axis=0, concat_axis=0, tiled=True)  4.3 us
    all_to_all x1, starting transfers between devices, body(): halo = lax.all_to_all(sides, 'sec', split_axis=0, concat_axis=0, tiled=True)  3.85 us
    pallas_call x1, Pallas kernels, body(): call(rim_body, out, [SMEM] + [VMEM] * 7, 'rim', 32, [pltpu.VMEM((2 * len(...  3.51 us
  transfers between devices with their start and end apart: 8, of which 7 were waited for; matrix products, arithmetic and copies ran while one was open for 1% of the time, Pallas kernels for 5%

profile of v2, /device:TPU:24, one launch (start us, length us, event | category | flops | bytes accessed | tf_op | source)
XLA Modules:
  0.0 143.8 jit_solution(14909855347234685668)
XLA Ops:
  0.0 0.0 copy-start.10
  0.0 1.4 fusion.11
  1.4 3.8 %collective-permute-start.2 = (s32[1,1]{1,0:T(1,128)}, s32[1,1]{1,0:T(1,128)}, u32[]{:S(2)}, u32[]{:S(2)}) collective-permute-start(s32[1,1]{1,0:T(1,128)} %bitcast.5), channel_id=1, source_target_pairs={{0,1},{1,2},{2,3},{3,4},{4,5},{5,6},{6,7},{7,8},{8,9},{9,10},{10,1... | collective-permute-start | bytes 20 | tf_op jit(solution)/shard_map/ppermute | solution.py:43
  5.2 9.7 %collective-permute-start = (s32[1,1]{1,0:T(1,128)}, s32[1,1]{1,0:T(1,128)}, u32[]{:S(2)}, u32[]{:S(2)}) collective-permute-start(s32[1,1]{1,0:T(1,128)} %bitcast.2), channel_id=1, source_target_pairs={{1,0},{2,1},{3,2},{4,3},{5,4},{6,5},{7,6},{8,7},{9,8},{10,9},{11,1... | collective-permute-start | bytes 20 | tf_op jit(solution)/shard_map/ppermute | solution.py:43
  14.9 0.0 collective-permute-done.2
  15.5 0.8 collective-permute-done
  17.0 1.3 broadcast_select_fusion
  18.3 0.0 copy-start.1
  18.3 0.0 copy-start.2
  18.3 0.0 copy-start.4
  18.3 0.0 copy-start.5
  18.4 0.0 copy-start.7
  18.4 0.0 copy-start.8
  18.4 6.5 %collective-permute-start.3 = (bf16[1,512,512]{2,1,0:T(8,128)(2,1)S(1)}, bf16[1,512,512]{2,1,0:T(8,128)(2,1)S(1)}, u32[]{:S(2)}, u32[]{:S(2)}) collective-permute-start(bf16[1,512,512]{2,1,0:T(8,128)(2,1)S(1)} %get-tuple-element.41), channel_id=1, source_target_pairs={{1,0},{2,1},{3,2},{4,3},{5,4},{6,5},{7,6},{8,7},{9,8},{10,9},{11,1... | collective-permute-start | bytes 1572872 | tf_op jit(solution)/shard_map/ppermute | solution.py:43
  24.9 1.9 %collective-permute-start.1 = (bf16[1,512,512]{2,1,0:T(8,128)(2,1)S(1)}, bf16[1,512,512]{2,1,0:T(8,128)(2,1)S(1)}, u32[]{:S(2)}, u32[]{:S(2)}) collective-permute-start(bf16[1,512,512]{2,1,0:T(8,128)(2,1)S(1)} %get-tuple-element.42), channel_id=1, source_target_pairs={{0,1},{1,2},{2,3},{3,4},{4,5},{5,6},{6,7},{7,8},{8,9},{9,10},{10,1... | collective-permute-start | bytes 1572872 | tf_op jit(solution)/shard_map/ppermute | solution.py:43
  26.8 0.0 copy-done.10
  26.8 0.0 copy-start
  26.8 0.0 copy-start.9
  26.9 1.0 matrices.1.matrix_ref
  27.8 0.0 copy-done.1
  27.9 0.0 copy-done.2
  27.9 0.0 copy-done.4
  27.9 0.0 copy-done.5
  27.9 0.0 copy-done.7
  27.9 0.0 copy-done.8
  27.9 1.1 stencils.1
  29.0 0.1 add_convert_fusion.place_ref
  29.1 5.5 %collective-permute-done.3.below_ref = bf16[1,512,512]{2,1,0:T(8,128)(2,1)S(1)} collective-permute-done((bf16[1,512,512]{2,1,0:T(8,128)(2,1)S(1)}, bf16[1,512,512]{2,1,0:T(8,128)(2,1)S(1)}, u32[]{:S(2)}, u32[]{:S(2)}) %collective-permute-start.3) | collective-permute-done | bytes 524320 | tf_op jit(solution)/shard_map/ppermute | solution.py:43
  34.6 6.2 %collective-permute-done.1.above_ref = bf16[1,512,512]{2,1,0:T(8,128)(2,1)S(1)} collective-permute-done((bf16[1,512,512]{2,1,0:T(8,128)(2,1)S(1)}, bf16[1,512,512]{2,1,0:T(8,128)(2,1)S(1)}, u32[]{:S(2)}, u32[]{:S(2)}) %collective-permute-start.1) | collective-permute-done | bytes 524320 | tf_op jit(solution)/shard_map/ppermute | solution.py:43
  40.8 0.0 copy-done
  40.8 0.0 copy-done.9
  40.8 2.1 %warp.1 = bf16[64,4,16,128]{3,2,1,0:T(8,128)(2,1)S(1)} custom-call(s32[1,2,2]{2,1,0:T(2,128)S(1)} %copy-done.9, bf16[1,512,1024]{2,1,0:T(8,128)(2,1)S(1)} %copy-done, bf16[1,512,512]{2,1,0:T(8,128)(2,1)S(1)} %collective-permute-done.1.above_ref, bf16[1,512,512]{2,1,0:T(8,128)(2,1)S(1)} %collective-permute-done.3.below_ref, ...), custom_call_target="tpu_custom_call" | custom-call | tf_op jit(solution)/shard_map/warp/pallas_call | solution.py:270
  42.9 59.0 %all_to_all.15 = bf16[64,4,16,128]{3,2,1,0:T(8,128)(2,1)S(1)} all-to-all(bf16[64,4,16,128]{3,2,1,0:T(8,128)(2,1)S(1)} %warp.1), channel_id=1, replica_groups=mesh['sec'=8,'xy'=64] {'xy'}, dimensions={0} | all-to-all | bytes 2097152 | tf_op jit(solution)/shard_map/all_to_all | solution.py:273
  101.9 0.7 fusion.1
  102.5 0.7 fusion.9
  103.2 0.7 fusion.8
  103.9 0.7 fusion.7
  104.5 0.7 fusion.6
  105.2 0.7 fusion.5
  105.9 0.7 fusion.4
  106.5 0.7 fusion.3.refs_0_
  107.2 4.3 %all-to-all-start.2 = ((bf16[8,34,16,128]{3,2,1,0:T(8,128)(2,1)}), bf16[8,34,16,128]{3,2,1,0:T(8,128)(2,1)S(1)}, u32[]{:S(2)}, u32[]{:S(2)}) async-start(bf16[8,34,16,128]{3,2,1,0:T(8,128)(2,1)} %fusion.3.refs_0_), calls=%async_computation.2 | async-start | bytes 2228224 | tf_op jit(solution)/shard_map/all_to_all | solution.py:277
  111.5 0.0 copy-start.6
  111.5 1.8 %edges.1 = (bf16[8,80,128]{2,1,0:T(8,128)(2,1)S(1)}, bf16[8,80,128]{2,1,0:T(8,128)(2,1)S(1)}) custom-call(bf16[8,34,16,128]{3,2,1,0:T(8,128)(2,1)} %fusion.3.refs_0_), custom_call_target="tpu_custom_call" | custom-call | tf_op jit(solution)/shard_map/edges/pallas_call | solution.py:280
  113.4 5.1 %collective-permute-start.4 = (bf16[8,80,128]{2,1,0:T(8,128)(2,1)S(1)}, bf16[8,80,128]{2,1,0:T(8,128)(2,1)S(1)}, u32[]{:S(2)}, u32[]{:S(2)}) collective-permute-start(bf16[8,80,128]{2,1,0:T(8,128)(2,1)S(1)} %get-tuple-element.32), channel_id=1, source_target_pairs={{0,1},{1,2},{2,3},{3,4},{4,5},{5,6},{6,7},{7,8},{8,9},{9,10},{10,1... | collective-permute-start | bytes 491528 | tf_op jit(solution)/shard_map/ppermute | solution.py:43
  118.5 2.9 %collective-permute-start.5 = (bf16[8,80,128]{2,1,0:T(8,128)(2,1)S(1)}, bf16[8,80,128]{2,1,0:T(8,128)(2,1)S(1)}, u32[]{:S(2)}, u32[]{:S(2)}) collective-permute-start(bf16[8,80,128]{2,1,0:T(8,128)(2,1)S(1)} %get-tuple-element.33), channel_id=1, source_target_pairs={{1,0},{2,1},{3,2},{4,3},{5,4},{6,5},{7,6},{8,7},{9,8},{10,9},{11,1... | collective-permute-start | bytes 491528 | tf_op jit(solution)/shard_map/ppermute | solution.py:43
  121.3 2.6 %collective-permute-done.4 = bf16[8,80,128]{2,1,0:T(8,128)(2,1)S(1)} collective-permute-done((bf16[8,80,128]{2,1,0:T(8,128)(2,1)S(1)}, bf16[8,80,128]{2,1,0:T(8,128)(2,1)S(1)}, u32[]{:S(2)}, u32[]{:S(2)}) %collective-permute-start.4) | collective-permute-done | bytes 163872 | tf_op jit(solution)/shard_map/ppermute | solution.py:43
  124.0 2.7 %collective-permute-done.5 = bf16[8,80,128]{2,1,0:T(8,128)(2,1)S(1)} collective-permute-done((bf16[8,80,128]{2,1,0:T(8,128)(2,1)S(1)}, bf16[8,80,128]{2,1,0:T(8,128)(2,1)S(1)}, u32[]{:S(2)}, u32[]{:S(2)}) %collective-permute-start.5) | collective-permute-done | bytes 163872 | tf_op jit(solution)/shard_map/ppermute | solution.py:43
  126.7 0.8 pad_maximum_fusion
  127.4 0.0 copy-start.3
  127.4 0.7 all-to-all-done.2.data_ref
  128.2 3.8 %all-to-all-start.1 = ((bf16[8,2,80,128]{3,2,1,0:T(8,128)(2,1)}), bf16[8,2,80,128]{3,2,1,0:T(8,128)(2,1)S(1)}, u32[]{:S(2)}, u32[]{:S(2)}) async-start(bf16[8,2,80,128]{3,2,1,0:T(8,128)(2,1)} %pad_maximum_fusion), calls=%async_computation.1 | async-start | bytes 655360 | tf_op jit(solution)/shard_map/all_to_all | solution.py:284
  132.0 0.0 copy-done.6
  132.0 3.4 %interior.1 = (bf16[8,16,4096]{2,1,0:T(8,128)(2,1)S(1)}, bf16[32,4352]{1,0:T(8,128)(2,1)S(1)}, bf16[32,4352]{1,0:T(8,128)(2,1)S(1)}) custom-call(s32[4]{0:T(128)S(1)} %add_convert_fusion.place_ref, bf16[336,256]{1,0:T(8,128)(2,1)S(1)} %get-tuple-element.34.first_ref, bf16[384,224]{1,0:T(8,128)(2,1)S(1)} %get-tuple-element.35.second_ref, ...), custom_call_target="tpu_custom_call" | custom-call | tf_op jit(solution)/shard_map/interior/pallas_call | solution.py:288
  135.5 4.8 %all-to-all-done.1.halo_ref = bf16[8,2,80,128]{3,2,1,0:T(8,128)(2,1)S(1)} async-done(((bf16[8,2,80,128]{3,2,1,0:T(8,128)(2,1)}), bf16[8,2,80,128]{3,2,1,0:T(8,128)(2,1)S(1)}, u32[]{:S(2)}, u32[]{:S(2)}) %all-to-all-start.1) | async-done | bytes 327712 | tf_op jit(solution)/shard_map/all_to_all | solution.py:284
  140.3 0.0 copy-done.3
  140.3 3.5 %rim.1 = bf16[8,16,4096]{2,1,0:T(8,128)(2,1)} custom-call(s32[4]{0:T(128)S(1)} %add_convert_fusion.place_ref, bf16[96,128]{1,0:T(8,128)(2,1)S(1)} %get-tuple-element.27.first_ref, bf16[96,128]{1,0:T(8,128)(2,1)S(1)} %get-tuple-element.28.second_ref, bf16[128,32]{1,0:T(8,128)(2,1)S(1)} %copy-done.3, bf16[8,2,80,128]{3,2,1,0:T(8,128)(2,1)S(1)} %all-to-all-done.1.halo_ref, ...), custom_call_target="tpu_custom_call" | custom-call | tf_op jit(solution)/shard_map/rim/pallas_call | solution.py:296
Async XLA Ops:
  0.0 26.8 %copy-start.10 = (f32[1,2,2]{2,1,0:T(2,128)S(1)}, f32[1,2,2]{2,1,0:T(2,128)}, u32[]{:S(2)}) copy-start(f32[1,2,2]{2,1,0:T(2,128)} %fraction_ref.1) | copy-start | bytes 52
  1.4 13.5 %collective-permute-start.2 = (s32[1,1]{1,0:T(1,128)}, s32[1,1]{1,0:T(1,128)}, u32[]{:S(2)}, u32[]{:S(2)}) collective-permute-start(s32[1,1]{1,0:T(1,128)} %bitcast.5), channel_id=1, source_target_pairs={{0,1},{1,2},{2,3},{3,4},{4,5},{5,6},{6,7},{7,8},{8,9},{9,10},{10,1... | collective-permute-start | bytes 20 | tf_op jit(solution)/shard_map/ppermute | solution.py:43
  5.2 11.2 %collective-permute-start = (s32[1,1]{1,0:T(1,128)}, s32[1,1]{1,0:T(1,128)}, u32[]{:S(2)}, u32[]{:S(2)}) collective-permute-start(s32[1,1]{1,0:T(1,128)} %bitcast.2), channel_id=1, source_target_pairs={{1,0},{2,1},{3,2},{4,3},{5,4},{6,5},{7,6},{8,7},{9,8},{10,9},{11,1... | collective-permute-start | bytes 20 | tf_op jit(solution)/shard_map/ppermute | solution.py:43
  18.3 9.5 %copy-start.1 = (s32[128,112]{1,0:T(8,128)S(1)}, s32[128,112]{1,0:T(8,128)}, u32[]{:S(2)}) copy-start(s32[128,112]{1,0:T(8,128)} %constant.35.clone.refs_1_) | copy-start | bytes 172036
  18.3 9.5 %copy-start.2 = (s32[112,128]{1,0:T(8,128)S(1)}, s32[112,128]{1,0:T(8,128)}, u32[]{:S(2)}) copy-start(s32[112,128]{1,0:T(8,128)} %constant.34.clone.refs_0_) | copy-start | bytes 172036
  18.3 9.5 %copy-start.4 = (s32[32,64]{1,0:T(8,128)S(1)}, s32[32,64]{1,0:T(8,128)}, u32[]{:S(2)}) copy-start(s32[32,64]{1,0:T(8,128)} %constant.37.clone.refs_3_) | copy-start | bytes 24580
  18.3 9.5 %copy-start.5 = (s32[32,64]{1,0:T(8,128)S(1)}, s32[32,64]{1,0:T(8,128)}, u32[]{:S(2)}) copy-start(s32[32,64]{1,0:T(8,128)} %constant.36.clone.refs_2_) | copy-start | bytes 24580
  18.4 9.5 %copy-start.7 = (f32[3,3,3]{2,1,0:T(4,128)S(1)}, f32[3,3,3]{2,1,0:T(4,128)}, u32[]{:S(2)}) copy-start(f32[3,3,3]{2,1,0:T(4,128)} %one_ref.1) | copy-start | bytes 328
  18.4 9.5 %copy-start.8 = (f32[3,3,3]{2,1,0:T(4,128)S(1)}, f32[3,3,3]{2,1,0:T(4,128)}, u32[]{:S(2)}) copy-start(f32[3,3,3]{2,1,0:T(4,128)} %two_ref.1) | copy-start | bytes 328
  18.4 16.2 %collective-permute-start.3 = (bf16[1,512,512]{2,1,0:T(8,128)(2,1)S(1)}, bf16[1,512,512]{2,1,0:T(8,128)(2,1)S(1)}, u32[]{:S(2)}, u32[]{:S(2)}) collective-permute-start(bf16[1,512,512]{2,1,0:T(8,128)(2,1)S(1)} %get-tuple-element.41), channel_id=1, source_target_pairs={{1,0},{2,1},{3,2},{4,3},{5,4},{6,5},{7,6},{8,7},{9,8},{10,9},{11,1... | collective-permute-start | bytes 1572872 | tf_op jit(solution)/shard_map/ppermute | solution.py:43
  24.9 15.9 %collective-permute-start.1 = (bf16[1,512,512]{2,1,0:T(8,128)(2,1)S(1)}, bf16[1,512,512]{2,1,0:T(8,128)(2,1)S(1)}, u32[]{:S(2)}, u32[]{:S(2)}) collective-permute-start(bf16[1,512,512]{2,1,0:T(8,128)(2,1)S(1)} %get-tuple-element.42), channel_id=1, source_target_pairs={{0,1},{1,2},{2,3},{3,4},{4,5},{5,6},{6,7},{7,8},{8,9},{9,10},{10,1... | collective-permute-start | bytes 1572872 | tf_op jit(solution)/shard_map/ppermute | solution.py:43
  26.8 14.0 %copy-start = (bf16[1,512,1024]{2,1,0:T(8,128)(2,1)S(1)}, bf16[1,512,1024]{2,1,0:T(8,128)(2,1)}, u32[]{:S(2)}) copy-start(bf16[1,512,1024]{2,1,0:T(8,128)(2,1)} %source_ref.1) | copy-start | bytes 3145732
  26.8 14.0 %copy-start.9 = (s32[1,2,2]{2,1,0:T(2,128)S(1)}, s32[1,2,2]{2,1,0:T(2,128)}, u32[]{:S(2)}) copy-start(s32[1,2,2]{2,1,0:T(2,128)} %coarse_ref.1) | copy-start | bytes 52
  107.2 21.0 %all-to-all-start.2 = ((bf16[8,34,16,128]{3,2,1,0:T(8,128)(2,1)}), bf16[8,34,16,128]{3,2,1,0:T(8,128)(2,1)S(1)}, u32[]{:S(2)}, u32[]{:S(2)}) async-start(bf16[8,34,16,128]{3,2,1,0:T(8,128)(2,1)} %fusion.3.refs_0_), calls=%async_computation.2 | async-start | bytes 2228224 | tf_op jit(solution)/shard_map/all_to_all | solution.py:277
  111.5 20.5 %copy-start.6 = (bf16[32,128]{1,0:T(8,128)(2,1)S(1)}, bf16[32,128]{1,0:T(8,128)(2,1)}, u32[]{:S(2)}) copy-start(bf16[32,128]{1,0:T(8,128)(2,1)} %constant.38.clone.rim_ref) | copy-start | bytes 24580
  113.4 10.6 %collective-permute-start.4 = (bf16[8,80,128]{2,1,0:T(8,128)(2,1)S(1)}, bf16[8,80,128]{2,1,0:T(8,128)(2,1)S(1)}, u32[]{:S(2)}, u32[]{:S(2)}) collective-permute-start(bf16[8,80,128]{2,1,0:T(8,128)(2,1)S(1)} %get-tuple-element.32), channel_id=1, source_target_pairs={{0,1},{1,2},{2,3},{3,4},{4,5},{5,6},{6,7},{7,8},{8,9},{9,10},{10,1... | collective-permute-start | bytes 491528 | tf_op jit(solution)/shard_map/ppermute | solution.py:43
  118.5 8.2 %collective-permute-start.5 = (bf16[8,80,128]{2,1,0:T(8,128)(2,1)S(1)}, bf16[8,80,128]{2,1,0:T(8,128)(2,1)S(1)}, u32[]{:S(2)}, u32[]{:S(2)}) collective-permute-start(bf16[8,80,128]{2,1,0:T(8,128)(2,1)S(1)} %get-tuple-element.33), channel_id=1, source_target_pairs={{1,0},{2,1},{3,2},{4,3},{5,4},{6,5},{7,6},{8,7},{9,8},{10,9},{11,1... | collective-permute-start | bytes 491528 | tf_op jit(solution)/shard_map/ppermute | solution.py:43
  127.4 12.8 %copy-start.3 = (bf16[128,32]{1,0:T(8,128)(2,1)S(1)}, bf16[128,32]{1,0:T(8,128)(2,1)}, u32[]{:S(2)}) copy-start(bf16[128,32]{1,0:T(8,128)(2,1)} %constant.39.clone.put_ref) | copy-start | bytes 24580
  128.2 12.1 %all-to-all-start.1 = ((bf16[8,2,80,128]{3,2,1,0:T(8,128)(2,1)}), bf16[8,2,80,128]{3,2,1,0:T(8,128)(2,1)S(1)}, u32[]{:S(2)}, u32[]{:S(2)}) async-start(bf16[8,2,80,128]{3,2,1,0:T(8,128)(2,1)} %pad_maximum_fusion), calls=%async_computation.1 | async-start | bytes 655360 | tf_op jit(solution)/shard_map/all_to_all | solution.py:284

commit v3 on v2

--- a/solution.py
+++ b/solution.py
@@ -63,6 +63,20 @@
     for kind in range(kinds):
         for block in range(columns):
             out_ref[kind, block] = interpolation(fraction_ref[0, kind, block], edge).astype(BF16)
+
+
+def choose_body(below_ref, above_ref, source_ref, for_below_ref, for_above_ref):
+    edge = for_below_ref.shape[-1]
+    columns = source_ref.shape[-1] // edge
+    for coarse_ref, sign, out_ref in ((below_ref, -1, for_below_ref), (above_ref, 1, for_above_ref)):
+        wanted = 0
+        for block in range(columns):
+            wanted += jnp.where(coarse_ref[0, 0, block] == sign, block + coarse_ref[0, 1, block], 0)
+        for column in range(columns):
+
+            @pl.when(wanted == column)
+            def _():
+                out_ref[0] = source_ref[0, :, column * edge : (column + 1) * edge]
 
 
 def warp_body(coarse_ref, source_ref, above_ref, below_ref, matrix_ref, out_ref):
@@ -114,20 +128,14 @@
         stencil_matrix(index_ref[...], one_ref if place % 2 == 0 else two_ref, out_ref)
 
 
-def edges_body(pad, data_ref, first_ref, last_ref):
-    parts, chunks, cols, lanes = data_ref.shape
-    shape = (pad, chunks * cols)
-    index = lax.broadcasted_iota(jnp.int32, shape, 0)
-    source = lax.broadcasted_iota(jnp.int32, shape, 1)
-    head = index // HALO * cols + index % HALO
-    used = index < chunks * HALO
-    take_first = jnp.where(used & (source == head), 1.0, 0.0).astype(BF16)
-    take_last = jnp.where(used & (source == head + cols - HALO), 1.0, 0.0).astype(BF16)
-    take = jnp.concatenate([take_first, take_last], axis=0)
-    for part in range(parts):
-        rim = dot(take, data_ref[part].reshape(chunks * cols, lanes)).astype(BF16)
-        first_ref[part] = rim[:pad]
-        last_ref[part] = rim[pad:]
+def edges_body(data_ref, take_ref, first_ref, last_ref):
+    sections, chunks, cols, lanes = data_ref.shape
+    side = first_ref.shape[0]
+    for chunk in range(chunks):
+        rim = dot(take_ref[...], data_ref[:, chunk].reshape(sections * cols, lanes)).astype(BF16)
+        where = slice(chunk * lanes, (chunk + 1) * lanes)
+        first_ref[:, where] = rim[:side]
+        last_ref[:, where] = rim[side:]
 
 
 def shifted_sum(matrix_ref, volume, rows):
@@ -167,27 +175,15 @@
     out_ref[...] = jnp.where(inside, total, 0.0).astype(BF16).reshape(out_ref.shape)
 
 
-def rim_body(place_ref, first_ref, second_ref, put_ref, halo_ref, passed_ref, aligned_ref, inner_ref, out_ref, volume_ref, pass_ref):
-    sections, sides, pad, lanes = halo_ref.shape
+def rim_body(place_ref, first_ref, second_ref, put_ref, left_ref, right_ref, passed_ref, aligned_ref, inner_ref, out_ref, volume_ref, pass_ref):
+    lanes = LANES
+    sections = inner_ref.shape[0]
     rim, length = aligned_ref.shape
-    chunks = length // lanes
-    side = sections * HALO
-    shape = (chunks * side, sections * pad)
-    index = lax.broadcasted_iota(jnp.int32, shape, 0)
-    source = lax.broadcasted_iota(jnp.int32, shape, 1)
-    wanted = (index % side) // HALO * pad + index // side * HALO + index % HALO
-    gather = jnp.where(source == wanted, 1.0, 0.0).astype(BF16)
-    high = rim + sides * side
-    volume_ref[0:rim] = aligned_ref[...]
-    volume_ref[high : high + rim] = aligned_ref[...]
-    for which in range(sides):
-        halo = dot(gather, halo_ref[:, which].reshape(sections * pad, lanes)).astype(BF16)
-        for chunk in range(chunks):
-            where = slice(chunk * lanes, (chunk + 1) * lanes)
-            block = halo[chunk * side : (chunk + 1) * side]
-            start = rim + which * side
-            volume_ref[start : start + side, where] = block
-            volume_ref[high + start : high + start + side, where] = block
+    side = left_ref.shape[0]
+    for start in (0, rim + 2 * side):
+        volume_ref[start : start + rim] = aligned_ref[...]
+        volume_ref[start + rim : start + rim + side] = left_ref[...]
+        volume_ref[start + rim + side : start + rim + 2 * side] = right_ref[...]
     rows = first_ref.shape[0] // 3
     passed = jnp.maximum(shifted_sum(first_ref, volume_ref[...], rows), 0.0)
     row = lax.broadcasted_iota(jnp.int32, passed.shape, 0)
@@ -218,20 +214,11 @@
     cols = width // n_xy
     chunks = edge // LANES
 
-    down, anchor = coarse[0, 0], coarse[0, 1] + jnp.arange(columns, dtype=jnp.int32)
-    want_above = jnp.sum(jnp.where(down < 0, anchor, 0)).reshape(1, 1)
-    want_below = jnp.sum(jnp.where(down > 0, anchor, 0)).reshape(1, 1)
-    for_below = from_behind(want_above, "xy", -1)
-    for_above = from_behind(want_below, "xy", 1)
-
-    def choose(column):
-        block = source[:, :, 0:edge]
-        for index in range(1, columns):
-            block = jnp.where(column == index, source[:, :, index * edge : (index + 1) * edge], block)
-        return block
-
-    above = from_behind(choose(for_below[0, 0]), "xy", 1)
-    below = from_behind(choose(for_above[0, 0]), "xy", -1)
+    of_below, of_above = from_behind(coarse, "xy", -1), from_behind(coarse, "xy", 1)
+    for_below, for_above = call(
+        choose_body, (shaped(1, edge, edge),) * 2, [SMEM, SMEM, VMEM], "choose", 8
+    )(of_below, of_above, source)
+    above, below = from_behind(for_below, "xy", 1), from_behind(for_above, "xy", -1)
 
     matrix = call(matrices_body, shaped(2, columns, edge, edge), [SMEM], "matrices", 16)(fraction)
 
@@ -276,15 +263,12 @@
     spread = jnp.stack([mine[index * per_sec : (index + 1) * per_sec + 2] for index in range(n_sec)])
     data = lax.all_to_all(spread, "sec", split_axis=0, concat_axis=0, tiled=True)
 
-    pad = -(-(per_sec + 2) * HALO // 16) * 16
-    firsts, lasts = call(
-        lambda *refs: edges_body(pad, *refs), (shaped(n_sec, pad, LANES),) * 2, [VMEM], "edges", 8
-    )(spread)
-    sides = jnp.stack([from_behind(lasts, "xy", 1), from_behind(firsts, "xy", -1)], axis=1)
-    halo = lax.all_to_all(sides, "sec", split_axis=0, concat_axis=0, tiled=True)
-
     length = (per_sec + 2) * LANES
     out = shaped(n_sec, cols, per_sec * LANES)
+    firsts, lasts = call(
+        edges_body, (shaped(n_sec * HALO, length),) * 2, [VMEM, VMEM], "edges", 8
+    )(data, one_hot(pixels(0, 1) + pixels(last - 1, last), natural))
+    left, right = from_behind(lasts, "xy", 1), from_behind(firsts, "xy", -1)
     inner, passed, aligned = call(
         interior_body,
         (out, shaped(len(near), length), shaped(len(rim), length)),
@@ -296,11 +280,11 @@
     return call(
         rim_body,
         out,
-        [SMEM] + [VMEM] * 7,
+        [SMEM] + [VMEM] * 8,
         "rim",
         32,
         [pltpu.VMEM((2 * len(rim_in), length), BF16), pltpu.VMEM((2 * (len(near) + len(rim_pass)), length), BF16)],
-    )(place, stencils[2], stencils[3], one_hot(natural, rim), halo, passed, aligned, inner)
+    )(place, stencils[2], stencils[3], one_hot(natural, rim), left, right, passed, aligned, inner)
 
 
 def solution(mesh):

time: 145 us -> 137 us (0.945)
  blocking collectives: 59 us -> 79.7 us
  waiting for transfers between devices: 23.5 us -> 12.9 us
  starting transfers between devices: 38 us -> 29.5 us
  other arithmetic: 3.51 us -> 0.08 us
  local copies, waits for them, and re-layouts: 5.39 us -> 2.11 us
    all_to_all x0 -> x1, blocking collectives: none -> 20.9 us  [body(): lax.all_to_all(spread, 'sec', split_axis=0, concat_axis=0, tiled=True)]
    all_to_all x2 -> x0, starting transfers between devices: 8.15 us -> none  [the longest x1 4.3 us: body(): lax.all_to_all(spread, 'sec', split_axis=0, concat_axis=0, tiled=True)]
    all_to_all x2 -> x0, waiting for transfers between devices: 5.52 us -> none  [the longest x1 4.79 us: body(): halo = lax.all_to_all(sides, 'sec', split_axis=0, concat_axis=0, tiled=True)]
    ppermute x6, waiting for transfers between devices: 17.9 us -> 12.9 us  [from_behind(): return lax.ppermute(value, axis, shift_pairs(lax.axis_size(axis), steps))]
    unnamed x29 -> x33, local copies, waits for them, and re-layouts: 4.72 us -> 2.09 us
    pallas_call x2 -> x3, Pallas kernels: 5.36 us -> 4.08 us  [the longest x1 3.03 us: body(): call(rim_body, out, [SMEM] + [VMEM] * 8, 'rim', 32, [pltpu.VMEM((2 * len(...]
  transfers between devices with their start and end apart: 8 -> 6, of which waited for: 7 -> 4; matrix products, arithmetic and copies ran while one was open for 1% -> 0% of each run, Pallas kernels for 5% -> 4%
where the time goes in v3:
time: 137 us; the launch traced here: 136 us
  blocking collectives  79.7 us (58%)
  starting transfers between devices  29.5 us (22%)
  waiting for transfers between devices  12.9 us (9%)
  Pallas kernels  11.7 us (9%)
  local copies, waits for them, and re-layouts  2.11 us (2%)
    all_to_all x1, blocking collectives, body(): mine = lax.all_to_all(strip, 'xy', split_axis=0, concat_axis=0, tiled=True)  58.8 us
    ppermute x6, starting transfers between devices, from_behind(): return lax.ppermute(value, axis, shift_pairs(lax.axis_size(axis), steps))  29.5 us
    all_to_all x1, blocking collectives, body(): lax.all_to_all(spread, 'sec', split_axis=0, concat_axis=0, tiled=True)  20.9 us
    ppermute x6, waiting for transfers between devices, from_behind(): return lax.ppermute(value, axis, shift_pairs(lax.axis_size(axis), steps))  12.9 us
    pallas_call x1, Pallas kernels, body(): call(interior_body, (out, shaped(len(near), length), shaped(len(rim), len...  3.49 us
    pallas_call x1, Pallas kernels, body(): call(rim_body, out, [SMEM] + [VMEM] * 8, 'rim', 32, [pltpu.VMEM((2 * len(...  3.03 us
  transfers between devices with their start and end apart: 6, of which 4 were waited for; matrix products, arithmetic and copies ran while one was open for 0% of the time, Pallas kernels for 4%

profile of v3, /device:TPU:24, one launch (start us, length us, event | category | flops | bytes accessed | tf_op | source)
XLA Modules:
  0.0 136.3 jit_solution(15717918321668261293)
XLA Ops:
  0.0 11.6 %collective-permute-start = (s32[1,2,2]{2,1,0:T(2,128)}, s32[1,2,2]{2,1,0:T(2,128)S(1)}, u32[]{:S(2)}, u32[]{:S(2)}) collective-permute-start(s32[1,2,2]{2,1,0:T(2,128)} %coarse_ref.1), channel_id=1, source_target_pairs={{1,0},{2,1},{3,2},{4,3},{5,4},{6,5},{7,6},{8,7},{9,8},{10,9},{11,1... | collective-permute-start | bytes 56 | tf_op jit(solution)/shard_map/ppermute | solution.py:43
  11.6 1.9 %collective-permute-start.1 = (s32[1,2,2]{2,1,0:T(2,128)}, s32[1,2,2]{2,1,0:T(2,128)S(1)}, u32[]{:S(2)}, u32[]{:S(2)}) collective-permute-start(s32[1,2,2]{2,1,0:T(2,128)} %coarse_ref.1), channel_id=1, source_target_pairs={{0,1},{1,2},{2,3},{3,4},{4,5},{5,6},{6,7},{7,8},{8,9},{9,10},{10,1... | collective-permute-start | bytes 56 | tf_op jit(solution)/shard_map/ppermute | solution.py:43
  13.5 0.0 collective-permute-done.below_ref
  13.5 5.8 %collective-permute-done.1.above_ref = s32[1,2,2]{2,1,0:T(2,128)S(1)} collective-permute-done((s32[1,2,2]{2,1,0:T(2,128)}, s32[1,2,2]{2,1,0:T(2,128)S(1)}, u32[]{:S(2)}, u32[]{:S(2)}) %collective-permute-start.1) | collective-permute-done | bytes 48 | tf_op jit(solution)/shard_map/ppermute | solution.py:43
  19.4 0.0 copy-start
  19.4 1.2 copy-done
  20.6 0.6 choose.1
  21.2 0.0 copy-start.2
  21.3 0.0 copy-start.3
  21.3 0.0 copy-start.5
  21.3 0.0 copy-start.6
  21.3 0.0 copy-start.9
  21.3 0.0 copy-start.10
  21.3 2.1 %collective-permute-start.2 = (bf16[1,512,512]{2,1,0:T(8,128)(2,1)S(1)}, bf16[1,512,512]{2,1,0:T(8,128)(2,1)S(1)}, u32[]{:S(2)}, u32[]{:S(2)}) collective-permute-start(bf16[1,512,512]{2,1,0:T(8,128)(2,1)S(1)} %get-tuple-element.24), channel_id=1, source_target_pairs={{0,1},{1,2},{2,3},{3,4},{4,5},{5,6},{6,7},{7,8},{8,9},{9,10},{10,1... | collective-permute-start | bytes 1572872 | tf_op jit(solution)/shard_map/ppermute | solution.py:43
  23.4 6.0 %collective-permute-start.3 = (bf16[1,512,512]{2,1,0:T(8,128)(2,1)S(1)}, bf16[1,512,512]{2,1,0:T(8,128)(2,1)S(1)}, u32[]{:S(2)}, u32[]{:S(2)}) collective-permute-start(bf16[1,512,512]{2,1,0:T(8,128)(2,1)S(1)} %get-tuple-element.25), channel_id=1, source_target_pairs={{1,0},{2,1},{3,2},{4,3},{5,4},{6,5},{7,6},{8,7},{9,8},{10,9},{11,1... | collective-permute-start | bytes 1572872 | tf_op jit(solution)/shard_map/ppermute | solution.py:43
  29.4 0.0 copy-start.11
  29.4 0.7 copy-done.11
  30.1 0.0 copy-start.1
  30.1 0.0 copy-start.12
  30.1 1.0 matrices.1.matrix_ref
  31.1 0.0 copy-done.2
  31.1 0.0 copy-done.3
  31.1 0.0 copy-done.5
  31.1 0.0 copy-done.6
  31.1 0.0 copy-done.9
  31.2 0.0 copy-done.10
  31.2 1.1 stencils.1
  32.2 0.1 add_convert_fusion.place_ref
  32.3 5.4 %collective-permute-done.2.above_ref = bf16[1,512,512]{2,1,0:T(8,128)(2,1)S(1)} collective-permute-done((bf16[1,512,512]{2,1,0:T(8,128)(2,1)S(1)}, bf16[1,512,512]{2,1,0:T(8,128)(2,1)S(1)}, u32[]{:S(2)}, u32[]{:S(2)}) %collective-permute-start.2) | collective-permute-done | bytes 524320 | tf_op jit(solution)/shard_map/ppermute | solution.py:43
  37.7 1.2 collective-permute-done.3.below_ref
  38.9 0.0 copy-done.1
  38.9 0.0 copy-done.12
  38.9 2.1 %warp.1 = bf16[64,4,16,128]{3,2,1,0:T(8,128)(2,1)S(1)} custom-call(s32[1,2,2]{2,1,0:T(2,128)S(1)} %copy-done.12, bf16[1,512,1024]{2,1,0:T(8,128)(2,1)S(1)} %copy-done.1, bf16[1,512,512]{2,1,0:T(8,128)(2,1)S(1)} %collective-permute-done.2.above_ref, bf16[1,512,512]{2,1,0:T(8,128)(2,1)S(1)} %collective-permute-done.3.below_ref, ...), custom_call_target="tpu_custom_call" | custom-call | tf_op jit(solution)/shard_map/warp/pallas_call | solution.py:257
  40.9 58.8 %all_to_all.10 = bf16[64,4,16,128]{3,2,1,0:T(8,128)(2,1)S(1)} all-to-all(bf16[64,4,16,128]{3,2,1,0:T(8,128)(2,1)S(1)} %warp.1), channel_id=1, replica_groups=mesh['sec'=8,'xy'=64] {'xy'}, dimensions={0} | all-to-all | bytes 2097152 | tf_op jit(solution)/shard_map/all_to_all | solution.py:260
  99.9 0.0 copy-start.8
  100.0 20.9 %all_to_all.11.data_ref = bf16[8,34,16,128]{3,2,1,0:T(8,128)(2,1)S(1)} all-to-all(bf16[8,34,16,128]{3,2,1,0:T(8,128)(2,1)S(1)} %fusion.3), channel_id=1, replica_groups=mesh['sec'=8,'xy'=64] {'sec'}, dimensions={0} | all-to-all | bytes 2228224 | tf_op jit(solution)/shard_map/all_to_all | solution.py:264
  120.9 0.0 copy-done.8
  120.9 0.0 copy-start.7
  120.9 0.0 copy-start.4
  120.9 0.4 edges.1
  121.3 5.0 %collective-permute-start.4 = (bf16[16,4352]{1,0:T(8,128)(2,1)S(1)}, bf16[16,4352]{1,0:T(8,128)(2,1)S(1)}, u32[]{:S(2)}, u32[]{:S(2)}) collective-permute-start(bf16[16,4352]{1,0:T(8,128)(2,1)S(1)} %get-tuple-element.36), channel_id=1, source_target_pairs={{0,1},{1,2},{2,3},{3,4},{4,5},{5,6},{6,7},{7,8},{8,9},{9,10},{10,1... | collective-permute-start | bytes 417800 | tf_op jit(solution)/shard_map/ppermute | solution.py:43
  126.3 2.9 %collective-permute-start.5 = (bf16[16,4352]{1,0:T(8,128)(2,1)S(1)}, bf16[16,4352]{1,0:T(8,128)(2,1)S(1)}, u32[]{:S(2)}, u32[]{:S(2)}) collective-permute-start(bf16[16,4352]{1,0:T(8,128)(2,1)S(1)} %get-tuple-element.37), channel_id=1, source_target_pairs={{1,0},{2,1},{3,2},{4,3},{5,4},{6,5},{7,6},{8,7},{9,8},{10,9},{11,1... | collective-permute-start | bytes 417800 | tf_op jit(solution)/shard_map/ppermute | solution.py:43
  129.2 0.0 copy-done.7
  129.2 3.5 %interior.1 = (bf16[8,16,4096]{2,1,0:T(8,128)(2,1)S(1)}, bf16[32,4352]{1,0:T(8,128)(2,1)S(1)}, bf16[32,4352]{1,0:T(8,128)(2,1)S(1)}) custom-call(s32[4]{0:T(128)S(1)} %add_convert_fusion.place_ref, bf16[336,256]{1,0:T(8,128)(2,1)S(1)} %get-tuple-element.38.first_ref, bf16[384,224]{1,0:T(8,128)(2,1)S(1)} %get-tuple-element.39.second_ref, ...), custom_call_target="tpu_custom_call" | custom-call | tf_op jit(solution)/shard_map/interior/pallas_call | solution.py:272
  132.7 0.0 collective-permute-done.4.left_ref
  132.7 0.5 collective-permute-done.5.right_ref
  133.2 0.0 copy-done.4
  133.2 3.0 %rim.1 = bf16[8,16,4096]{2,1,0:T(8,128)(2,1)} custom-call(s32[4]{0:T(128)S(1)} %add_convert_fusion.place_ref, bf16[96,128]{1,0:T(8,128)(2,1)S(1)} %get-tuple-element.31.first_ref, bf16[96,128]{1,0:T(8,128)(2,1)S(1)} %get-tuple-element.32.second_ref, bf16[128,32]{1,0:T(8,128)(2,1)S(1)} %copy-done.4, bf16[16,4352]{1,0:T(8,128)(2,1)S(1)} %collective-permute-done.4.left_ref, ...), custom_call_target="tpu_custom_call" | custom-call | tf_op jit(solution)/shard_map/rim/pallas_call | solution.py:280
  (8 shorter events, 0.2 us)
Async XLA Ops:
  0.0 13.5 %collective-permute-start = (s32[1,2,2]{2,1,0:T(2,128)}, s32[1,2,2]{2,1,0:T(2,128)S(1)}, u32[]{:S(2)}, u32[]{:S(2)}) collective-permute-start(s32[1,2,2]{2,1,0:T(2,128)} %coarse_ref.1), channel_id=1, source_target_pairs={{1,0},{2,1},{3,2},{4,3},{5,4},{6,5},{7,6},{8,7},{9,8},{10,9},{11,1... | collective-permute-start | bytes 56 | tf_op jit(solution)/shard_map/ppermute | solution.py:43
  11.6 7.8 %collective-permute-start.1 = (s32[1,2,2]{2,1,0:T(2,128)}, s32[1,2,2]{2,1,0:T(2,128)S(1)}, u32[]{:S(2)}, u32[]{:S(2)}) collective-permute-start(s32[1,2,2]{2,1,0:T(2,128)} %coarse_ref.1), channel_id=1, source_target_pairs={{0,1},{1,2},{2,3},{3,4},{4,5},{5,6},{6,7},{7,8},{8,9},{9,10},{10,1... | collective-permute-start | bytes 56 | tf_op jit(solution)/shard_map/ppermute | solution.py:43
  19.4 1.2 copy-start
  21.2 9.9 %copy-start.2 = (s32[128,112]{1,0:T(8,128)S(1)}, s32[128,112]{1,0:T(8,128)}, u32[]{:S(2)}) copy-start(s32[128,112]{1,0:T(8,128)} %constant.32.clone.refs_1_) | copy-start | bytes 172036
  21.3 9.9 %copy-start.3 = (s32[112,128]{1,0:T(8,128)S(1)}, s32[112,128]{1,0:T(8,128)}, u32[]{:S(2)}) copy-start(s32[112,128]{1,0:T(8,128)} %constant.31.clone.refs_0_) | copy-start | bytes 172036
  21.3 9.9 %copy-start.5 = (s32[32,64]{1,0:T(8,128)S(1)}, s32[32,64]{1,0:T(8,128)}, u32[]{:S(2)}) copy-start(s32[32,64]{1,0:T(8,128)} %constant.34.clone.refs_3_) | copy-start | bytes 24580
  21.3 9.9 %copy-start.6 = (s32[32,64]{1,0:T(8,128)S(1)}, s32[32,64]{1,0:T(8,128)}, u32[]{:S(2)}) copy-start(s32[32,64]{1,0:T(8,128)} %constant.33.clone.refs_2_) | copy-start | bytes 24580
  21.3 9.9 %copy-start.9 = (f32[3,3,3]{2,1,0:T(4,128)S(1)}, f32[3,3,3]{2,1,0:T(4,128)}, u32[]{:S(2)}) copy-start(f32[3,3,3]{2,1,0:T(4,128)} %one_ref.1) | copy-start | bytes 328
  21.3 9.8 %copy-start.10 = (f32[3,3,3]{2,1,0:T(4,128)S(1)}, f32[3,3,3]{2,1,0:T(4,128)}, u32[]{:S(2)}) copy-start(f32[3,3,3]{2,1,0:T(4,128)} %two_ref.1) | copy-start | bytes 328
  21.3 16.4 %collective-permute-start.2 = (bf16[1,512,512]{2,1,0:T(8,128)(2,1)S(1)}, bf16[1,512,512]{2,1,0:T(8,128)(2,1)S(1)}, u32[]{:S(2)}, u32[]{:S(2)}) collective-permute-start(bf16[1,512,512]{2,1,0:T(8,128)(2,1)S(1)} %get-tuple-element.24), channel_id=1, source_target_pairs={{0,1},{1,2},{2,3},{3,4},{4,5},{5,6},{6,7},{7,8},{8,9},{9,10},{10,1... | collective-permute-start | bytes 1572872 | tf_op jit(solution)/shard_map/ppermute | solution.py:43
  23.4 15.5 %collective-permute-start.3 = (bf16[1,512,512]{2,1,0:T(8,128)(2,1)S(1)}, bf16[1,512,512]{2,1,0:T(8,128)(2,1)S(1)}, u32[]{:S(2)}, u32[]{:S(2)}) collective-permute-start(bf16[1,512,512]{2,1,0:T(8,128)(2,1)S(1)} %get-tuple-element.25), channel_id=1, source_target_pairs={{1,0},{2,1},{3,2},{4,3},{5,4},{6,5},{7,6},{8,7},{9,8},{10,9},{11,1... | collective-permute-start | bytes 1572872 | tf_op jit(solution)/shard_map/ppermute | solution.py:43
  29.4 0.7 copy-start.11
  30.1 8.8 %copy-start.1 = (bf16[1,512,1024]{2,1,0:T(8,128)(2,1)S(1)}, bf16[1,512,1024]{2,1,0:T(8,128)(2,1)}, u32[]{:S(2)}) copy-start(bf16[1,512,1024]{2,1,0:T(8,128)(2,1)} %source_ref.3) | copy-start | bytes 3145732
  30.1 8.8 %copy-start.12 = (s32[1,2,2]{2,1,0:T(2,128)S(1)}, s32[1,2,2]{2,1,0:T(2,128)}, u32[]{:S(2)}) copy-start(s32[1,2,2]{2,1,0:T(2,128)} %coarse_ref.1) | copy-start | bytes 52
  99.9 20.9 %copy-start.8 = (bf16[32,128]{1,0:T(8,128)(2,1)S(1)}, bf16[32,128]{1,0:T(8,128)(2,1)}, u32[]{:S(2)}) copy-start(bf16[32,128]{1,0:T(8,128)(2,1)} %constant.35.clone.take_ref) | copy-start | bytes 24580
  120.9 8.4 %copy-start.7 = (bf16[32,128]{1,0:T(8,128)(2,1)S(1)}, bf16[32,128]{1,0:T(8,128)(2,1)}, u32[]{:S(2)}) copy-start(bf16[32,128]{1,0:T(8,128)(2,1)} %constant.36.clone.rim_ref) | copy-start | bytes 24580
  120.9 12.4 %copy-start.4 = (bf16[128,32]{1,0:T(8,128)(2,1)S(1)}, bf16[128,32]{1,0:T(8,128)(2,1)}, u32[]{:S(2)}) copy-start(bf16[128,32]{1,0:T(8,128)(2,1)} %constant.37.clone.put_ref) | copy-start | bytes 24580
  121.3 11.5 %collective-permute-start.4 = (bf16[16,4352]{1,0:T(8,128)(2,1)S(1)}, bf16[16,4352]{1,0:T(8,128)(2,1)S(1)}, u32[]{:S(2)}, u32[]{:S(2)}) collective-permute-start(bf16[16,4352]{1,0:T(8,128)(2,1)S(1)} %get-tuple-element.36), channel_id=1, source_target_pairs={{0,1},{1,2},{2,3},{3,4},{4,5},{5,6},{6,7},{7,8},{8,9},{9,10},{10,1... | collective-permute-start | bytes 417800 | tf_op jit(solution)/shard_map/ppermute | solution.py:43
  126.3 7.0 %collective-permute-start.5 = (bf16[16,4352]{1,0:T(8,128)(2,1)S(1)}, bf16[16,4352]{1,0:T(8,128)(2,1)S(1)}, u32[]{:S(2)}, u32[]{:S(2)}) collective-permute-start(bf16[16,4352]{1,0:T(8,128)(2,1)S(1)} %get-tuple-element.37), channel_id=1, source_target_pairs={{1,0},{2,1},{3,2},{4,3},{5,4},{6,5},{7,6},{8,7},{9,8},{10,9},{11,1... | collective-permute-start | bytes 417800 | tf_op jit(solution)/shard_map/ppermute | solution.py:43

commit v4 on v3

--- a/solution.py
+++ b/solution.py
@@ -8,6 +8,7 @@
 
 LANES = 128
 HALO = 2
+PARTS = 2
 BF16 = jnp.bfloat16
 F32 = jnp.float32
 VMEM = pl.BlockSpec(memory_space=pltpu.VMEM)
@@ -39,12 +40,20 @@
     return [(source, source + steps) for source in range(first, last)]
 
 
+def far_pairs(step, count):
+    half = count // 2
+    return [(i, (i // 2 + step // 2) % half * 2 + (i + step) % 2) for i in range(count)]
+
+
 def from_behind(value, axis, steps):
     return lax.ppermute(value, axis, shift_pairs(lax.axis_size(axis), steps))
 
 
-def interpolation(amount, edge):
-    row_index = lax.broadcasted_iota(jnp.int32, (edge, edge), 0)
+def interpolation(amount, edge, cols, parts):
+    order = lax.broadcasted_iota(jnp.int32, (edge, edge), 0)
+    size = cols // parts
+    inside = order % (edge // parts)
+    row_index = inside // size * cols + order // (edge // parts) * size + inside % size
     col_index = lax.broadcasted_iota(jnp.int32, (edge, edge), 1)
     offset = col_index - row_index
     w_before = ((-0.5 * amount + 1.0) * amount - 0.5) * amount
@@ -57,12 +66,14 @@
     return jnp.where(offset == 2, w_beyond, matrix)
 
 
-def matrices_body(fraction_ref, out_ref):
+def matrices_body(cols, parts, fraction_ref, out_ref):
     _, kinds, columns = fraction_ref.shape
     edge = out_ref.shape[-1]
     for kind in range(kinds):
         for block in range(columns):
-            out_ref[kind, block] = interpolation(fraction_ref[0, kind, block], edge).astype(BF16)
+            out_ref[kind, block] = interpolation(
+                fraction_ref[0, kind, block], edge, cols, parts if kind else 1
+            ).astype(BF16)
 
 
 def choose_body(below_ref, above_ref, source_ref, for_below_ref, for_above_ref):
@@ -79,11 +90,12 @@
                 out_ref[0] = source_ref[0, :, column * edge : (column + 1) * edge]
 
 
-def warp_body(coarse_ref, source_ref, above_ref, below_ref, matrix_ref, out_ref):
+def warp_body(coarse_ref, source_ref, above_ref, below_ref, matrix_ref, *out_refs):
     _, edge, width = source_ref.shape
     columns = width // edge
-    groups = out_ref.shape[0] // columns
-    chunks, cols = out_ref.shape[1], out_ref.shape[2]
+    parts = len(out_refs)
+    groups = out_refs[0].shape[0] // columns
+    chunks, cols = out_refs[0].shape[1], out_refs[0].shape[2]
     for block in range(columns):
         down = coarse_ref[0, 0, block]
         anchor = block + coarse_ref[0, 1, block]
@@ -96,11 +108,11 @@
         warped = lax.dot_general(
             matrix_ref[1, block], rows_warped, (((1,), (1,)), ((), ())), preferred_element_type=F32
         ).astype(BF16)
-        warped = warped.reshape(groups, cols, edge)
-        for chunk in range(chunks):
-            out_ref[block * groups : (block + 1) * groups, chunk] = warped[
-                :, :, chunk * LANES : (chunk + 1) * LANES
-            ]
+        size = edge // parts
+        for part, out_ref in enumerate(out_refs):
+            half = warped[part * size : (part + 1) * size].reshape(groups, cols, edge)
+            for chunk in range(chunks):
+                out_ref[block * groups : (block + 1) * groups, chunk] = half[:, :, chunk * LANES : (chunk + 1) * LANES]
 
 
 def tap_index(out_pixels, in_pixels):
@@ -128,14 +140,34 @@
         stencil_matrix(index_ref[...], one_ref if place % 2 == 0 else two_ref, out_ref)
 
 
-def edges_body(data_ref, take_ref, first_ref, last_ref):
+def owner(device, step, count, sign):
+    around = lax.rem(lax.div(device, 2) + (sign * (step // 2)) % (count // 2), count // 2)
+    return around * 2 + lax.rem(lax.rem(device, 2) + step % 2, 2)
+
+
+def spread_body(steps, place_ref, data_ref, *out_refs):
+    total = data_ref.shape[0]
+    for out_ref, step in zip(out_refs, steps):
+        count = out_ref.shape[0] - 2
+        first = owner(place_ref[4], step, len(steps), 1) * count
+        before = data_ref[jnp.maximum(first - 1, 0)]
+        after = data_ref[jnp.minimum(first + count, total - 1)]
+        out_ref[0] = jnp.where(first > 0, before, jnp.zeros_like(before))
+        out_ref[1 : count + 1] = data_ref[pl.ds(first, count)]
+        out_ref[count + 1] = jnp.where(first + count < total, after, jnp.zeros_like(after))
+
+
+def assemble_body(steps, place_ref, *refs):
+    ins, out_ref = refs[:-1], refs[-1]
+    for in_ref, step in zip(ins, steps):
+        out_ref[owner(place_ref[4], step, len(steps), -1)] = in_ref[...]
+
+
+def edges_body(data_ref, take_ref, out_ref):
     sections, chunks, cols, lanes = data_ref.shape
-    side = first_ref.shape[0]
     for chunk in range(chunks):
-        rim = dot(take_ref[...], data_ref[:, chunk].reshape(sections * cols, lanes)).astype(BF16)
-        where = slice(chunk * lanes, (chunk + 1) * lanes)
-        first_ref[:, where] = rim[:side]
-        last_ref[:, where] = rim[side:]
+        block = data_ref[:, chunk].reshape(sections * cols, lanes)
+        out_ref[:, chunk * lanes : (chunk + 1) * lanes] = dot(take_ref[...], block).astype(BF16)
 
 
 def shifted_sum(matrix_ref, volume, rows):
@@ -152,14 +184,16 @@
     return gone | ((lane >= shape[1] - lanes) & (place_ref[3] > 0))
 
 
-def interior_body(place_ref, first_ref, second_ref, rim_ref, data_ref, out_ref, passed_ref, aligned_ref, volume_ref, pass_ref):
-    sections, chunks, cols, lanes = data_ref.shape
-    main = sections * cols
+def interior_body(place_ref, first_ref, second_ref, rim_ref, low_ref, high_ref, out_ref, passed_ref, aligned_ref, volume_ref, pass_ref):
+    sections, chunks, cols, lanes = low_ref.shape
+    half = sections * cols
+    main = 2 * half
     length = chunks * lanes
     for chunk in range(chunks):
-        block = data_ref[:, chunk].reshape(main, lanes)
-        volume_ref[0:main, chunk * lanes : (chunk + 1) * lanes] = block
-        volume_ref[main : 2 * main, chunk * lanes : (chunk + 1) * lanes] = block
+        for start, data_ref in ((0, low_ref), (half, high_ref)):
+            block = data_ref[:, chunk].reshape(half, lanes)
+            volume_ref[start : start + half, chunk * lanes : (chunk + 1) * lanes] = block
+            volume_ref[main + start : main + start + half, chunk * lanes : (chunk + 1) * lanes] = block
     volume = volume_ref[...]
     aligned_ref[...] = dot(rim_ref[...], volume[0:main]).astype(BF16)
     rows = first_ref.shape[0] // 3
@@ -170,9 +204,13 @@
     pass_ref[rows : 2 * rows] = passed
     second = shifted_sum(second_ref, pass_ref[...], main)
     total = (second + volume_ref[0:main, :].astype(F32))[:, lanes : length - lanes]
-    column = lax.broadcasted_iota(jnp.int32, total.shape, 0) % cols
-    inside = (column >= HALO) & (column < cols - HALO)
-    out_ref[...] = jnp.where(inside, total, 0.0).astype(BF16).reshape(out_ref.shape)
+    row = lax.broadcasted_iota(jnp.int32, total.shape, 0)
+    column = jnp.where(row < half, row % cols, cols - 1 - row % cols)
+    total = jnp.where(column >= HALO, total, 0.0).astype(BF16)
+    for part in range(2):
+        out_ref[:, part * cols : (part + 1) * cols, :] = total[part * half : (part + 1) * half].reshape(
+            sections, cols, length - 2 * lanes
+        )
 
 
 def rim_body(place_ref, first_ref, second_ref, put_ref, left_ref, right_ref, passed_ref, aligned_ref, inner_ref, out_ref, volume_ref, pass_ref):
@@ -220,7 +258,9 @@
     )(of_below, of_above, source)
     above, below = from_behind(for_below, "xy", 1), from_behind(for_above, "xy", -1)
 
-    matrix = call(matrices_body, shaped(2, columns, edge, edge), [SMEM], "matrices", 16)(fraction)
+    matrix = call(
+        lambda *refs: matrices_body(cols, PARTS, *refs), shaped(2, columns, edge, edge), [SMEM], "matrices", 16
+    )(fraction)
 
     def pixels(*columns_taken):
         return [(section, column) for section in range(n_sec) for column in columns_taken]
@@ -229,15 +269,17 @@
         return [(section, column) for column in columns_taken for section in range(n_sec)]
 
     last = cols - 1
-    natural = pixels(*range(cols))
+    half = cols // PARTS
+    low, high = pixels(*range(half)), pixels(*range(half, cols))
+    natural, stored = pixels(*range(cols)), low + high
     near = pixels(1, 2, last - 2, last - 1)
     rim = pixels(0, 1, last - 1, last)
     inner_pass = near + pixels(*range(3, last - 2))
     rim_in = rim + pixels(-2, -1) + pixels(last + 1, last + 2)
     rim_pass = by_column(-1, 0, last, last + 1)
-    inner_out = [(s, c) if HALO <= c < cols - HALO else (-9, -9) for s, c in natural]
+    inner_out = [(s, c) if HALO <= c < cols - HALO else (-9, -9) for s, c in stored]
     indices = [
-        tap_index(inner_pass, natural),
+        tap_index(inner_pass, stored),
         tap_index(inner_out, inner_pass),
         tap_index(rim_pass, rim_in),
         tap_index(rim, near + rim_pass),
@@ -251,32 +293,55 @@
     )(kernel_one, kernel_two, *map(jnp.asarray, indices))
 
     at_xy, at_sec = lax.axis_index("xy"), lax.axis_index("sec")
-    place = jnp.stack([at_xy == 0, at_xy == n_xy - 1, at_sec == 0, at_sec == n_sec - 1]).astype(jnp.int32)
+    rims = [at_xy == 0, at_xy == n_xy - 1, at_sec == 0, at_sec == n_sec - 1]
+    place = jnp.stack([*(rim.astype(jnp.int32) for rim in rims), at_sec.astype(jnp.int32)])
     above, below, matrix, stencils, place = lax.optimization_barrier((above, below, matrix, stencils, place))
 
-    strip = call(warp_body, shaped(n_xy, chunks, cols, LANES), [SMEM] + [VMEM] * 4, "warp", 16)(
+    strips = call(warp_body, (shaped(n_xy, chunks, half, LANES),) * PARTS, [SMEM] + [VMEM] * 4, "warp", 16)(
         coarse, source, above, below, matrix
     )
-    mine = lax.all_to_all(strip, "xy", split_axis=0, concat_axis=0, tiled=True)
     per_sec = n_xy * chunks // n_sec
-    mine = jnp.pad(mine.reshape(n_xy * chunks, cols, LANES), ((1, 1), (0, 0), (0, 0)))
-    spread = jnp.stack([mine[index * per_sec : (index + 1) * per_sec + 2] for index in range(n_sec)])
-    data = lax.all_to_all(spread, "sec", split_axis=0, concat_axis=0, tiled=True)
-
     length = (per_sec + 2) * LANES
+
+    def over_xy(strip):
+        part = lax.all_to_all(strip, "xy", split_axis=0, concat_axis=0, tiled=True)
+        return part.reshape(n_xy * chunks, half, LANES)
+
+    def rim_of(data, taken, held, name):
+        return call(edges_body, shaped(n_sec * HALO, length), [VMEM, VMEM], name, 8)(data, one_hot(taken, held))
+
+    first_part = over_xy(strips[0])
+    second_part = over_xy(strips[1])
+    far = [step for step in range(n_sec) if step != 0]
+    far = [0] + sorted(far, key=lambda step: -min(step // 2, n_sec // 2 - step // 2))
+
+    pieces = call(
+        lambda *refs: spread_body(far, *refs), (shaped(per_sec + 2, half, LANES),) * n_sec, [SMEM, VMEM], "spread", 8
+    )(place, first_part)
+    pieces = [pieces[0]] + [
+        lax.ppermute(piece, "sec", far_pairs(step, n_sec))
+        for step, piece in zip(far[1:], pieces[1:])
+    ]
+    data_low = call(
+        lambda *refs: assemble_body(far, *refs), shaped(n_sec, per_sec + 2, half, LANES), [SMEM] + [VMEM] * n_sec, "assemble", 8
+    )(place, *pieces)
+    right = from_behind(rim_of(data_low, pixels(0, 1), low, "firsts"), "xy", -1)
+    second_part, data_low, right = lax.optimization_barrier((second_part, data_low, right))
+
+    second_part = jnp.pad(second_part, ((1, 1), (0, 0), (0, 0)))
+    spread = jnp.stack([second_part[index * per_sec : (index + 1) * per_sec + 2] for index in range(n_sec)])
+    data_high = lax.all_to_all(spread, "sec", split_axis=0, concat_axis=0, tiled=True)
+    left = from_behind(rim_of(data_high, pixels(last - 1, last), high, "lasts"), "xy", 1)
+
     out = shaped(n_sec, cols, per_sec * LANES)
-    firsts, lasts = call(
-        edges_body, (shaped(n_sec * HALO, length),) * 2, [VMEM, VMEM], "edges", 8
-    )(data, one_hot(pixels(0, 1) + pixels(last - 1, last), natural))
-    left, right = from_behind(lasts, "xy", 1), from_behind(firsts, "xy", -1)
     inner, passed, aligned = call(
         interior_body,
         (out, shaped(len(near), length), shaped(len(rim), length)),
-        [SMEM] + [VMEM] * 4,
+        [SMEM] + [VMEM] * 5,
         "interior",
         32,
         [pltpu.VMEM((2 * len(natural), length), BF16), pltpu.VMEM((2 * len(inner_pass), length), BF16)],
-    )(place, stencils[0], stencils[1], one_hot(rim, natural), data)
+    )(place, stencils[0], stencils[1], one_hot(rim, stored), data_low, data_high)
     return call(
         rim_body,
         out,

time: 137 us -> 150 us (1.095)
  starting transfers between devices: 29.5 us -> 58.3 us
  blocking collectives: 79.7 us -> 52.4 us
  local copies, waits for them, and re-layouts: 2.11 us -> 7.75 us
  Pallas kernels: 11.7 us -> 15.5 us
  waiting for transfers between devices: 12.9 us -> 14.9 us
    ppermute x0 -> x7, starting transfers between devices: none -> 21.7 us  [body(): lax.ppermute(piece, 'sec', far_pairs(step, n_sec))]
    all_to_all x1, blocking collectives: 58.8 us -> 38.1 us  [over_xy(): part = lax.all_to_all(strip, 'xy', split_axis=0, concat_axis=0, tiled=True)]
    all_to_all x0 -> x1, starting transfers between devices: none -> 7.31 us  [over_xy(): part = lax.all_to_all(strip, 'xy', split_axis=0, concat_axis=0, tiled=True)]
    all_to_all x1, blocking collectives: 20.9 us -> 14.3 us  [body(): lax.all_to_all(spread, 'sec', split_axis=0, concat_axis=0, tiled=True)]
    unnamed x33 -> x43, local copies, waits for them, and re-layouts: 2.09 us -> 7.07 us
    pallas_call x3 -> x6, Pallas kernels: 3.43 us -> 6.37 us  [the longest x1 2.65 us: body(): call(warp_body, (shaped(n_xy, chunks, half, LANES),) * PARTS, [SMEM] + [V...]
  transfers between devices with their start and end apart: 6 -> 14, of which waited for: 4 -> 5; matrix products, arithmetic and copies ran while one was open for 0% -> 0% of each run, Pallas kernels for 4% -> 5%
where the time goes in v4:
time: 150 us; the launch traced here: 149 us
  starting transfers between devices  58.3 us (39%)
  blocking collectives  52.4 us (35%)
  Pallas kernels  15.5 us (10%)
  waiting for transfers between devices  14.9 us (10%)
  local copies, waits for them, and re-layouts  7.75 us (5%)
    all_to_all x1, blocking collectives, over_xy(): part = lax.all_to_all(strip, 'xy', split_axis=0, concat_axis=0, tiled=True)  38.1 us
    ppermute x6, starting transfers between devices, from_behind(): return lax.ppermute(value, axis, shift_pairs(lax.axis_size(axis), steps))  29.3 us
    ppermute x7, starting transfers between devices, body(): lax.ppermute(piece, 'sec', far_pairs(step, n_sec))  21.7 us
    all_to_all x1, blocking collectives, body(): lax.all_to_all(spread, 'sec', split_axis=0, concat_axis=0, tiled=True)  14.3 us
    ppermute x6, waiting for transfers between devices, from_behind(): return lax.ppermute(value, axis, shift_pairs(lax.axis_size(axis), steps))  13.8 us
    all_to_all x1, starting transfers between devices, over_xy(): part = lax.all_to_all(strip, 'xy', split_axis=0, concat_axis=0, tiled=True)  7.31 us
    unnamed x43, local copies, waits for them, and re-layouts  7.07 us
    pallas_call x1, Pallas kernels, body(): call(interior_body, (out, shaped(len(near), length), shaped(len(rim), len...  3.44 us
  transfers between devices with their start and end apart: 14, of which 5 were waited for; matrix products, arithmetic and copies ran while one was open for 0% of the time, Pallas kernels for 5%

profile of v4, /device:TPU:24, one launch (start us, length us, event | category | flops | bytes accessed | tf_op | source)
XLA Modules:
  0.0 149.3 jit_solution(12026105015085846730)
XLA Ops:
  0.0 11.6 %collective-permute-start = (s32[1,2,2]{2,1,0:T(2,128)}, s32[1,2,2]{2,1,0:T(2,128)S(1)}, u32[]{:S(2)}, u32[]{:S(2)}) collective-permute-start(s32[1,2,2]{2,1,0:T(2,128)} %coarse_ref.1), channel_id=1, source_target_pairs={{1,0},{2,1},{3,2},{4,3},{5,4},{6,5},{7,6},{8,7},{9,8},{10,9},{11,1... | collective-permute-start | bytes 56 | tf_op jit(solution)/shard_map/ppermute | solution.py:49
  11.6 1.9 %collective-permute-start.1 = (s32[1,2,2]{2,1,0:T(2,128)}, s32[1,2,2]{2,1,0:T(2,128)S(1)}, u32[]{:S(2)}, u32[]{:S(2)}) collective-permute-start(s32[1,2,2]{2,1,0:T(2,128)} %coarse_ref.1), channel_id=1, source_target_pairs={{0,1},{1,2},{2,3},{3,4},{4,5},{5,6},{6,7},{7,8},{8,9},{9,10},{10,1... | collective-permute-start | bytes 56 | tf_op jit(solution)/shard_map/ppermute | solution.py:49
  13.5 0.0 collective-permute-done.below_ref
  13.5 5.8 %collective-permute-done.1.above_ref = s32[1,2,2]{2,1,0:T(2,128)S(1)} collective-permute-done((s32[1,2,2]{2,1,0:T(2,128)}, s32[1,2,2]{2,1,0:T(2,128)S(1)}, u32[]{:S(2)}, u32[]{:S(2)}) %collective-permute-start.1) | collective-permute-done | bytes 48 | tf_op jit(solution)/shard_map/ppermute | solution.py:49
  19.4 1.2 copy-done
  20.6 1.6 %choose.1 = (bf16[1,512,512]{2,1,0:T(8,128)(2,1)}, bf16[1,512,512]{2,1,0:T(8,128)(2,1)}) custom-call(s32[1,2,2]{2,1,0:T(2,128)S(1)} %collective-permute-done.below_ref, s32[1,2,2]{2,1,0:T(2,128)S(1)} %collective-permute-done.1.above_ref, bf16[1,512,1024]{2,1,0:T(8,128)(2,1)S(1)} %copy-done), custom_call_target="tpu_custom_call" | custom-call | tf_op jit(solution)/shard_map/choose/pallas_call | solution.py:256
  22.2 1.9 %collective-permute-start.2 = (bf16[1,512,512]{2,1,0:T(8,128)(2,1)}, bf16[1,512,512]{2,1,0:T(8,128)(2,1)}, u32[]{:S(2)}, u32[]{:S(2)}) collective-permute-start(bf16[1,512,512]{2,1,0:T(8,128)(2,1)} %get-tuple-element.35), channel_id=1, source_target_pairs={{0,1},{1,2},{2,3},{3,4},{4,5},{5,6},{6,7},{7,8},{8,9},{9,10},{10,1... | collective-permute-start | bytes 1572872 | tf_op jit(solution)/shard_map/ppermute | solution.py:49
  24.1 6.0 %collective-permute-start.3 = (bf16[1,512,512]{2,1,0:T(8,128)(2,1)}, bf16[1,512,512]{2,1,0:T(8,128)(2,1)}, u32[]{:S(2)}, u32[]{:S(2)}) collective-permute-start(bf16[1,512,512]{2,1,0:T(8,128)(2,1)} %get-tuple-element.36), channel_id=1, source_target_pairs={{1,0},{2,1},{3,2},{4,3},{5,4},{6,5},{7,6},{8,7},{9,8},{10,9},{11,1... | collective-permute-start | bytes 1572872 | tf_op jit(solution)/shard_map/ppermute | solution.py:49
  30.2 0.0 copy-start.16
  30.2 0.7 copy-done.16
  30.9 2.0 %matrices.1.matrix_ref = bf16[2,2,512,512]{3,2,1,0:T(8,128)(2,1)S(1)} custom-call(f32[1,2,2]{2,1,0:T(2,128)S(1)} %copy-done.16), custom_call_target="tpu_custom_call" | custom-call | tf_op jit(solution)/shard_map/matrices/pallas_call | solution.py:261
  32.9 0.7 stack.66.refs_0_.place_ref
  33.5 0.0 copy-done.8
  33.5 0.8 copy-done.3
  34.4 0.8 copy-done.4
  35.2 0.7 copy-done.9
  35.9 0.7 copy-done.12
  36.6 0.7 copy-done.13
  37.3 1.1 stencils.1
  38.4 0.0 copy-start.6
  38.4 0.6 copy-done.6
  39.0 0.0 collective-permute-done.2.above_ref
  39.0 1.0 collective-permute-done.3.below_ref
  39.9 0.0 copy-done.1
  39.9 0.7 copy-done.17
  40.6 2.6 %warp.1 = (bf16[64,4,8,128]{3,2,1,0:T(8,128)(2,1)S(1)}, bf16[64,4,8,128]{3,2,1,0:T(8,128)(2,1)S(1)}) custom-call(s32[1,2,2]{2,1,0:T(2,128)S(1)} %copy-done.17, bf16[1,512,1024]{2,1,0:T(8,128)(2,1)S(1)} %copy-done.1, bf16[1,512,512]{2,1,0:T(8,128)(2,1)} %collective-permute-done.2.above_ref, bf16[1,512,512]{2,1,0:T(8,128)(2,1)} %collective-permute-done.3.below_ref, ...), custom_call_target="tpu_custom_call" | custom-call | tf_op jit(solution)/shard_map/warp/pallas_call | solution.py:300
  43.3 0.0 copy-start.2
  43.3 0.0 copy-start.10
  43.3 0.0 copy-start.15
  43.3 38.1 %all_to_all.15 = bf16[64,4,8,128]{3,2,1,0:T(8,128)(2,1)S(1)} all-to-all(bf16[64,4,8,128]{3,2,1,0:T(8,128)(2,1)S(1)} %get-tuple-element.48), channel_id=1, replica_groups=mesh['sec'=8,'xy'=64] {'xy'}, dimensions={0} | all-to-all | bytes 1048576 | tf_op jit(solution)/shard_map/all_to_all | solution.py:307
  81.4 0.0 copy-done.2
  81.4 7.3 %all-to-all-start = ((bf16[64,4,8,128]{3,2,1,0:T(8,128)(2,1)}), bf16[64,4,8,128]{3,2,1,0:T(8,128)(2,1)S(1)}, u32[]{:S(2)}, u32[]{:S(2)}) async-start(bf16[64,4,8,128]{3,2,1,0:T(8,128)(2,1)} %copy-done.2), calls=%async_computation | async-start | bytes 1048576 | tf_op jit(solution)/shard_map/all_to_all | solution.py:307
  88.7 0.0 copy-done.10
  88.8 0.6 spread.1
  89.4 4.9 %collective-permute-start.4 = (bf16[34,8,128]{2,1,0:T(8,128)(2,1)S(1)}, bf16[34,8,128]{2,1,0:T(8,128)(2,1)S(1)}, u32[]{:S(2)}, u32[]{:S(2)}) collective-permute-start(bf16[34,8,128]{2,1,0:T(8,128)(2,1)S(1)} %get-tuple-element.50), channel_id=1, source_target_pairs={{0,256},{64,320},{128,384},{192,448},{256,0},{320,64},{384,128},{4... | collective-permute-start | bytes 208904 | tf_op jit(solution)/shard_map/ppermute | solution.py:322
  94.3 1.9 %collective-permute-start.5 = (bf16[34,8,128]{2,1,0:T(8,128)(2,1)S(1)}, bf16[34,8,128]{2,1,0:T(8,128)(2,1)S(1)}, u32[]{:S(2)}, u32[]{:S(2)}) collective-permute-start(bf16[34,8,128]{2,1,0:T(8,128)(2,1)S(1)} %get-tuple-element.51), channel_id=1, source_target_pairs={{0,320},{64,256},{128,448},{192,384},{256,64},{320,0},{384,192},{4... | collective-permute-start | bytes 208904 | tf_op jit(solution)/shard_map/ppermute | solution.py:322
  96.2 2.5 %collective-permute-start.6 = (bf16[34,8,128]{2,1,0:T(8,128)(2,1)S(1)}, bf16[34,8,128]{2,1,0:T(8,128)(2,1)S(1)}, u32[]{:S(2)}, u32[]{:S(2)}) collective-permute-start(bf16[34,8,128]{2,1,0:T(8,128)(2,1)S(1)} %get-tuple-element.52), channel_id=1, source_target_pairs={{0,128},{64,192},{128,256},{192,320},{256,384},{320,448},{384,0},{... | collective-permute-start | bytes 208904 | tf_op jit(solution)/shard_map/ppermute | solution.py:322
  98.8 4.2 %collective-permute-start.7 = (bf16[34,8,128]{2,1,0:T(8,128)(2,1)S(1)}, bf16[34,8,128]{2,1,0:T(8,128)(2,1)S(1)}, u32[]{:S(2)}, u32[]{:S(2)}) collective-permute-start(bf16[34,8,128]{2,1,0:T(8,128)(2,1)S(1)} %get-tuple-element.53), channel_id=1, source_target_pairs={{0,192},{64,128},{128,320},{192,256},{256,448},{320,384},{384,64},... | collective-permute-start | bytes 208904 | tf_op jit(solution)/shard_map/ppermute | solution.py:322
  103.0 3.7 %collective-permute-start.8 = (bf16[34,8,128]{2,1,0:T(8,128)(2,1)S(1)}, bf16[34,8,128]{2,1,0:T(8,128)(2,1)S(1)}, u32[]{:S(2)}, u32[]{:S(2)}) collective-permute-start(bf16[34,8,128]{2,1,0:T(8,128)(2,1)S(1)} %get-tuple-element.54), channel_id=1, source_target_pairs={{0,384},{64,448},{128,0},{192,64},{256,128},{320,192},{384,256},{4... | collective-permute-start | bytes 208904 | tf_op jit(solution)/shard_map/ppermute | solution.py:322
  106.7 0.0 collective-permute-done.4.refs_2_
  106.7 1.9 %collective-permute-start.9 = (bf16[34,8,128]{2,1,0:T(8,128)(2,1)S(1)}, bf16[34,8,128]{2,1,0:T(8,128)(2,1)S(1)}, u32[]{:S(2)}, u32[]{:S(2)}) collective-permute-start(bf16[34,8,128]{2,1,0:T(8,128)(2,1)S(1)} %get-tuple-element.55), channel_id=1, source_target_pairs={{0,448},{64,384},{128,64},{192,0},{256,192},{320,128},{384,320},{4... | collective-permute-start | bytes 208904 | tf_op jit(solution)/shard_map/ppermute | solution.py:322
  108.6 0.0 collective-permute-done.5.refs_3_
  108.6 2.5 %collective-permute-start.10 = (bf16[34,8,128]{2,1,0:T(8,128)(2,1)S(1)}, bf16[34,8,128]{2,1,0:T(8,128)(2,1)S(1)}, u32[]{:S(2)}, u32[]{:S(2)}) collective-permute-start(bf16[34,8,128]{2,1,0:T(8,128)(2,1)S(1)} %get-tuple-element.56), channel_id=1, source_target_pairs={{0,64},{64,0},{128,192},{192,128},{256,320},{320,256},{384,448},{4... | collective-permute-start | bytes 208904 | tf_op jit(solution)/shard_map/ppermute | solution.py:322
  111.2 0.0 collective-permute-done.6.refs_4_
  111.2 0.0 collective-permute-done.7.refs_5_
  111.2 0.0 collective-permute-done.8.refs_6_
  111.2 1.1 collective-permute-done.9.refs_7_
  112.3 0.0 collective-permute-done.10.refs_8_
  112.3 0.6 assemble.1.data_ref.low_ref
  112.9 0.0 copy-done.15
  112.9 0.0 copy-start.14
  112.9 0.0 copy-start.11
  112.9 0.3 firsts.1
  113.2 4.9 %collective-permute-start.11 = (bf16[16,4352]{1,0:T(8,128)(2,1)S(1)}, bf16[16,4352]{1,0:T(8,128)(2,1)S(1)}, u32[]{:S(2)}, u32[]{:S(2)}) collective-permute-start(bf16[16,4352]{1,0:T(8,128)(2,1)S(1)} %firsts.1), channel_id=1, source_target_pairs={{1,0},{2,1},{3,2},{4,3},{5,4},{6,5},{7,6},{8,7},{9,8},{10,9},{11,1... | collective-permute-start | bytes 417800 | tf_op jit(solution)/shard_map/ppermute | solution.py:49
  118.1 0.0 all-to-all-done
  118.1 3.2 %collective-permute-done.11.right_ref = bf16[16,4352]{1,0:T(8,128)(2,1)S(1)} collective-permute-done((bf16[16,4352]{1,0:T(8,128)(2,1)S(1)}, bf16[16,4352]{1,0:T(8,128)(2,1)S(1)}, u32[]{:S(2)}, u32[]{:S(2)}) %collective-permute-start.11) | collective-permute-done | bytes 139296 | tf_op jit(solution)/shard_map/ppermute | solution.py:49
  121.3 0.0 copy-start.5
  121.3 0.0 copy-start.7
  121.4 14.3 %all_to_all.16.data_ref.high_ref = bf16[8,34,8,128]{3,2,1,0:T(8,128)(2,1)S(1)} all-to-all(bf16[8,34,8,128]{3,2,1,0:T(8,128)(2,1)S(1)} %fusion.3), channel_id=1, replica_groups=mesh['sec'=8,'xy'=64] {'sec'}, dimensions={0} | all-to-all | bytes 1114112 | tf_op jit(solution)/shard_map/all_to_all | solution.py:333
  135.7 0.3 lasts.1
  136.0 3.0 %collective-permute-start.12 = (bf16[16,4352]{1,0:T(8,128)(2,1)S(1)}, bf16[16,4352]{1,0:T(8,128)(2,1)S(1)}, u32[]{:S(2)}, u32[]{:S(2)}) collective-permute-start(bf16[16,4352]{1,0:T(8,128)(2,1)S(1)} %lasts.1), channel_id=1, source_target_pairs={{0,1},{1,2},{2,3},{3,4},{4,5},{5,6},{6,7},{7,8},{8,9},{9,10},{10,1... | collective-permute-start | bytes 417800 | tf_op jit(solution)/shard_map/ppermute | solution.py:49
  139.0 3.4 %interior.1 = (bf16[8,16,4096]{2,1,0:T(8,128)(2,1)S(1)}, bf16[32,4352]{1,0:T(8,128)(2,1)S(1)}, bf16[32,4352]{1,0:T(8,128)(2,1)S(1)}) custom-call(s32[5]{0:T(128)S(1)} %copy-done.10, bf16[336,256]{1,0:T(8,128)(2,1)S(1)} %get-tuple-element.59.first_ref, bf16[384,224]{1,0:T(8,128)(2,1)S(1)} %get-tuple-element.60.second_ref, bf16[32,128]{1,0:T(8,128)(2,1)S(1)} %copy-done.11, ...), custom_call_target="tpu_custom_call" | custom-call | tf_op jit(solution)/shard_map/interior/pallas_call | solution.py:337
  142.4 3.8 %collective-permute-done.12.left_ref = bf16[16,4352]{1,0:T(8,128)(2,1)S(1)} collective-permute-done((bf16[16,4352]{1,0:T(8,128)(2,1)S(1)}, bf16[16,4352]{1,0:T(8,128)(2,1)S(1)}, u32[]{:S(2)}, u32[]{:S(2)}) %collective-permute-start.12) | collective-permute-done | bytes 139296 | tf_op jit(solution)/shard_map/ppermute | solution.py:49
  146.3 3.0 %rim.1 = bf16[8,16,4096]{2,1,0:T(8,128)(2,1)} custom-call(s32[5]{0:T(128)S(1)} %copy-done.10, bf16[96,128]{1,0:T(8,128)(2,1)S(1)} %get-tuple-element.42.first_ref, bf16[96,128]{1,0:T(8,128)(2,1)S(1)} %copy-done.7, bf16[128,32]{1,0:T(8,128)(2,1)S(1)} %copy-done.5, bf16[16,4352]{1,0:T(8,128)(2,1)S(1)} %collective-permute-done.12.left_ref, ...), custom_call_target="tpu_custom_call" | custom-call | tf_op jit(solution)/shard_map/rim/pallas_call | solution.py:345
  (21 shorter events, 0.1 us)
Async XLA Ops:
  0.0 13.5 %collective-permute-start = (s32[1,2,2]{2,1,0:T(2,128)}, s32[1,2,2]{2,1,0:T(2,128)S(1)}, u32[]{:S(2)}, u32[]{:S(2)}) collective-permute-start(s32[1,2,2]{2,1,0:T(2,128)} %coarse_ref.1), channel_id=1, source_target_pairs={{1,0},{2,1},{3,2},{4,3},{5,4},{6,5},{7,6},{8,7},{9,8},{10,9},{11,1... | collective-permute-start | bytes 56 | tf_op jit(solution)/shard_map/ppermute | solution.py:49
  11.6 7.8 %collective-permute-start.1 = (s32[1,2,2]{2,1,0:T(2,128)}, s32[1,2,2]{2,1,0:T(2,128)S(1)}, u32[]{:S(2)}, u32[]{:S(2)}) collective-permute-start(s32[1,2,2]{2,1,0:T(2,128)} %coarse_ref.1), channel_id=1, source_target_pairs={{0,1},{1,2},{2,3},{3,4},{4,5},{5,6},{6,7},{7,8},{8,9},{9,10},{10,1... | collective-permute-start | bytes 56 | tf_op jit(solution)/shard_map/ppermute | solution.py:49
  19.4 1.2 copy-start
  20.6 12.9 %copy-start.8 = (s32[32,64]{1,0:T(8,128)S(1)}, s32[32,64]{1,0:T(8,128)}, u32[]{:S(2)}) copy-start(s32[32,64]{1,0:T(8,128)} %constant.36.clone.refs_3_) | copy-start | bytes 24580
  20.6 19.3 %copy-start.1 = (bf16[1,512,1024]{2,1,0:T(8,128)(2,1)S(1)}, bf16[1,512,1024]{2,1,0:T(8,128)(2,1)}, u32[]{:S(2)}) copy-start(bf16[1,512,1024]{2,1,0:T(8,128)(2,1)} %source_ref.3) | copy-start | bytes 3145732
  22.2 16.8 %collective-permute-start.2 = (bf16[1,512,512]{2,1,0:T(8,128)(2,1)}, bf16[1,512,512]{2,1,0:T(8,128)(2,1)}, u32[]{:S(2)}, u32[]{:S(2)}) collective-permute-start(bf16[1,512,512]{2,1,0:T(8,128)(2,1)} %get-tuple-element.35), channel_id=1, source_target_pairs={{0,1},{1,2},{2,3},{3,4},{4,5},{5,6},{6,7},{7,8},{8,9},{9,10},{10,1... | collective-permute-start | bytes 1572872 | tf_op jit(solution)/shard_map/ppermute | solution.py:49
  24.1 15.8 %collective-permute-start.3 = (bf16[1,512,512]{2,1,0:T(8,128)(2,1)}, bf16[1,512,512]{2,1,0:T(8,128)(2,1)}, u32[]{:S(2)}, u32[]{:S(2)}) collective-permute-start(bf16[1,512,512]{2,1,0:T(8,128)(2,1)} %get-tuple-element.36), channel_id=1, source_target_pairs={{1,0},{2,1},{3,2},{4,3},{5,4},{6,5},{7,6},{8,7},{9,8},{10,9},{11,1... | collective-permute-start | bytes 1572872 | tf_op jit(solution)/shard_map/ppermute | solution.py:49
  30.2 0.7 copy-start.16
  33.5 0.8 copy-start.3
  34.4 0.8 copy-start.4
  35.2 0.7 copy-start.9
  35.9 0.7 copy-start.12
  36.6 0.7 copy-start.13
  38.4 0.6 copy-start.6
  39.9 0.7 copy-start.17
  43.3 38.2 %copy-start.2 = (bf16[64,4,8,128]{3,2,1,0:T(8,128)(2,1)}, bf16[64,4,8,128]{3,2,1,0:T(8,128)(2,1)S(1)}, u32[]{:S(2)}) copy-start(bf16[64,4,8,128]{3,2,1,0:T(8,128)(2,1)S(1)} %get-tuple-element.47) | copy-start | bytes 1572868
  43.3 45.5 %copy-start.10 = (s32[5]{0:T(128)S(1)}, s32[5]{0:T(128)}, u32[]{:S(2)}) copy-start(s32[5]{0:T(128)} %stack.66.refs_0_.place_ref) | copy-start | bytes 64
  43.3 69.6 %copy-start.15 = (bf16[16,64]{1,0:T(8,128)(2,1)S(1)}, bf16[16,64]{1,0:T(8,128)(2,1)}, u32[]{:S(2)}) copy-start(bf16[16,64]{1,0:T(8,128)(2,1)} %constant.37.clone.take_ref) | copy-start | bytes 6148
  81.4 36.6 %all-to-all-start = ((bf16[64,4,8,128]{3,2,1,0:T(8,128)(2,1)}), bf16[64,4,8,128]{3,2,1,0:T(8,128)(2,1)S(1)}, u32[]{:S(2)}, u32[]{:S(2)}) async-start(bf16[64,4,8,128]{3,2,1,0:T(8,128)(2,1)} %copy-done.2), calls=%async_computation | async-start | bytes 1048576 | tf_op jit(solution)/shard_map/all_to_all | solution.py:307
  89.4 17.3 %collective-permute-start.4 = (bf16[34,8,128]{2,1,0:T(8,128)(2,1)S(1)}, bf16[34,8,128]{2,1,0:T(8,128)(2,1)S(1)}, u32[]{:S(2)}, u32[]{:S(2)}) collective-permute-start(bf16[34,8,128]{2,1,0:T(8,128)(2,1)S(1)} %get-tuple-element.50), channel_id=1, source_target_pairs={{0,256},{64,320},{128,384},{192,448},{256,0},{320,64},{384,128},{4... | collective-permute-start | bytes 208904 | tf_op jit(solution)/shard_map/ppermute | solution.py:322
  94.3 14.3 %collective-permute-start.5 = (bf16[34,8,128]{2,1,0:T(8,128)(2,1)S(1)}, bf16[34,8,128]{2,1,0:T(8,128)(2,1)S(1)}, u32[]{:S(2)}, u32[]{:S(2)}) collective-permute-start(bf16[34,8,128]{2,1,0:T(8,128)(2,1)S(1)} %get-tuple-element.51), channel_id=1, source_target_pairs={{0,320},{64,256},{128,448},{192,384},{256,64},{320,0},{384,192},{4... | collective-permute-start | bytes 208904 | tf_op jit(solution)/shard_map/ppermute | solution.py:322
  96.2 14.9 %collective-permute-start.6 = (bf16[34,8,128]{2,1,0:T(8,128)(2,1)S(1)}, bf16[34,8,128]{2,1,0:T(8,128)(2,1)S(1)}, u32[]{:S(2)}, u32[]{:S(2)}) collective-permute-start(bf16[34,8,128]{2,1,0:T(8,128)(2,1)S(1)} %get-tuple-element.52), channel_id=1, source_target_pairs={{0,128},{64,192},{128,256},{192,320},{256,384},{320,448},{384,0},{... | collective-permute-start | bytes 208904 | tf_op jit(solution)/shard_map/ppermute | solution.py:322
  98.8 12.4 %collective-permute-start.7 = (bf16[34,8,128]{2,1,0:T(8,128)(2,1)S(1)}, bf16[34,8,128]{2,1,0:T(8,128)(2,1)S(1)}, u32[]{:S(2)}, u32[]{:S(2)}) collective-permute-start(bf16[34,8,128]{2,1,0:T(8,128)(2,1)S(1)} %get-tuple-element.53), channel_id=1, source_target_pairs={{0,192},{64,128},{128,320},{192,256},{256,448},{320,384},{384,64},... | collective-permute-start | bytes 208904 | tf_op jit(solution)/shard_map/ppermute | solution.py:322
  103.0 8.2 %collective-permute-start.8 = (bf16[34,8,128]{2,1,0:T(8,128)(2,1)S(1)}, bf16[34,8,128]{2,1,0:T(8,128)(2,1)S(1)}, u32[]{:S(2)}, u32[]{:S(2)}) collective-permute-start(bf16[34,8,128]{2,1,0:T(8,128)(2,1)S(1)} %get-tuple-element.54), channel_id=1, source_target_pairs={{0,384},{64,448},{128,0},{192,64},{256,128},{320,192},{384,256},{4... | collective-permute-start | bytes 208904 | tf_op jit(solution)/shard_map/ppermute | solution.py:322
  106.7 5.6 %collective-permute-start.9 = (bf16[34,8,128]{2,1,0:T(8,128)(2,1)S(1)}, bf16[34,8,128]{2,1,0:T(8,128)(2,1)S(1)}, u32[]{:S(2)}, u32[]{:S(2)}) collective-permute-start(bf16[34,8,128]{2,1,0:T(8,128)(2,1)S(1)} %get-tuple-element.55), channel_id=1, source_target_pairs={{0,448},{64,384},{128,64},{192,0},{256,192},{320,128},{384,320},{4... | collective-permute-start | bytes 208904 | tf_op jit(solution)/shard_map/ppermute | solution.py:322
  108.6 3.7 %collective-permute-start.10 = (bf16[34,8,128]{2,1,0:T(8,128)(2,1)S(1)}, bf16[34,8,128]{2,1,0:T(8,128)(2,1)S(1)}, u32[]{:S(2)}, u32[]{:S(2)}) collective-permute-start(bf16[34,8,128]{2,1,0:T(8,128)(2,1)S(1)} %get-tuple-element.56), channel_id=1, source_target_pairs={{0,64},{64,0},{128,192},{192,128},{256,320},{320,256},{384,448},{4... | collective-permute-start | bytes 208904 | tf_op jit(solution)/shard_map/ppermute | solution.py:322
  112.9 22.8 %copy-start.14 = (bf16[16,64]{1,0:T(8,128)(2,1)S(1)}, bf16[16,64]{1,0:T(8,128)(2,1)}, u32[]{:S(2)}) copy-start(bf16[16,64]{1,0:T(8,128)(2,1)} %constant.38.clone.take_ref) | copy-start | bytes 6148
  112.9 26.1 %copy-start.11 = (bf16[32,128]{1,0:T(8,128)(2,1)S(1)}, bf16[32,128]{1,0:T(8,128)(2,1)}, u32[]{:S(2)}) copy-start(bf16[32,128]{1,0:T(8,128)(2,1)} %constant.39.clone.rim_ref) | copy-start | bytes 24580
  113.2 8.0 %collective-permute-start.11 = (bf16[16,4352]{1,0:T(8,128)(2,1)S(1)}, bf16[16,4352]{1,0:T(8,128)(2,1)S(1)}, u32[]{:S(2)}, u32[]{:S(2)}) collective-permute-start(bf16[16,4352]{1,0:T(8,128)(2,1)S(1)} %firsts.1), channel_id=1, source_target_pairs={{1,0},{2,1},{3,2},{4,3},{5,4},{6,5},{7,6},{8,7},{9,8},{10,9},{11,1... | collective-permute-start | bytes 417800 | tf_op jit(solution)/shard_map/ppermute | solution.py:49
  121.3 24.9 %copy-start.5 = (bf16[128,32]{1,0:T(8,128)(2,1)S(1)}, bf16[128,32]{1,0:T(8,128)(2,1)}, u32[]{:S(2)}) copy-start(bf16[128,32]{1,0:T(8,128)(2,1)} %constant.40.clone.put_ref) | copy-start | bytes 24580
  121.3 24.9 %copy-start.7 = (bf16[96,128]{1,0:T(8,128)(2,1)S(1)}, bf16[96,128]{1,0:T(8,128)(2,1)}, u32[]{:S(2)}) copy-start(bf16[96,128]{1,0:T(8,128)(2,1)} %copy-done.6) | copy-start | bytes 73732
  136.0 10.3 %collective-permute-start.12 = (bf16[16,4352]{1,0:T(8,128)(2,1)S(1)}, bf16[16,4352]{1,0:T(8,128)(2,1)S(1)}, u32[]{:S(2)}, u32[]{:S(2)}) collective-permute-start(bf16[16,4352]{1,0:T(8,128)(2,1)S(1)} %lasts.1), channel_id=1, source_target_pairs={{0,1},{1,2},{2,3},{3,4},{4,5},{5,6},{6,7},{7,8},{8,9},{9,10},{10,1... | collective-permute-start | bytes 417800 | tf_op jit(solution)/shard_map/ppermute | solution.py:49

commit v5 on v3

--- a/solution.py
+++ b/solution.py
@@ -12,14 +12,15 @@
 F32 = jnp.float32
 VMEM = pl.BlockSpec(memory_space=pltpu.VMEM)
 SMEM = pl.BlockSpec(memory_space=pltpu.SMEM)
-
-
-def call(body, outs, ins, name, mib, scratch=()):
+ANY = pl.BlockSpec(memory_space=pl.ANY)
+
+
+def call(body, outs, ins, name, mib, scratch=(), space=VMEM):
     return pl.pallas_call(
         body,
         out_shape=outs,
         in_specs=ins,
-        out_specs=jax.tree.map(lambda _: VMEM, outs),
+        out_specs=jax.tree.map(lambda _: space, outs),
         scratch_shapes=scratch,
         compiler_params=pltpu.CompilerParams(vmem_limit_bytes=mib << 20),
         name=name,
@@ -63,6 +64,12 @@
     for kind in range(kinds):
         for block in range(columns):
             out_ref[kind, block] = interpolation(fraction_ref[0, kind, block], edge).astype(BF16)
+
+
+def stage_body(source_ref, out_ref, sem):
+    copy = pltpu.make_async_copy(source_ref, out_ref, sem)
+    copy.start()
+    copy.wait()
 
 
 def choose_body(below_ref, above_ref, source_ref, for_below_ref, for_above_ref):
@@ -175,7 +182,7 @@
     out_ref[...] = jnp.where(inside, total, 0.0).astype(BF16).reshape(out_ref.shape)
 
 
-def rim_body(place_ref, first_ref, second_ref, put_ref, left_ref, right_ref, passed_ref, aligned_ref, inner_ref, out_ref, volume_ref, pass_ref):
+def rim_body(place_ref, first_ref, second_ref, put_ref, left_ref, right_ref, passed_ref, aligned_ref, inner_ref, out_ref, volume_ref, pass_ref, done_ref, sems):
     lanes = LANES
     sections = inner_ref.shape[0]
     rim, length = aligned_ref.shape
@@ -197,9 +204,17 @@
         pass_ref[start + inner : start + inner + rows] = passed
     second = shifted_sum(second_ref, pass_ref[...], rim)
     total = (second + aligned_ref[...].astype(F32))[:, lanes : length - lanes].astype(BF16)
-    placed = dot(put_ref[...], total)
-    inner_out = inner_ref[...].reshape(placed.shape).astype(F32)
-    out_ref[...] = (placed + inner_out).astype(BF16).reshape(out_ref.shape)
+    pieces = sems.shape[0]
+    width = total.shape[1] // pieces
+    copies = []
+    for piece in range(pieces):
+        where = slice(piece * width, (piece + 1) * width)
+        placed = dot(put_ref[...], total[:, where]).astype(BF16).reshape(sections, -1, width)
+        done_ref[:, :, where] = placed + inner_ref[:, :, where]
+        copies.append(pltpu.make_async_copy(done_ref.at[:, :, where], out_ref.at[:, :, where], sems.at[piece]))
+        copies[-1].start()
+    for copy in copies:
+        copy.wait()
 
 
 def one_hot(out_pixels, in_pixels):
@@ -215,9 +230,11 @@
     chunks = edge // LANES
 
     of_below, of_above = from_behind(coarse, "xy", -1), from_behind(coarse, "xy", 1)
+    staged = call(stage_body, shaped(*source.shape), [ANY], "stage", 8, [pltpu.SemaphoreType.DMA])(source)
+    of_below, of_above, staged = lax.optimization_barrier((of_below, of_above, staged))
     for_below, for_above = call(
         choose_body, (shaped(1, edge, edge),) * 2, [SMEM, SMEM, VMEM], "choose", 8
-    )(of_below, of_above, source)
+    )(of_below, of_above, staged)
     above, below = from_behind(for_below, "xy", 1), from_behind(for_above, "xy", -1)
 
     matrix = call(matrices_body, shaped(2, columns, edge, edge), [SMEM], "matrices", 16)(fraction)
@@ -255,7 +272,7 @@
     above, below, matrix, stencils, place = lax.optimization_barrier((above, below, matrix, stencils, place))
 
     strip = call(warp_body, shaped(n_xy, chunks, cols, LANES), [SMEM] + [VMEM] * 4, "warp", 16)(
-        coarse, source, above, below, matrix
+        coarse, staged, above, below, matrix
     )
     mine = lax.all_to_all(strip, "xy", split_axis=0, concat_axis=0, tiled=True)
     per_sec = n_xy * chunks // n_sec
@@ -283,7 +300,13 @@
         [SMEM] + [VMEM] * 8,
         "rim",
         32,
-        [pltpu.VMEM((2 * len(rim_in), length), BF16), pltpu.VMEM((2 * (len(near) + len(rim_pass)), length), BF16)],
+        [
+            pltpu.VMEM((2 * len(rim_in), length), BF16),
+            pltpu.VMEM((2 * (len(near) + len(rim_pass)), length), BF16),
+            pltpu.VMEM(out.shape, BF16),
+            pltpu.SemaphoreType.DMA((4,)),
+        ],
+        ANY,
     )(place, stencils[2], stencils[3], one_hot(natural, rim), left, right, passed, aligned, inner)
 
 

time: 137 us -> 135 us (0.985)
  no operation moved by 1% of the time
where the time goes in v5:
time: 135 us
  blocking collectives  79.7 us (59%)
  starting transfers between devices  29.5 us (22%)
  waiting for transfers between devices  12.2 us (9%)
  Pallas kernels  11.5 us (9%)
  local copies, waits for them, and re-layouts  1.44 us (1%)
    all_to_all x1, blocking collectives, body(): mine = lax.all_to_all(strip, 'xy', split_axis=0, concat_axis=0, tiled=True)  58.8 us
    ppermute x6, starting transfers between devices, from_behind(): return lax.ppermute(value, axis, shift_pairs(lax.axis_size(axis), steps))  29.5 us
    all_to_all x1, blocking collectives, body(): lax.all_to_all(spread, 'sec', split_axis=0, concat_axis=0, tiled=True)  20.9 us
    ppermute x6, waiting for transfers between devices, from_behind(): return lax.ppermute(value, axis, shift_pairs(lax.axis_size(axis), steps))  12.2 us
    pallas_call x1, Pallas kernels, body(): call(interior_body, (out, shaped(len(near), length), shaped(len(rim), len...  3.49 us
    pallas_call x1, Pallas kernels, body(): call(rim_body, out, [SMEM] + [VMEM] * 8, 'rim', 32, [pltpu.VMEM((2 * len(...  2.83 us
  transfers between devices with their start and end apart: 6, of which 4 were waited for; matrix products, arithmetic and copies ran while one was open for 0% of the time, Pallas kernels for 4%

profile of v5, /device:TPU:24, one launch (start us, length us, event | category | flops | bytes accessed | tf_op | source)
XLA Modules:
  0.0 134.8 jit_solution(2090171648459794416)
XLA Ops:
  0.0 11.6 %collective-permute-start = (s32[1,2,2]{2,1,0:T(2,128)}, s32[1,2,2]{2,1,0:T(2,128)S(1)}, u32[]{:S(2)}, u32[]{:S(2)}) collective-permute-start(s32[1,2,2]{2,1,0:T(2,128)} %coarse_ref.1), channel_id=1, source_target_pairs={{1,0},{2,1},{3,2},{4,3},{5,4},{6,5},{7,6},{8,7},{9,8},{10,9},{11,1... | collective-permute-start | bytes 56 | tf_op jit(solution)/shard_map/ppermute | solution.py:44
  11.6 1.9 %collective-permute-start.1 = (s32[1,2,2]{2,1,0:T(2,128)}, s32[1,2,2]{2,1,0:T(2,128)S(1)}, u32[]{:S(2)}, u32[]{:S(2)}) collective-permute-start(s32[1,2,2]{2,1,0:T(2,128)} %coarse_ref.1), channel_id=1, source_target_pairs={{0,1},{1,2},{2,3},{3,4},{4,5},{5,6},{6,7},{7,8},{8,9},{9,10},{10,1... | collective-permute-start | bytes 56 | tf_op jit(solution)/shard_map/ppermute | solution.py:44
  13.5 0.0 copy-start
  13.5 1.2 copy-done
  14.7 0.0 copy-start.10
  14.7 0.1 stage.1.source_ref
  14.8 0.0 collective-permute-done.below_ref
  14.8 4.5 %collective-permute-done.1.above_ref = s32[1,2,2]{2,1,0:T(2,128)S(1)} collective-permute-done((s32[1,2,2]{2,1,0:T(2,128)}, s32[1,2,2]{2,1,0:T(2,128)S(1)}, u32[]{:S(2)}, u32[]{:S(2)}) %collective-permute-start.1) | collective-permute-done | bytes 48 | tf_op jit(solution)/shard_map/ppermute | solution.py:44
  19.4 0.6 choose.1
  20.0 0.0 copy-start.1
  20.0 0.0 copy-start.2
  20.0 0.0 copy-start.4
  20.1 0.0 copy-start.5
  20.1 0.0 copy-start.8
  20.1 0.0 copy-start.9
  20.1 2.1 %collective-permute-start.2 = (bf16[1,512,512]{2,1,0:T(8,128)(2,1)S(1)}, bf16[1,512,512]{2,1,0:T(8,128)(2,1)S(1)}, u32[]{:S(2)}, u32[]{:S(2)}) collective-permute-start(bf16[1,512,512]{2,1,0:T(8,128)(2,1)S(1)} %get-tuple-element.30), channel_id=1, source_target_pairs={{0,1},{1,2},{2,3},{3,4},{4,5},{5,6},{6,7},{7,8},{8,9},{9,10},{10,1... | collective-permute-start | bytes 1572872 | tf_op jit(solution)/shard_map/ppermute | solution.py:44
  22.2 6.0 %collective-permute-start.3 = (bf16[1,512,512]{2,1,0:T(8,128)(2,1)S(1)}, bf16[1,512,512]{2,1,0:T(8,128)(2,1)S(1)}, u32[]{:S(2)}, u32[]{:S(2)}) collective-permute-start(bf16[1,512,512]{2,1,0:T(8,128)(2,1)S(1)} %get-tuple-element.31), channel_id=1, source_target_pairs={{1,0},{2,1},{3,2},{4,3},{5,4},{6,5},{7,6},{8,7},{9,8},{10,9},{11,1... | collective-permute-start | bytes 1572872 | tf_op jit(solution)/shard_map/ppermute | solution.py:44
  28.2 0.0 copy-done.10
  28.2 0.0 copy-start.11
  28.2 1.0 matrices.1.matrix_ref
  29.2 0.0 copy-done.1
  29.2 0.0 copy-done.2
  29.2 0.0 copy-done.4
  29.2 0.0 copy-done.5
  29.3 0.0 copy-done.8
  29.3 0.0 copy-done.9
  29.3 1.1 stencils.1
  30.4 0.1 add_convert_fusion.place_ref
  30.4 6.0 %collective-permute-done.2.above_ref = bf16[1,512,512]{2,1,0:T(8,128)(2,1)S(1)} collective-permute-done((bf16[1,512,512]{2,1,0:T(8,128)(2,1)S(1)}, bf16[1,512,512]{2,1,0:T(8,128)(2,1)S(1)}, u32[]{:S(2)}, u32[]{:S(2)}) %collective-permute-start.2) | collective-permute-done | bytes 524320 | tf_op jit(solution)/shard_map/ppermute | solution.py:44
  36.5 1.2 collective-permute-done.3.below_ref
  37.6 0.0 copy-done.11
  37.7 2.0 %warp.1 = bf16[64,4,16,128]{3,2,1,0:T(8,128)(2,1)S(1)} custom-call(s32[1,2,2]{2,1,0:T(2,128)S(1)} %copy-done.11, bf16[1,512,1024]{2,1,0:T(8,128)(2,1)S(1)} %stage.1.source_ref, bf16[1,512,512]{2,1,0:T(8,128)(2,1)S(1)} %collective-permute-done.2.above_ref, bf16[1,512,512]{2,1,0:T(8,128)(2,1)S(1)} %collective-permute-done.3.below_ref, ...), custom_call_target="tpu_custom_call" | custom-call | tf_op jit(solution)/shard_map/warp/pallas_call | solution.py:274
  39.7 58.8 %all_to_all.10 = bf16[64,4,16,128]{3,2,1,0:T(8,128)(2,1)S(1)} all-to-all(bf16[64,4,16,128]{3,2,1,0:T(8,128)(2,1)S(1)} %warp.1), channel_id=1, replica_groups=mesh['sec'=8,'xy'=64] {'xy'}, dimensions={0} | all-to-all | bytes 2097152 | tf_op jit(solution)/shard_map/all_to_all | solution.py:277
  98.7 0.0 copy-start.7
  98.7 20.9 %all_to_all.11.data_ref = bf16[8,34,16,128]{3,2,1,0:T(8,128)(2,1)S(1)} all-to-all(bf16[8,34,16,128]{3,2,1,0:T(8,128)(2,1)S(1)} %fusion.3), channel_id=1, replica_groups=mesh['sec'=8,'xy'=64] {'sec'}, dimensions={0} | all-to-all | bytes 2228224 | tf_op jit(solution)/shard_map/all_to_all | solution.py:281
  119.6 0.0 copy-done.7
  119.6 0.0 copy-start.6
  119.6 0.0 copy-start.3
  119.6 0.4 edges.1
  120.0 5.0 %collective-permute-start.4 = (bf16[16,4352]{1,0:T(8,128)(2,1)S(1)}, bf16[16,4352]{1,0:T(8,128)(2,1)S(1)}, u32[]{:S(2)}, u32[]{:S(2)}) collective-permute-start(bf16[16,4352]{1,0:T(8,128)(2,1)S(1)} %get-tuple-element.42), channel_id=1, source_target_pairs={{0,1},{1,2},{2,3},{3,4},{4,5},{5,6},{6,7},{7,8},{8,9},{9,10},{10,1... | collective-permute-start | bytes 417800 | tf_op jit(solution)/shard_map/ppermute | solution.py:44
  125.0 2.9 %collective-permute-start.5 = (bf16[16,4352]{1,0:T(8,128)(2,1)S(1)}, bf16[16,4352]{1,0:T(8,128)(2,1)S(1)}, u32[]{:S(2)}, u32[]{:S(2)}) collective-permute-start(bf16[16,4352]{1,0:T(8,128)(2,1)S(1)} %get-tuple-element.43), channel_id=1, source_target_pairs={{1,0},{2,1},{3,2},{4,3},{5,4},{6,5},{7,6},{8,7},{9,8},{10,9},{11,1... | collective-permute-start | bytes 417800 | tf_op jit(solution)/shard_map/ppermute | solution.py:44
  128.0 0.0 copy-done.6
  128.0 3.5 %interior.1 = (bf16[8,16,4096]{2,1,0:T(8,128)(2,1)S(1)}, bf16[32,4352]{1,0:T(8,128)(2,1)S(1)}, bf16[32,4352]{1,0:T(8,128)(2,1)S(1)}) custom-call(s32[4]{0:T(128)S(1)} %add_convert_fusion.place_ref, bf16[336,256]{1,0:T(8,128)(2,1)S(1)} %get-tuple-element.44.first_ref, bf16[384,224]{1,0:T(8,128)(2,1)S(1)} %get-tuple-element.45.second_ref, ...), custom_call_target="tpu_custom_call" | custom-call | tf_op jit(solution)/shard_map/interior/pallas_call | solution.py:289
  131.5 0.0 collective-permute-done.4.left_ref
  131.5 0.5 collective-permute-done.5.right_ref
  132.0 0.0 copy-done.3
  132.0 2.8 %rim.1 = bf16[8,16,4096]{2,1,0:T(8,128)(2,1)} custom-call(s32[4]{0:T(128)S(1)} %add_convert_fusion.place_ref, bf16[96,128]{1,0:T(8,128)(2,1)S(1)} %get-tuple-element.37.first_ref, bf16[96,128]{1,0:T(8,128)(2,1)S(1)} %get-tuple-element.38.second_ref, bf16[128,32]{1,0:T(8,128)(2,1)S(1)} %copy-done.3, bf16[16,4352]{1,0:T(8,128)(2,1)S(1)} %collective-permute-done.4.left_ref, ...), custom_call_target="tpu_custom_call" | custom-call | tf_op jit(solution)/shard_map/rim/pallas_call | solution.py:297
  (8 shorter events, 0.2 us)
Async XLA Ops:
  0.0 14.8 %collective-permute-start = (s32[1,2,2]{2,1,0:T(2,128)}, s32[1,2,2]{2,1,0:T(2,128)S(1)}, u32[]{:S(2)}, u32[]{:S(2)}) collective-permute-start(s32[1,2,2]{2,1,0:T(2,128)} %coarse_ref.1), channel_id=1, source_target_pairs={{1,0},{2,1},{3,2},{4,3},{5,4},{6,5},{7,6},{8,7},{9,8},{10,9},{11,1... | collective-permute-start | bytes 56 | tf_op jit(solution)/shard_map/ppermute | solution.py:44
  11.6 7.8 %collective-permute-start.1 = (s32[1,2,2]{2,1,0:T(2,128)}, s32[1,2,2]{2,1,0:T(2,128)S(1)}, u32[]{:S(2)}, u32[]{:S(2)}) collective-permute-start(s32[1,2,2]{2,1,0:T(2,128)} %coarse_ref.1), channel_id=1, source_target_pairs={{0,1},{1,2},{2,3},{3,4},{4,5},{5,6},{6,7},{7,8},{8,9},{9,10},{10,1... | collective-permute-start | bytes 56 | tf_op jit(solution)/shard_map/ppermute | solution.py:44
  13.5 1.2 copy-start
  14.7 13.5 %copy-start.10 = (f32[1,2,2]{2,1,0:T(2,128)S(1)}, f32[1,2,2]{2,1,0:T(2,128)}, u32[]{:S(2)}) copy-start(f32[1,2,2]{2,1,0:T(2,128)} %fraction_ref.1) | copy-start | bytes 52
  20.0 9.2 %copy-start.1 = (s32[128,112]{1,0:T(8,128)S(1)}, s32[128,112]{1,0:T(8,128)}, u32[]{:S(2)}) copy-start(s32[128,112]{1,0:T(8,128)} %constant.32.clone.refs_1_) | copy-start | bytes 172036
  20.0 9.2 %copy-start.2 = (s32[112,128]{1,0:T(8,128)S(1)}, s32[112,128]{1,0:T(8,128)}, u32[]{:S(2)}) copy-start(s32[112,128]{1,0:T(8,128)} %constant.31.clone.refs_0_) | copy-start | bytes 172036
  20.0 9.2 %copy-start.4 = (s32[32,64]{1,0:T(8,128)S(1)}, s32[32,64]{1,0:T(8,128)}, u32[]{:S(2)}) copy-start(s32[32,64]{1,0:T(8,128)} %constant.34.clone.refs_3_) | copy-start | bytes 24580
  20.1 9.2 %copy-start.5 = (s32[32,64]{1,0:T(8,128)S(1)}, s32[32,64]{1,0:T(8,128)}, u32[]{:S(2)}) copy-start(s32[32,64]{1,0:T(8,128)} %constant.33.clone.refs_2_) | copy-start | bytes 24580
  20.1 9.2 %copy-start.8 = (f32[3,3,3]{2,1,0:T(4,128)S(1)}, f32[3,3,3]{2,1,0:T(4,128)}, u32[]{:S(2)}) copy-start(f32[3,3,3]{2,1,0:T(4,128)} %one_ref.1) | copy-start | bytes 328
  20.1 9.2 %copy-start.9 = (f32[3,3,3]{2,1,0:T(4,128)S(1)}, f32[3,3,3]{2,1,0:T(4,128)}, u32[]{:S(2)}) copy-start(f32[3,3,3]{2,1,0:T(4,128)} %two_ref.1) | copy-start | bytes 328
  20.1 16.4 %collective-permute-start.2 = (bf16[1,512,512]{2,1,0:T(8,128)(2,1)S(1)}, bf16[1,512,512]{2,1,0:T(8,128)(2,1)S(1)}, u32[]{:S(2)}, u32[]{:S(2)}) collective-permute-start(bf16[1,512,512]{2,1,0:T(8,128)(2,1)S(1)} %get-tuple-element.30), channel_id=1, source_target_pairs={{0,1},{1,2},{2,3},{3,4},{4,5},{5,6},{6,7},{7,8},{8,9},{9,10},{10,1... | collective-permute-start | bytes 1572872 | tf_op jit(solution)/shard_map/ppermute | solution.py:44
  22.2 15.5 %collective-permute-start.3 = (bf16[1,512,512]{2,1,0:T(8,128)(2,1)S(1)}, bf16[1,512,512]{2,1,0:T(8,128)(2,1)S(1)}, u32[]{:S(2)}, u32[]{:S(2)}) collective-permute-start(bf16[1,512,512]{2,1,0:T(8,128)(2,1)S(1)} %get-tuple-element.31), channel_id=1, source_target_pairs={{1,0},{2,1},{3,2},{4,3},{5,4},{6,5},{7,6},{8,7},{9,8},{10,9},{11,1... | collective-permute-start | bytes 1572872 | tf_op jit(solution)/shard_map/ppermute | solution.py:44
  28.2 9.4 %copy-start.11 = (s32[1,2,2]{2,1,0:T(2,128)S(1)}, s32[1,2,2]{2,1,0:T(2,128)}, u32[]{:S(2)}) copy-start(s32[1,2,2]{2,1,0:T(2,128)} %coarse_ref.1) | copy-start | bytes 52
  98.7 20.9 %copy-start.7 = (bf16[32,128]{1,0:T(8,128)(2,1)S(1)}, bf16[32,128]{1,0:T(8,128)(2,1)}, u32[]{:S(2)}) copy-start(bf16[32,128]{1,0:T(8,128)(2,1)} %constant.35.clone.take_ref) | copy-start | bytes 24580
  119.6 8.4 %copy-start.6 = (bf16[32,128]{1,0:T(8,128)(2,1)S(1)}, bf16[32,128]{1,0:T(8,128)(2,1)}, u32[]{:S(2)}) copy-start(bf16[32,128]{1,0:T(8,128)(2,1)} %constant.36.clone.rim_ref) | copy-start | bytes 24580
  119.6 12.4 %copy-start.3 = (bf16[128,32]{1,0:T(8,128)(2,1)S(1)}, bf16[128,32]{1,0:T(8,128)(2,1)}, u32[]{:S(2)}) copy-start(bf16[128,32]{1,0:T(8,128)(2,1)} %constant.37.clone.put_ref) | copy-start | bytes 24580
  120.0 11.5 %collective-permute-start.4 = (bf16[16,4352]{1,0:T(8,128)(2,1)S(1)}, bf16[16,4352]{1,0:T(8,128)(2,1)S(1)}, u32[]{:S(2)}, u32[]{:S(2)}) collective-permute-start(bf16[16,4352]{1,0:T(8,128)(2,1)S(1)} %get-tuple-element.42), channel_id=1, source_target_pairs={{0,1},{1,2},{2,3},{3,4},{4,5},{5,6},{6,7},{7,8},{8,9},{9,10},{10,1... | collective-permute-start | bytes 417800 | tf_op jit(solution)/shard_map/ppermute | solution.py:44
  125.0 7.0 %collective-permute-start.5 = (bf16[16,4352]{1,0:T(8,128)(2,1)S(1)}, bf16[16,4352]{1,0:T(8,128)(2,1)S(1)}, u32[]{:S(2)}, u32[]{:S(2)}) collective-permute-start(bf16[16,4352]{1,0:T(8,128)(2,1)S(1)} %get-tuple-element.43), channel_id=1, source_target_pairs={{1,0},{2,1},{3,2},{4,3},{5,4},{6,5},{7,6},{8,7},{9,8},{10,9},{11,1... | collective-permute-start | bytes 417800 | tf_op jit(solution)/shard_map/ppermute | solution.py:44

commit v6 on v5

--- a/solution.py
+++ b/solution.py
@@ -147,9 +147,8 @@
 
 def shifted_sum(matrix_ref, volume, rows):
     size = volume.shape[1]
-    before = dot(matrix_ref[0:rows], volume)
-    here = dot(matrix_ref[rows : 2 * rows], volume)
-    after = dot(matrix_ref[2 * rows : 3 * rows], volume)
+    every = dot(matrix_ref[...], volume)
+    before, here, after = every[0:rows], every[rows : 2 * rows], every[2 * rows : 3 * rows]
     return pltpu.roll(before, 1, 1) + here + pltpu.roll(after, size - 1, 1)
 
 
@@ -159,7 +158,7 @@
     return gone | ((lane >= shape[1] - lanes) & (place_ref[3] > 0))
 
 
-def interior_body(place_ref, first_ref, second_ref, rim_ref, data_ref, out_ref, passed_ref, aligned_ref, volume_ref, pass_ref):
+def interior_body(place_ref, first_ref, second_ref, order_ref, data_ref, out_ref, passed_ref, aligned_ref, volume_ref, pass_ref):
     sections, chunks, cols, lanes = data_ref.shape
     main = sections * cols
     length = chunks * lanes
@@ -168,23 +167,22 @@
         volume_ref[0:main, chunk * lanes : (chunk + 1) * lanes] = block
         volume_ref[main : 2 * main, chunk * lanes : (chunk + 1) * lanes] = block
     volume = volume_ref[...]
-    aligned_ref[...] = dot(rim_ref[...], volume[0:main]).astype(BF16)
+    ordered = dot(order_ref[...], volume[0:main])
+    rim = aligned_ref.shape[0]
+    aligned_ref[...] = ordered[0:rim].astype(BF16)
     rows = first_ref.shape[0] // 3
     passed = jnp.maximum(shifted_sum(first_ref, volume, rows), 0.0)
     passed = jnp.where(outside(place_ref, passed.shape, lanes), 0.0, passed).astype(BF16)
     passed_ref[...] = passed[0 : passed_ref.shape[0]]
     pass_ref[0:rows] = passed
     pass_ref[rows : 2 * rows] = passed
-    second = shifted_sum(second_ref, pass_ref[...], main)
-    total = (second + volume_ref[0:main, :].astype(F32))[:, lanes : length - lanes]
-    column = lax.broadcasted_iota(jnp.int32, total.shape, 0) % cols
-    inside = (column >= HALO) & (column < cols - HALO)
-    out_ref[...] = jnp.where(inside, total, 0.0).astype(BF16).reshape(out_ref.shape)
+    total = shifted_sum(second_ref, pass_ref[...], main - rim) + ordered[rim:]
+    out_ref[...] = total[:, lanes : length - lanes].astype(BF16)
 
 
 def rim_body(place_ref, first_ref, second_ref, put_ref, left_ref, right_ref, passed_ref, aligned_ref, inner_ref, out_ref, volume_ref, pass_ref, done_ref, sems):
     lanes = LANES
-    sections = inner_ref.shape[0]
+    sections = out_ref.shape[0]
     rim, length = aligned_ref.shape
     side = left_ref.shape[0]
     for start in (0, rim + 2 * side):
@@ -209,8 +207,8 @@
     copies = []
     for piece in range(pieces):
         where = slice(piece * width, (piece + 1) * width)
-        placed = dot(put_ref[...], total[:, where]).astype(BF16).reshape(sections, -1, width)
-        done_ref[:, :, where] = placed + inner_ref[:, :, where]
+        rows_out = jnp.concatenate([total[:, where], inner_ref[:, where]], axis=0)
+        done_ref[:, :, where] = dot(put_ref[...], rows_out).astype(BF16).reshape(sections, -1, width)
         copies.append(pltpu.make_async_copy(done_ref.at[:, :, where], out_ref.at[:, :, where], sems.at[piece]))
         copies[-1].start()
     for copy in copies:
@@ -252,7 +250,7 @@
     inner_pass = near + pixels(*range(3, last - 2))
     rim_in = rim + pixels(-2, -1) + pixels(last + 1, last + 2)
     rim_pass = by_column(-1, 0, last, last + 1)
-    inner_out = [(s, c) if HALO <= c < cols - HALO else (-9, -9) for s, c in natural]
+    inner_out = pixels(*range(HALO, cols - HALO))
     indices = [
         tap_index(inner_pass, natural),
         tap_index(inner_out, inner_pass),
@@ -288,12 +286,12 @@
     left, right = from_behind(lasts, "xy", 1), from_behind(firsts, "xy", -1)
     inner, passed, aligned = call(
         interior_body,
-        (out, shaped(len(near), length), shaped(len(rim), length)),
+        (shaped(len(inner_out), per_sec * LANES), shaped(len(near), length), shaped(len(rim), length)),
         [SMEM] + [VMEM] * 4,
         "interior",
         32,
         [pltpu.VMEM((2 * len(natural), length), BF16), pltpu.VMEM((2 * len(inner_pass), length), BF16)],
-    )(place, stencils[0], stencils[1], one_hot(rim, natural), data)
+    )(place, stencils[0], stencils[1], one_hot(rim + inner_out, natural), data)
     return call(
         rim_body,
         out,
@@ -307,7 +305,7 @@
             pltpu.SemaphoreType.DMA((4,)),
         ],
         ANY,
-    )(place, stencils[2], stencils[3], one_hot(natural, rim), left, right, passed, aligned, inner)
+    )(place, stencils[2], stencils[3], one_hot(natural, rim + inner_out), left, right, passed, aligned, inner)
 
 
 def solution(mesh):

time: 135 us -> 135 us (level)
  no operation moved by 1% of the time
where the time goes in v6:
time: 135 us; the launch traced here: 134 us
  blocking collectives  79.7 us (59%)
  starting transfers between devices  29.5 us (22%)
  waiting for transfers between devices  12.5 us (9%)
  Pallas kernels  10.9 us (8%)
  local copies, waits for them, and re-layouts  1.44 us (1%)
    all_to_all x1, blocking collectives, body(): mine = lax.all_to_all(strip, 'xy', split_axis=0, concat_axis=0, tiled=True)  58.8 us
    ppermute x6, starting transfers between devices, from_behind(): return lax.ppermute(value, axis, shift_pairs(lax.axis_size(axis), steps))  29.5 us
    all_to_all x1, blocking collectives, body(): lax.all_to_all(spread, 'sec', split_axis=0, concat_axis=0, tiled=True)  20.9 us
    ppermute x6, waiting for transfers between devices, from_behind(): return lax.ppermute(value, axis, shift_pairs(lax.axis_size(axis), steps))  12.5 us
    pallas_call x1, Pallas kernels, body(): call(interior_body, (shaped(len(inner_out), per_sec * LANES), shaped(len(...  3.25 us
  transfers between devices with their start and end apart: 6, of which 4 were waited for; matrix products, arithmetic and copies ran while one was open for 0% of the time, Pallas kernels for 4%

profile of v6, /device:TPU:24, one launch (start us, length us, event | category | flops | bytes accessed | tf_op | source)
XLA Modules:
  0.0 134.5 jit_solution(2270132232447088170)
XLA Ops:
  0.0 11.6 %collective-permute-start = (s32[1,2,2]{2,1,0:T(2,128)}, s32[1,2,2]{2,1,0:T(2,128)S(1)}, u32[]{:S(2)}, u32[]{:S(2)}) collective-permute-start(s32[1,2,2]{2,1,0:T(2,128)} %coarse_ref.1), channel_id=1, source_target_pairs={{1,0},{2,1},{3,2},{4,3},{5,4},{6,5},{7,6},{8,7},{9,8},{10,9},{11,1... | collective-permute-start | bytes 56 | tf_op jit(solution)/shard_map/ppermute | solution.py:44
  11.6 1.9 %collective-permute-start.1 = (s32[1,2,2]{2,1,0:T(2,128)}, s32[1,2,2]{2,1,0:T(2,128)S(1)}, u32[]{:S(2)}, u32[]{:S(2)}) collective-permute-start(s32[1,2,2]{2,1,0:T(2,128)} %coarse_ref.1), channel_id=1, source_target_pairs={{0,1},{1,2},{2,3},{3,4},{4,5},{5,6},{6,7},{7,8},{8,9},{9,10},{10,1... | collective-permute-start | bytes 56 | tf_op jit(solution)/shard_map/ppermute | solution.py:44
  13.5 0.0 copy-start
  13.5 1.2 copy-done
  14.7 0.0 copy-start.10
  14.7 0.1 stage.1.source_ref
  14.8 0.0 collective-permute-done.below_ref
  14.8 4.5 %collective-permute-done.1.above_ref = s32[1,2,2]{2,1,0:T(2,128)S(1)} collective-permute-done((s32[1,2,2]{2,1,0:T(2,128)}, s32[1,2,2]{2,1,0:T(2,128)S(1)}, u32[]{:S(2)}, u32[]{:S(2)}) %collective-permute-start.1) | collective-permute-done | bytes 48 | tf_op jit(solution)/shard_map/ppermute | solution.py:44
  19.4 0.6 choose.1
  20.0 0.0 copy-start.1
  20.0 0.0 copy-start.2
  20.0 0.0 copy-start.5
  20.1 0.0 copy-start.6
  20.1 0.0 copy-start.8
  20.1 0.0 copy-start.9
  20.1 2.1 %collective-permute-start.2 = (bf16[1,512,512]{2,1,0:T(8,128)(2,1)S(1)}, bf16[1,512,512]{2,1,0:T(8,128)(2,1)S(1)}, u32[]{:S(2)}, u32[]{:S(2)}) collective-permute-start(bf16[1,512,512]{2,1,0:T(8,128)(2,1)S(1)} %get-tuple-element.30), channel_id=1, source_target_pairs={{0,1},{1,2},{2,3},{3,4},{4,5},{5,6},{6,7},{7,8},{8,9},{9,10},{10,1... | collective-permute-start | bytes 1572872 | tf_op jit(solution)/shard_map/ppermute | solution.py:44
  22.2 6.0 %collective-permute-start.3 = (bf16[1,512,512]{2,1,0:T(8,128)(2,1)S(1)}, bf16[1,512,512]{2,1,0:T(8,128)(2,1)S(1)}, u32[]{:S(2)}, u32[]{:S(2)}) collective-permute-start(bf16[1,512,512]{2,1,0:T(8,128)(2,1)S(1)} %get-tuple-element.31), channel_id=1, source_target_pairs={{1,0},{2,1},{3,2},{4,3},{5,4},{6,5},{7,6},{8,7},{9,8},{10,9},{11,1... | collective-permute-start | bytes 1572872 | tf_op jit(solution)/shard_map/ppermute | solution.py:44
  28.2 0.0 copy-done.10
  28.2 0.0 copy-start.11
  28.2 1.0 matrices.1.matrix_ref
  29.2 0.0 copy-done.1
  29.2 0.0 copy-done.2
  29.2 0.0 copy-done.5
  29.2 0.0 copy-done.6
  29.3 0.0 copy-done.8
  29.3 0.0 copy-done.9
  29.3 1.0 stencils.1
  30.3 0.1 add_convert_fusion.place_ref
  30.4 6.1 %collective-permute-done.2.above_ref = bf16[1,512,512]{2,1,0:T(8,128)(2,1)S(1)} collective-permute-done((bf16[1,512,512]{2,1,0:T(8,128)(2,1)S(1)}, bf16[1,512,512]{2,1,0:T(8,128)(2,1)S(1)}, u32[]{:S(2)}, u32[]{:S(2)}) %collective-permute-start.2) | collective-permute-done | bytes 524320 | tf_op jit(solution)/shard_map/ppermute | solution.py:44
  36.5 1.2 collective-permute-done.3.below_ref
  37.6 0.0 copy-done.11
  37.7 2.0 %warp.1 = bf16[64,4,16,128]{3,2,1,0:T(8,128)(2,1)S(1)} custom-call(s32[1,2,2]{2,1,0:T(2,128)S(1)} %copy-done.11, bf16[1,512,1024]{2,1,0:T(8,128)(2,1)S(1)} %stage.1.source_ref, bf16[1,512,512]{2,1,0:T(8,128)(2,1)S(1)} %collective-permute-done.2.above_ref, bf16[1,512,512]{2,1,0:T(8,128)(2,1)S(1)} %collective-permute-done.3.below_ref, ...), custom_call_target="tpu_custom_call" | custom-call | tf_op jit(solution)/shard_map/warp/pallas_call | solution.py:272
  39.7 58.8 %all_to_all.10 = bf16[64,4,16,128]{3,2,1,0:T(8,128)(2,1)S(1)} all-to-all(bf16[64,4,16,128]{3,2,1,0:T(8,128)(2,1)S(1)} %warp.1), channel_id=1, replica_groups=mesh['sec'=8,'xy'=64] {'xy'}, dimensions={0} | all-to-all | bytes 2097152 | tf_op jit(solution)/shard_map/all_to_all | solution.py:275
  98.7 0.0 copy-start.7
  98.7 20.9 %all_to_all.11.data_ref = bf16[8,34,16,128]{3,2,1,0:T(8,128)(2,1)S(1)} all-to-all(bf16[8,34,16,128]{3,2,1,0:T(8,128)(2,1)S(1)} %fusion.3), channel_id=1, replica_groups=mesh['sec'=8,'xy'=64] {'sec'}, dimensions={0} | all-to-all | bytes 2228224 | tf_op jit(solution)/shard_map/all_to_all | solution.py:279
  119.6 0.0 copy-done.7
  119.6 0.0 copy-start.4
  119.6 0.0 copy-start.3
  119.6 0.4 edges.1
  120.0 5.0 %collective-permute-start.4 = (bf16[16,4352]{1,0:T(8,128)(2,1)S(1)}, bf16[16,4352]{1,0:T(8,128)(2,1)S(1)}, u32[]{:S(2)}, u32[]{:S(2)}) collective-permute-start(bf16[16,4352]{1,0:T(8,128)(2,1)S(1)} %get-tuple-element.42), channel_id=1, source_target_pairs={{0,1},{1,2},{2,3},{3,4},{4,5},{5,6},{6,7},{7,8},{8,9},{9,10},{10,1... | collective-permute-start | bytes 417800 | tf_op jit(solution)/shard_map/ppermute | solution.py:44
  125.0 2.9 %collective-permute-start.5 = (bf16[16,4352]{1,0:T(8,128)(2,1)S(1)}, bf16[16,4352]{1,0:T(8,128)(2,1)S(1)}, u32[]{:S(2)}, u32[]{:S(2)}) collective-permute-start(bf16[16,4352]{1,0:T(8,128)(2,1)S(1)} %get-tuple-element.43), channel_id=1, source_target_pairs={{1,0},{2,1},{3,2},{4,3},{5,4},{6,5},{7,6},{8,7},{9,8},{10,9},{11,1... | collective-permute-start | bytes 417800 | tf_op jit(solution)/shard_map/ppermute | solution.py:44
  128.0 0.0 copy-done.4
  128.0 3.3 %interior.1 = (bf16[96,4096]{1,0:T(8,128)(2,1)S(1)}, bf16[32,4352]{1,0:T(8,128)(2,1)S(1)}, bf16[32,4352]{1,0:T(8,128)(2,1)S(1)}) custom-call(s32[4]{0:T(128)S(1)} %add_convert_fusion.place_ref, bf16[336,256]{1,0:T(8,128)(2,1)S(1)} %get-tuple-element.44.first_ref, bf16[288,224]{1,0:T(8,128)(2,1)S(1)} %get-tuple-element.45.second_ref, ...), custom_call_target="tpu_custom_call" | custom-call | tf_op jit(solution)/shard_map/interior/pallas_call | solution.py:287
  131.2 0.0 collective-permute-done.4.left_ref
  131.3 0.7 collective-permute-done.5.right_ref
  132.0 0.0 copy-done.3
  132.0 2.5 %rim.1 = bf16[8,16,4096]{2,1,0:T(8,128)(2,1)} custom-call(s32[4]{0:T(128)S(1)} %add_convert_fusion.place_ref, bf16[96,128]{1,0:T(8,128)(2,1)S(1)} %get-tuple-element.37.first_ref, bf16[96,128]{1,0:T(8,128)(2,1)S(1)} %get-tuple-element.38.second_ref, bf16[128,128]{1,0:T(8,128)(2,1)S(1)} %copy-done.3, bf16[16,4352]{1,0:T(8,128)(2,1)S(1)} %collective-permute-done.4.left_ref, ...), custom_call_target="tpu_custom_call" | custom-call | tf_op jit(solution)/shard_map/rim/pallas_call | solution.py:295
  (8 shorter events, 0.2 us)
Async XLA Ops:
  0.0 14.8 %collective-permute-start = (s32[1,2,2]{2,1,0:T(2,128)}, s32[1,2,2]{2,1,0:T(2,128)S(1)}, u32[]{:S(2)}, u32[]{:S(2)}) collective-permute-start(s32[1,2,2]{2,1,0:T(2,128)} %coarse_ref.1), channel_id=1, source_target_pairs={{1,0},{2,1},{3,2},{4,3},{5,4},{6,5},{7,6},{8,7},{9,8},{10,9},{11,1... | collective-permute-start | bytes 56 | tf_op jit(solution)/shard_map/ppermute | solution.py:44
  11.6 7.8 %collective-permute-start.1 = (s32[1,2,2]{2,1,0:T(2,128)}, s32[1,2,2]{2,1,0:T(2,128)S(1)}, u32[]{:S(2)}, u32[]{:S(2)}) collective-permute-start(s32[1,2,2]{2,1,0:T(2,128)} %coarse_ref.1), channel_id=1, source_target_pairs={{0,1},{1,2},{2,3},{3,4},{4,5},{5,6},{6,7},{7,8},{8,9},{9,10},{10,1... | collective-permute-start | bytes 56 | tf_op jit(solution)/shard_map/ppermute | solution.py:44
  13.5 1.2 copy-start
  14.7 13.5 %copy-start.10 = (f32[1,2,2]{2,1,0:T(2,128)S(1)}, f32[1,2,2]{2,1,0:T(2,128)}, u32[]{:S(2)}) copy-start(f32[1,2,2]{2,1,0:T(2,128)} %fraction_ref.1) | copy-start | bytes 52
  20.0 9.2 %copy-start.1 = (s32[112,128]{1,0:T(8,128)S(1)}, s32[112,128]{1,0:T(8,128)}, u32[]{:S(2)}) copy-start(s32[112,128]{1,0:T(8,128)} %constant.31.clone.refs_0_) | copy-start | bytes 172036
  20.0 9.2 %copy-start.2 = (s32[96,112]{1,0:T(8,128)S(1)}, s32[96,112]{1,0:T(8,128)}, u32[]{:S(2)}) copy-start(s32[96,112]{1,0:T(8,128)} %constant.32.clone.refs_1_) | copy-start | bytes 129028
  20.0 9.2 %copy-start.5 = (s32[32,64]{1,0:T(8,128)S(1)}, s32[32,64]{1,0:T(8,128)}, u32[]{:S(2)}) copy-start(s32[32,64]{1,0:T(8,128)} %constant.34.clone.refs_3_) | copy-start | bytes 24580
  20.1 9.2 %copy-start.6 = (s32[32,64]{1,0:T(8,128)S(1)}, s32[32,64]{1,0:T(8,128)}, u32[]{:S(2)}) copy-start(s32[32,64]{1,0:T(8,128)} %constant.33.clone.refs_2_) | copy-start | bytes 24580
  20.1 9.2 %copy-start.8 = (f32[3,3,3]{2,1,0:T(4,128)S(1)}, f32[3,3,3]{2,1,0:T(4,128)}, u32[]{:S(2)}) copy-start(f32[3,3,3]{2,1,0:T(4,128)} %one_ref.1) | copy-start | bytes 328
  20.1 9.2 %copy-start.9 = (f32[3,3,3]{2,1,0:T(4,128)S(1)}, f32[3,3,3]{2,1,0:T(4,128)}, u32[]{:S(2)}) copy-start(f32[3,3,3]{2,1,0:T(4,128)} %two_ref.1) | copy-start | bytes 328
  20.1 16.4 %collective-permute-start.2 = (bf16[1,512,512]{2,1,0:T(8,128)(2,1)S(1)}, bf16[1,512,512]{2,1,0:T(8,128)(2,1)S(1)}, u32[]{:S(2)}, u32[]{:S(2)}) collective-permute-start(bf16[1,512,512]{2,1,0:T(8,128)(2,1)S(1)} %get-tuple-element.30), channel_id=1, source_target_pairs={{0,1},{1,2},{2,3},{3,4},{4,5},{5,6},{6,7},{7,8},{8,9},{9,10},{10,1... | collective-permute-start | bytes 1572872 | tf_op jit(solution)/shard_map/ppermute | solution.py:44
  22.2 15.5 %collective-permute-start.3 = (bf16[1,512,512]{2,1,0:T(8,128)(2,1)S(1)}, bf16[1,512,512]{2,1,0:T(8,128)(2,1)S(1)}, u32[]{:S(2)}, u32[]{:S(2)}) collective-permute-start(bf16[1,512,512]{2,1,0:T(8,128)(2,1)S(1)} %get-tuple-element.31), channel_id=1, source_target_pairs={{1,0},{2,1},{3,2},{4,3},{5,4},{6,5},{7,6},{8,7},{9,8},{10,9},{11,1... | collective-permute-start | bytes 1572872 | tf_op jit(solution)/shard_map/ppermute | solution.py:44
  28.2 9.4 %copy-start.11 = (s32[1,2,2]{2,1,0:T(2,128)S(1)}, s32[1,2,2]{2,1,0:T(2,128)}, u32[]{:S(2)}) copy-start(s32[1,2,2]{2,1,0:T(2,128)} %coarse_ref.1) | copy-start | bytes 52
  98.7 20.9 %copy-start.7 = (bf16[32,128]{1,0:T(8,128)(2,1)S(1)}, bf16[32,128]{1,0:T(8,128)(2,1)}, u32[]{:S(2)}) copy-start(bf16[32,128]{1,0:T(8,128)(2,1)} %constant.35.clone.take_ref) | copy-start | bytes 24580
  119.6 8.4 %copy-start.4 = (bf16[128,128]{1,0:T(8,128)(2,1)S(1)}, bf16[128,128]{1,0:T(8,128)(2,1)}, u32[]{:S(2)}) copy-start(bf16[128,128]{1,0:T(8,128)(2,1)} %constant.36.clone.order_ref) | copy-start | bytes 98308
  119.6 12.4 %copy-start.3 = (bf16[128,128]{1,0:T(8,128)(2,1)S(1)}, bf16[128,128]{1,0:T(8,128)(2,1)}, u32[]{:S(2)}) copy-start(bf16[128,128]{1,0:T(8,128)(2,1)} %constant.37.clone.put_ref) | copy-start | bytes 98308
  120.0 11.2 %collective-permute-start.4 = (bf16[16,4352]{1,0:T(8,128)(2,1)S(1)}, bf16[16,4352]{1,0:T(8,128)(2,1)S(1)}, u32[]{:S(2)}, u32[]{:S(2)}) collective-permute-start(bf16[16,4352]{1,0:T(8,128)(2,1)S(1)} %get-tuple-element.42), channel_id=1, source_target_pairs={{0,1},{1,2},{2,3},{3,4},{4,5},{5,6},{6,7},{7,8},{8,9},{9,10},{10,1... | collective-permute-start | bytes 417800 | tf_op jit(solution)/shard_map/ppermute | solution.py:44
  125.0 7.0 %collective-permute-start.5 = (bf16[16,4352]{1,0:T(8,128)(2,1)S(1)}, bf16[16,4352]{1,0:T(8,128)(2,1)S(1)}, u32[]{:S(2)}, u32[]{:S(2)}) collective-permute-start(bf16[16,4352]{1,0:T(8,128)(2,1)S(1)} %get-tuple-element.43), channel_id=1, source_target_pairs={{1,0},{2,1},{3,2},{4,3},{5,4},{6,5},{7,6},{8,7},{9,8},{10,9},{11,1... | collective-permute-start | bytes 417800 | tf_op jit(solution)/shard_map/ppermute | solution.py:44

commit v7 on v6

--- a/solution.py
+++ b/solution.py
@@ -72,13 +72,17 @@
     copy.wait()
 
 
+def offsets(coarse_ref):
+    tile = coarse_ref[0].astype(F32)
+    return tile[0:1], tile[1:2] + lax.broadcasted_iota(jnp.int32, (1, tile.shape[1]), 1).astype(F32)
+
+
 def choose_body(below_ref, above_ref, source_ref, for_below_ref, for_above_ref):
     edge = for_below_ref.shape[-1]
     columns = source_ref.shape[-1] // edge
     for coarse_ref, sign, out_ref in ((below_ref, -1, for_below_ref), (above_ref, 1, for_above_ref)):
-        wanted = 0
-        for block in range(columns):
-            wanted += jnp.where(coarse_ref[0, 0, block] == sign, block + coarse_ref[0, 1, block], 0)
+        down, anchor = offsets(coarse_ref)
+        wanted = jnp.sum(jnp.where(down == sign, anchor, 0.0)).astype(jnp.int32)
         for column in range(columns):
 
             @pl.when(wanted == column)
@@ -91,9 +95,11 @@
     columns = width // edge
     groups = out_ref.shape[0] // columns
     chunks, cols = out_ref.shape[1], out_ref.shape[2]
+    downs, anchors = offsets(coarse_ref)
+    lane = lax.broadcasted_iota(jnp.int32, downs.shape, 1)
     for block in range(columns):
-        down = coarse_ref[0, 0, block]
-        anchor = block + coarse_ref[0, 1, block]
+        down = jnp.sum(jnp.where(lane == block, downs, 0.0)).astype(jnp.int32)
+        anchor = jnp.sum(jnp.where(lane == block, anchors, 0.0)).astype(jnp.int32)
         picked = source_ref[0, :, 0:edge]
         for column in range(1, columns):
             picked = jnp.where(anchor == column, source_ref[0, :, column * edge : (column + 1) * edge], picked)
@@ -152,13 +158,12 @@
     return pltpu.roll(before, 1, 1) + here + pltpu.roll(after, size - 1, 1)
 
 
-def outside(place_ref, shape, lanes):
-    lane = lax.broadcasted_iota(jnp.int32, shape, 1)
-    gone = (lane < lanes) & (place_ref[2] > 0)
-    return gone | ((lane >= shape[1] - lanes) & (place_ref[3] > 0))
-
-
-def interior_body(place_ref, first_ref, second_ref, order_ref, data_ref, out_ref, passed_ref, aligned_ref, volume_ref, pass_ref):
+def inside(keep_ref, which, values):
+    keep = jnp.broadcast_to(keep_ref[which : which + 1], values.shape)
+    return jnp.where(keep > 0.0, values, 0.0)
+
+
+def interior_body(keep_ref, first_ref, second_ref, order_ref, data_ref, out_ref, passed_ref, aligned_ref, volume_ref, pass_ref):
     sections, chunks, cols, lanes = data_ref.shape
     main = sections * cols
     length = chunks * lanes
@@ -172,7 +177,7 @@
     aligned_ref[...] = ordered[0:rim].astype(BF16)
     rows = first_ref.shape[0] // 3
     passed = jnp.maximum(shifted_sum(first_ref, volume, rows), 0.0)
-    passed = jnp.where(outside(place_ref, passed.shape, lanes), 0.0, passed).astype(BF16)
+    passed = inside(keep_ref, 0, passed).astype(BF16)
     passed_ref[...] = passed[0 : passed_ref.shape[0]]
     pass_ref[0:rows] = passed
     pass_ref[rows : 2 * rows] = passed
@@ -180,7 +185,7 @@
     out_ref[...] = total[:, lanes : length - lanes].astype(BF16)
 
 
-def rim_body(place_ref, first_ref, second_ref, put_ref, left_ref, right_ref, passed_ref, aligned_ref, inner_ref, out_ref, volume_ref, pass_ref, done_ref, sems):
+def rim_body(keep_ref, first_ref, second_ref, put_ref, left_ref, right_ref, passed_ref, aligned_ref, inner_ref, out_ref, volume_ref, pass_ref, done_ref, sems):
     lanes = LANES
     sections = out_ref.shape[0]
     rim, length = aligned_ref.shape
@@ -191,11 +196,12 @@
         volume_ref[start + rim + side : start + rim + 2 * side] = right_ref[...]
     rows = first_ref.shape[0] // 3
     passed = jnp.maximum(shifted_sum(first_ref, volume_ref[...], rows), 0.0)
-    row = lax.broadcasted_iota(jnp.int32, passed.shape, 0)
-    gone = outside(place_ref, passed.shape, lanes)
-    gone = gone | ((row < sections) & (place_ref[0] > 0))
-    gone = gone | ((row >= rows - sections) & (place_ref[1] > 0))
-    passed = jnp.where(gone, 0.0, passed).astype(BF16)
+    passed = [
+        inside(keep_ref, 1, passed[0:sections]),
+        inside(keep_ref, 0, passed[sections : rows - sections]),
+        inside(keep_ref, 2, passed[rows - sections :]),
+    ]
+    passed = jnp.concatenate(passed, axis=0).astype(BF16)
     inner = passed_ref.shape[0]
     for start in (0, inner + rows):
         pass_ref[start : start + inner] = passed_ref[...]
@@ -231,8 +237,11 @@
     staged = call(stage_body, shaped(*source.shape), [ANY], "stage", 8, [pltpu.SemaphoreType.DMA])(source)
     of_below, of_above, staged = lax.optimization_barrier((of_below, of_above, staged))
     for_below, for_above = call(
-        choose_body, (shaped(1, edge, edge),) * 2, [SMEM, SMEM, VMEM], "choose", 8
+        choose_body, (shaped(1, edge, edge),) * 2, [VMEM] * 3, "choose", 8
     )(of_below, of_above, staged)
+    for_below, for_above, fraction, kernel_one, kernel_two = lax.optimization_barrier(
+        (for_below, for_above, fraction, kernel_one, kernel_two)
+    )
     above, below = from_behind(for_below, "xy", 1), from_behind(for_above, "xy", -1)
 
     matrix = call(matrices_body, shaped(2, columns, edge, edge), [SMEM], "matrices", 16)(fraction)
@@ -266,19 +275,21 @@
     )(kernel_one, kernel_two, *map(jnp.asarray, indices))
 
     at_xy, at_sec = lax.axis_index("xy"), lax.axis_index("sec")
-    place = jnp.stack([at_xy == 0, at_xy == n_xy - 1, at_sec == 0, at_sec == n_sec - 1]).astype(jnp.int32)
-    above, below, matrix, stencils, place = lax.optimization_barrier((above, below, matrix, stencils, place))
-
-    strip = call(warp_body, shaped(n_xy, chunks, cols, LANES), [SMEM] + [VMEM] * 4, "warp", 16)(
+    per_sec = n_xy * chunks // n_sec
+    length = (per_sec + 2) * LANES
+    lane = jnp.arange(length, dtype=jnp.int32)
+    real = (lane >= jnp.where(at_sec == 0, LANES, 0)) & (lane < length - jnp.where(at_sec == n_sec - 1, LANES, 0))
+    keep = jnp.stack([real, real & (at_xy > 0), real & (at_xy < n_xy - 1)]).astype(F32)
+    above, below, matrix, stencils, keep = lax.optimization_barrier((above, below, matrix, stencils, keep))
+
+    strip = call(warp_body, shaped(n_xy, chunks, cols, LANES), [VMEM] * 5, "warp", 16)(
         coarse, staged, above, below, matrix
     )
     mine = lax.all_to_all(strip, "xy", split_axis=0, concat_axis=0, tiled=True)
-    per_sec = n_xy * chunks // n_sec
     mine = jnp.pad(mine.reshape(n_xy * chunks, cols, LANES), ((1, 1), (0, 0), (0, 0)))
     spread = jnp.stack([mine[index * per_sec : (index + 1) * per_sec + 2] for index in range(n_sec)])
     data = lax.all_to_all(spread, "sec", split_axis=0, concat_axis=0, tiled=True)
 
-    length = (per_sec + 2) * LANES
     out = shaped(n_sec, cols, per_sec * LANES)
     firsts, lasts = call(
         edges_body, (shaped(n_sec * HALO, length),) * 2, [VMEM, VMEM], "edges", 8
@@ -287,15 +298,15 @@
     inner, passed, aligned = call(
         interior_body,
         (shaped(len(inner_out), per_sec * LANES), shaped(len(near), length), shaped(len(rim), length)),
-        [SMEM] + [VMEM] * 4,
+        [VMEM] * 5,
         "interior",
         32,
         [pltpu.VMEM((2 * len(natural), length), BF16), pltpu.VMEM((2 * len(inner_pass), length), BF16)],
-    )(place, stencils[0], stencils[1], one_hot(rim + inner_out, natural), data)
+    )(keep, stencils[0], stencils[1], one_hot(rim + inner_out, natural), data)
     return call(
         rim_body,
         out,
-        [SMEM] + [VMEM] * 8,
+        [VMEM] * 9,
         "rim",
         32,
         [
@@ -305,7 +316,7 @@
             pltpu.SemaphoreType.DMA((4,)),
         ],
         ANY,
-    )(place, stencils[2], stencils[3], one_hot(natural, rim + inner_out), left, right, passed, aligned, inner)
+    )(keep, stencils[2], stencils[3], one_hot(natural, rim + inner_out), left, right, passed, aligned, inner)
 
 
 def solution(mesh):

time: 135 us -> 134 us (level)
  Pallas kernels: 10.9 us -> 9.04 us
where the time goes in v7:
time: 134 us; the launch traced here: 133 us
  blocking collectives  79.7 us (59%)
  starting transfers between devices  29.5 us (22%)
  waiting for transfers between devices  12.9 us (10%)
  Pallas kernels  9.04 us (7%)
  local copies, waits for them, and re-layouts  1.44 us (1%)
    all_to_all x1, blocking collectives, body(): mine = lax.all_to_all(strip, 'xy', split_axis=0, concat_axis=0, tiled=True)  58.8 us
    ppermute x6, starting transfers between devices, from_behind(): return lax.ppermute(value, axis, shift_pairs(lax.axis_size(axis), steps))  29.5 us
    all_to_all x1, blocking collectives, body(): lax.all_to_all(spread, 'sec', split_axis=0, concat_axis=0, tiled=True)  20.9 us
    ppermute x6, waiting for transfers between devices, from_behind(): return lax.ppermute(value, axis, shift_pairs(lax.axis_size(axis), steps))  12.9 us
    pallas_call x1, Pallas kernels, body(): call(interior_body, (shaped(len(inner_out), per_sec * LANES), shaped(len(...  2.7 us
  transfers between devices with their start and end apart: 6, of which 4 were waited for; matrix products, arithmetic and copies ran while one was open for 0% of the time, Pallas kernels for 4%

profile of v7, /device:TPU:24, one launch (start us, length us, event | category | flops | bytes accessed | tf_op | source)
XLA Modules:
  0.0 133.2 jit_solution(4277419180646146397)
XLA Ops:
  0.0 11.6 %collective-permute-start = (s32[1,2,2]{2,1,0:T(2,128)}, s32[1,2,2]{2,1,0:T(2,128)S(1)}, u32[]{:S(2)}, u32[]{:S(2)}) collective-permute-start(s32[1,2,2]{2,1,0:T(2,128)} %coarse_ref.1), channel_id=1, source_target_pairs={{1,0},{2,1},{3,2},{4,3},{5,4},{6,5},{7,6},{8,7},{9,8},{10,9},{11,1... | collective-permute-start | bytes 56 | tf_op jit(solution)/shard_map/ppermute | solution.py:44
  11.6 1.9 %collective-permute-start.1 = (s32[1,2,2]{2,1,0:T(2,128)}, s32[1,2,2]{2,1,0:T(2,128)S(1)}, u32[]{:S(2)}, u32[]{:S(2)}) collective-permute-start(s32[1,2,2]{2,1,0:T(2,128)} %coarse_ref.1), channel_id=1, source_target_pairs={{0,1},{1,2},{2,3},{3,4},{4,5},{5,6},{6,7},{7,8},{8,9},{9,10},{10,1... | collective-permute-start | bytes 56 | tf_op jit(solution)/shard_map/ppermute | solution.py:44
  13.6 0.1 compare_and_fusion
  13.6 0.0 copy-start
  13.7 1.2 copy-done
  14.9 0.1 stage.1.source_ref
  15.0 0.0 copy-start.10
  15.0 0.0 collective-permute-done.below_ref
  15.0 4.4 %collective-permute-done.1.above_ref = s32[1,2,2]{2,1,0:T(2,128)S(1)} collective-permute-done((s32[1,2,2]{2,1,0:T(2,128)}, s32[1,2,2]{2,1,0:T(2,128)S(1)}, u32[]{:S(2)}, u32[]{:S(2)}) %collective-permute-start.1) | collective-permute-done | bytes 48 | tf_op jit(solution)/shard_map/ppermute | solution.py:44
  19.4 0.3 choose.1
  19.7 0.0 copy-start.1
  19.7 0.0 copy-start.2
  19.7 0.0 copy-start.5
  19.7 0.0 copy-start.6
  19.7 0.0 copy-start.8
  19.8 0.0 copy-start.9
  19.8 2.1 %collective-permute-start.2 = (bf16[1,512,512]{2,1,0:T(8,128)(2,1)S(1)}, bf16[1,512,512]{2,1,0:T(8,128)(2,1)S(1)}, u32[]{:S(2)}, u32[]{:S(2)}) collective-permute-start(bf16[1,512,512]{2,1,0:T(8,128)(2,1)S(1)} %get-tuple-element.37), channel_id=1, source_target_pairs={{0,1},{1,2},{2,3},{3,4},{4,5},{5,6},{6,7},{7,8},{8,9},{9,10},{10,1... | collective-permute-start | bytes 1572872 | tf_op jit(solution)/shard_map/ppermute | solution.py:44
  21.8 6.0 %collective-permute-start.3 = (bf16[1,512,512]{2,1,0:T(8,128)(2,1)S(1)}, bf16[1,512,512]{2,1,0:T(8,128)(2,1)S(1)}, u32[]{:S(2)}, u32[]{:S(2)}) collective-permute-start(bf16[1,512,512]{2,1,0:T(8,128)(2,1)S(1)} %get-tuple-element.38), channel_id=1, source_target_pairs={{1,0},{2,1},{3,2},{4,3},{5,4},{6,5},{7,6},{8,7},{9,8},{10,9},{11,1... | collective-permute-start | bytes 1572872 | tf_op jit(solution)/shard_map/ppermute | solution.py:44
  27.9 0.1 add_convert_fusion.keep_ref
  27.9 0.0 copy-done.10
  28.0 0.0 copy-start.11
  28.0 1.0 matrices.1.matrix_ref
  29.0 0.0 copy-done.1
  29.0 0.0 copy-done.2
  29.0 0.0 copy-done.5
  29.0 0.0 copy-done.6
  29.0 0.0 copy-done.8
  29.0 0.0 copy-done.9
  29.0 1.0 stencils.1
  30.1 6.1 %collective-permute-done.2.above_ref = bf16[1,512,512]{2,1,0:T(8,128)(2,1)S(1)} collective-permute-done((bf16[1,512,512]{2,1,0:T(8,128)(2,1)S(1)}, bf16[1,512,512]{2,1,0:T(8,128)(2,1)S(1)}, u32[]{:S(2)}, u32[]{:S(2)}) %collective-permute-start.2) | collective-permute-done | bytes 524320 | tf_op jit(solution)/shard_map/ppermute | solution.py:44
  36.1 1.2 collective-permute-done.3.below_ref
  37.3 0.0 copy-done.11
  37.3 1.6 %warp.1 = bf16[64,4,16,128]{3,2,1,0:T(8,128)(2,1)S(1)} custom-call(s32[1,2,2]{2,1,0:T(2,128)S(1)} %copy-done.11, bf16[1,512,1024]{2,1,0:T(8,128)(2,1)S(1)} %stage.1.source_ref, bf16[1,512,512]{2,1,0:T(8,128)(2,1)S(1)} %collective-permute-done.2.above_ref, bf16[1,512,512]{2,1,0:T(8,128)(2,1)S(1)} %collective-permute-done.3.below_ref, ...), custom_call_target="tpu_custom_call" | custom-call | tf_op jit(solution)/shard_map/warp/pallas_call | solution.py:285
  38.9 58.8 %all_to_all.10 = bf16[64,4,16,128]{3,2,1,0:T(8,128)(2,1)S(1)} all-to-all(bf16[64,4,16,128]{3,2,1,0:T(8,128)(2,1)S(1)} %warp.1), channel_id=1, replica_groups=mesh['sec'=8,'xy'=64] {'xy'}, dimensions={0} | all-to-all | bytes 2097152 | tf_op jit(solution)/shard_map/all_to_all | solution.py:288
  97.9 0.0 copy-start.7
  97.9 20.9 %all_to_all.11.data_ref = bf16[8,34,16,128]{3,2,1,0:T(8,128)(2,1)S(1)} all-to-all(bf16[8,34,16,128]{3,2,1,0:T(8,128)(2,1)S(1)} %fusion.3), channel_id=1, replica_groups=mesh['sec'=8,'xy'=64] {'sec'}, dimensions={0} | all-to-all | bytes 2228224 | tf_op jit(solution)/shard_map/all_to_all | solution.py:291
  118.8 0.0 copy-done.7
  118.8 0.0 copy-start.4
  118.8 0.0 copy-start.3
  118.8 0.4 edges.1
  119.2 5.0 %collective-permute-start.4 = (bf16[16,4352]{1,0:T(8,128)(2,1)S(1)}, bf16[16,4352]{1,0:T(8,128)(2,1)S(1)}, u32[]{:S(2)}, u32[]{:S(2)}) collective-permute-start(bf16[16,4352]{1,0:T(8,128)(2,1)S(1)} %get-tuple-element.52), channel_id=1, source_target_pairs={{0,1},{1,2},{2,3},{3,4},{4,5},{5,6},{6,7},{7,8},{8,9},{9,10},{10,1... | collective-permute-start | bytes 417800 | tf_op jit(solution)/shard_map/ppermute | solution.py:44
  124.3 2.9 %collective-permute-start.5 = (bf16[16,4352]{1,0:T(8,128)(2,1)S(1)}, bf16[16,4352]{1,0:T(8,128)(2,1)S(1)}, u32[]{:S(2)}, u32[]{:S(2)}) collective-permute-start(bf16[16,4352]{1,0:T(8,128)(2,1)S(1)} %get-tuple-element.53), channel_id=1, source_target_pairs={{1,0},{2,1},{3,2},{4,3},{5,4},{6,5},{7,6},{8,7},{9,8},{10,9},{11,1... | collective-permute-start | bytes 417800 | tf_op jit(solution)/shard_map/ppermute | solution.py:44
  127.2 0.0 copy-done.4
  127.2 2.7 %interior.1 = (bf16[96,4096]{1,0:T(8,128)(2,1)S(1)}, bf16[32,4352]{1,0:T(8,128)(2,1)S(1)}, bf16[32,4352]{1,0:T(8,128)(2,1)S(1)}) custom-call(f32[3,4352]{1,0:T(4,128)S(1)} %add_convert_fusion.keep_ref, bf16[336,256]{1,0:T(8,128)(2,1)S(1)} %get-tuple-element.54.first_ref, bf16[288,224]{1,0:T(8,128)(2,1)S(1)} %get-tuple-element.55.second_ref, ...), custom_call_target="tpu_custom_call" | custom-call | tf_op jit(solution)/shard_map/interior/pallas_call | solution.py:298
  129.9 0.0 collective-permute-done.4.left_ref
  129.9 1.3 collective-permute-done.5.right_ref
  131.2 0.0 copy-done.3
  131.2 1.9 %rim.1 = bf16[8,16,4096]{2,1,0:T(8,128)(2,1)} custom-call(f32[3,4352]{1,0:T(4,128)S(1)} %add_convert_fusion.keep_ref, bf16[96,128]{1,0:T(8,128)(2,1)S(1)} %get-tuple-element.47.first_ref, bf16[96,128]{1,0:T(8,128)(2,1)S(1)} %get-tuple-element.48.second_ref, bf16[128,128]{1,0:T(8,128)(2,1)S(1)} %copy-done.3, ...), custom_call_target="tpu_custom_call" | custom-call | tf_op jit(solution)/shard_map/rim/pallas_call | solution.py:306
  (9 shorter events, 0.2 us)
Async XLA Ops:
  0.0 15.0 %collective-permute-start = (s32[1,2,2]{2,1,0:T(2,128)}, s32[1,2,2]{2,1,0:T(2,128)S(1)}, u32[]{:S(2)}, u32[]{:S(2)}) collective-permute-start(s32[1,2,2]{2,1,0:T(2,128)} %coarse_ref.1), channel_id=1, source_target_pairs={{1,0},{2,1},{3,2},{4,3},{5,4},{6,5},{7,6},{8,7},{9,8},{10,9},{11,1... | collective-permute-start | bytes 56 | tf_op jit(solution)/shard_map/ppermute | solution.py:44
  11.6 7.8 %collective-permute-start.1 = (s32[1,2,2]{2,1,0:T(2,128)}, s32[1,2,2]{2,1,0:T(2,128)S(1)}, u32[]{:S(2)}, u32[]{:S(2)}) collective-permute-start(s32[1,2,2]{2,1,0:T(2,128)} %coarse_ref.1), channel_id=1, source_target_pairs={{0,1},{1,2},{2,3},{3,4},{4,5},{5,6},{6,7},{7,8},{8,9},{9,10},{10,1... | collective-permute-start | bytes 56 | tf_op jit(solution)/shard_map/ppermute | solution.py:44
  13.6 1.2 copy-start
  15.0 13.0 %copy-start.10 = (f32[1,2,2]{2,1,0:T(2,128)S(1)}, f32[1,2,2]{2,1,0:T(2,128)}, u32[]{:S(2)}) copy-start(f32[1,2,2]{2,1,0:T(2,128)} %fraction_ref) | copy-start | bytes 52
  19.7 9.3 %copy-start.1 = (s32[112,128]{1,0:T(8,128)S(1)}, s32[112,128]{1,0:T(8,128)}, u32[]{:S(2)}) copy-start(s32[112,128]{1,0:T(8,128)} %constant.35.clone.refs_0_) | copy-start | bytes 172036
  19.7 9.3 %copy-start.2 = (s32[96,112]{1,0:T(8,128)S(1)}, s32[96,112]{1,0:T(8,128)}, u32[]{:S(2)}) copy-start(s32[96,112]{1,0:T(8,128)} %constant.36.clone.refs_1_) | copy-start | bytes 129028
  19.7 9.3 %copy-start.5 = (s32[32,64]{1,0:T(8,128)S(1)}, s32[32,64]{1,0:T(8,128)}, u32[]{:S(2)}) copy-start(s32[32,64]{1,0:T(8,128)} %constant.38.clone.refs_3_) | copy-start | bytes 24580
  19.7 9.3 %copy-start.6 = (s32[32,64]{1,0:T(8,128)S(1)}, s32[32,64]{1,0:T(8,128)}, u32[]{:S(2)}) copy-start(s32[32,64]{1,0:T(8,128)} %constant.37.clone.refs_2_) | copy-start | bytes 24580
  19.7 9.3 %copy-start.8 = (f32[3,3,3]{2,1,0:T(4,128)S(1)}, f32[3,3,3]{2,1,0:T(4,128)}, u32[]{:S(2)}) copy-start(f32[3,3,3]{2,1,0:T(4,128)} %one_ref) | copy-start | bytes 328
  19.8 9.2 %copy-start.9 = (f32[3,3,3]{2,1,0:T(4,128)S(1)}, f32[3,3,3]{2,1,0:T(4,128)}, u32[]{:S(2)}) copy-start(f32[3,3,3]{2,1,0:T(4,128)} %two_ref) | copy-start | bytes 328
  19.8 16.4 %collective-permute-start.2 = (bf16[1,512,512]{2,1,0:T(8,128)(2,1)S(1)}, bf16[1,512,512]{2,1,0:T(8,128)(2,1)S(1)}, u32[]{:S(2)}, u32[]{:S(2)}) collective-permute-start(bf16[1,512,512]{2,1,0:T(8,128)(2,1)S(1)} %get-tuple-element.37), channel_id=1, source_target_pairs={{0,1},{1,2},{2,3},{3,4},{4,5},{5,6},{6,7},{7,8},{8,9},{9,10},{10,1... | collective-permute-start | bytes 1572872 | tf_op jit(solution)/shard_map/ppermute | solution.py:44
  21.8 15.5 %collective-permute-start.3 = (bf16[1,512,512]{2,1,0:T(8,128)(2,1)S(1)}, bf16[1,512,512]{2,1,0:T(8,128)(2,1)S(1)}, u32[]{:S(2)}, u32[]{:S(2)}) collective-permute-start(bf16[1,512,512]{2,1,0:T(8,128)(2,1)S(1)} %get-tuple-element.38), channel_id=1, source_target_pairs={{1,0},{2,1},{3,2},{4,3},{5,4},{6,5},{7,6},{8,7},{9,8},{10,9},{11,1... | collective-permute-start | bytes 1572872 | tf_op jit(solution)/shard_map/ppermute | solution.py:44
  28.0 9.4 %copy-start.11 = (s32[1,2,2]{2,1,0:T(2,128)S(1)}, s32[1,2,2]{2,1,0:T(2,128)}, u32[]{:S(2)}) copy-start(s32[1,2,2]{2,1,0:T(2,128)} %coarse_ref.1) | copy-start | bytes 52
  97.9 20.9 %copy-start.7 = (bf16[32,128]{1,0:T(8,128)(2,1)S(1)}, bf16[32,128]{1,0:T(8,128)(2,1)}, u32[]{:S(2)}) copy-start(bf16[32,128]{1,0:T(8,128)(2,1)} %constant.39.clone.take_ref) | copy-start | bytes 24580
  118.8 8.4 %copy-start.4 = (bf16[128,128]{1,0:T(8,128)(2,1)S(1)}, bf16[128,128]{1,0:T(8,128)(2,1)}, u32[]{:S(2)}) copy-start(bf16[128,128]{1,0:T(8,128)(2,1)} %constant.40.clone.order_ref) | copy-start | bytes 98308
  118.8 12.4 %copy-start.3 = (bf16[128,128]{1,0:T(8,128)(2,1)S(1)}, bf16[128,128]{1,0:T(8,128)(2,1)}, u32[]{:S(2)}) copy-start(bf16[128,128]{1,0:T(8,128)(2,1)} %constant.41.clone.put_ref) | copy-start | bytes 98308
  119.2 10.7 %collective-permute-start.4 = (bf16[16,4352]{1,0:T(8,128)(2,1)S(1)}, bf16[16,4352]{1,0:T(8,128)(2,1)S(1)}, u32[]{:S(2)}, u32[]{:S(2)}) collective-permute-start(bf16[16,4352]{1,0:T(8,128)(2,1)S(1)} %get-tuple-element.52), channel_id=1, source_target_pairs={{0,1},{1,2},{2,3},{3,4},{4,5},{5,6},{6,7},{7,8},{8,9},{9,10},{10,1... | collective-permute-start | bytes 417800 | tf_op jit(solution)/shard_map/ppermute | solution.py:44
  124.3 7.0 %collective-permute-start.5 = (bf16[16,4352]{1,0:T(8,128)(2,1)S(1)}, bf16[16,4352]{1,0:T(8,128)(2,1)S(1)}, u32[]{:S(2)}, u32[]{:S(2)}) collective-permute-start(bf16[16,4352]{1,0:T(8,128)(2,1)S(1)} %get-tuple-element.53), channel_id=1, source_target_pairs={{1,0},{2,1},{3,2},{4,3},{5,4},{6,5},{7,6},{8,7},{9,8},{10,9},{11,1... | collective-permute-start | bytes 417800 | tf_op jit(solution)/shard_map/ppermute | solution.py:44

commit v8 on v7

--- a/solution.py
+++ b/solution.py
@@ -141,6 +141,19 @@
         stencil_matrix(index_ref[...], one_ref if place % 2 == 0 else two_ref, out_ref)
 
 
+def spread_body(data_ref, out_ref):
+    parts, chunks, cols, lanes = out_ref.shape
+    count = chunks - 1
+    low = lax.broadcasted_iota(jnp.int32, (cols, lanes), 1) < lanes // 2
+    nothing = jnp.zeros((cols, lanes), F32)
+    for part in range(parts):
+        first, end = part * count, (part + 1) * count
+        before = data_ref[first - 1].astype(F32) if part > 0 else nothing
+        after = data_ref[end].astype(F32) if part < parts - 1 else nothing
+        out_ref[part, 0] = jnp.where(low, after, before).astype(BF16)
+        out_ref[part, 1:chunks] = data_ref[first:end]
+
+
 def edges_body(data_ref, take_ref, first_ref, last_ref):
     sections, chunks, cols, lanes = data_ref.shape
     side = first_ref.shape[0]
@@ -182,7 +195,7 @@
     pass_ref[0:rows] = passed
     pass_ref[rows : 2 * rows] = passed
     total = shifted_sum(second_ref, pass_ref[...], main - rim) + ordered[rim:]
-    out_ref[...] = total[:, lanes : length - lanes].astype(BF16)
+    out_ref[...] = total[:, lanes:].astype(BF16)
 
 
 def rim_body(keep_ref, first_ref, second_ref, put_ref, left_ref, right_ref, passed_ref, aligned_ref, inner_ref, out_ref, volume_ref, pass_ref, done_ref, sems):
@@ -207,7 +220,7 @@
         pass_ref[start : start + inner] = passed_ref[...]
         pass_ref[start + inner : start + inner + rows] = passed
     second = shifted_sum(second_ref, pass_ref[...], rim)
-    total = (second + aligned_ref[...].astype(F32))[:, lanes : length - lanes].astype(BF16)
+    total = (second + aligned_ref[...].astype(F32))[:, lanes:].astype(BF16)
     pieces = sems.shape[0]
     width = total.shape[1] // pieces
     copies = []
@@ -276,9 +289,10 @@
 
     at_xy, at_sec = lax.axis_index("xy"), lax.axis_index("sec")
     per_sec = n_xy * chunks // n_sec
-    length = (per_sec + 2) * LANES
+    length = (per_sec + 1) * LANES
     lane = jnp.arange(length, dtype=jnp.int32)
-    real = (lane >= jnp.where(at_sec == 0, LANES, 0)) & (lane < length - jnp.where(at_sec == n_sec - 1, LANES, 0))
+    after, before = lane < LANES // 2, (lane >= LANES // 2) & (lane < LANES)
+    real = ~(after & (at_sec == n_sec - 1)) & ~(before & (at_sec == 0))
     keep = jnp.stack([real, real & (at_xy > 0), real & (at_xy < n_xy - 1)]).astype(F32)
     above, below, matrix, stencils, keep = lax.optimization_barrier((above, below, matrix, stencils, keep))
 
@@ -286,8 +300,9 @@
         coarse, staged, above, below, matrix
     )
     mine = lax.all_to_all(strip, "xy", split_axis=0, concat_axis=0, tiled=True)
-    mine = jnp.pad(mine.reshape(n_xy * chunks, cols, LANES), ((1, 1), (0, 0), (0, 0)))
-    spread = jnp.stack([mine[index * per_sec : (index + 1) * per_sec + 2] for index in range(n_sec)])
+    spread = call(spread_body, shaped(n_sec, per_sec + 1, cols, LANES), [VMEM], "spread", 8)(
+        mine.reshape(n_xy * chunks, cols, LANES)
+    )
     data = lax.all_to_all(spread, "sec", split_axis=0, concat_axis=0, tiled=True)
 
     out = shaped(n_sec, cols, per_sec * LANES)

time: 134 us -> 133 us (level)
  no operation moved by 1% of the time
where the time goes in v8:
time: 133 us
  blocking collectives  79.3 us (60%)
  starting transfers between devices  29.4 us (22%)
  waiting for transfers between devices  13 us (10%)
  Pallas kernels  9.18 us (7%)
    all_to_all x1, blocking collectives, body(): mine = lax.all_to_all(strip, 'xy', split_axis=0, concat_axis=0, tiled=True)  58.8 us
    ppermute x6, starting transfers between devices, from_behind(): return lax.ppermute(value, axis, shift_pairs(lax.axis_size(axis), steps))  29.4 us
    all_to_all x1, blocking collectives, body(): lax.all_to_all(spread, 'sec', split_axis=0, concat_axis=0, tiled=True)  20.6 us
    ppermute x6, waiting for transfers between devices, from_behind(): return lax.ppermute(value, axis, shift_pairs(lax.axis_size(axis), steps))  13 us
    pallas_call x1, Pallas kernels, body(): call(interior_body, (shaped(len(inner_out), per_sec * LANES), shaped(len(...  2.74 us
  transfers between devices with their start and end apart: 6, of which 4 were waited for; matrix products, arithmetic and copies ran while one was open for 0% of the time, Pallas kernels for 4%

profile of v8, /device:TPU:24, one launch (start us, length us, event | category | flops | bytes accessed | tf_op | source)
XLA Modules:
  0.0 132.6 jit_solution(9456865473417567345)
XLA Ops:
  0.0 11.6 %collective-permute-start = (s32[1,2,2]{2,1,0:T(2,128)}, s32[1,2,2]{2,1,0:T(2,128)S(1)}, u32[]{:S(2)}, u32[]{:S(2)}) collective-permute-start(s32[1,2,2]{2,1,0:T(2,128)} %coarse_ref.1), channel_id=1, source_target_pairs={{1,0},{2,1},{3,2},{4,3},{5,4},{6,5},{7,6},{8,7},{9,8},{10,9},{11,1... | collective-permute-start | bytes 56 | tf_op jit(solution)/shard_map/ppermute | solution.py:44
  11.6 1.9 %collective-permute-start.1 = (s32[1,2,2]{2,1,0:T(2,128)}, s32[1,2,2]{2,1,0:T(2,128)S(1)}, u32[]{:S(2)}, u32[]{:S(2)}) collective-permute-start(s32[1,2,2]{2,1,0:T(2,128)} %coarse_ref.1), channel_id=1, source_target_pairs={{0,1},{1,2},{2,3},{3,4},{4,5},{5,6},{6,7},{7,8},{8,9},{9,10},{10,1... | collective-permute-start | bytes 56 | tf_op jit(solution)/shard_map/ppermute | solution.py:44
  13.6 0.0 copy-start
  13.6 1.2 copy-done
  14.8 0.1 stage.1.source_ref
  14.9 0.0 copy-start.10
  14.9 0.0 collective-permute-done.below_ref
  14.9 4.5 %collective-permute-done.1.above_ref = s32[1,2,2]{2,1,0:T(2,128)S(1)} collective-permute-done((s32[1,2,2]{2,1,0:T(2,128)}, s32[1,2,2]{2,1,0:T(2,128)S(1)}, u32[]{:S(2)}, u32[]{:S(2)}) %collective-permute-start.1) | collective-permute-done | bytes 48 | tf_op jit(solution)/shard_map/ppermute | solution.py:44
  19.4 0.3 choose.1
  19.7 1.9 %collective-permute-start.2 = (bf16[1,512,512]{2,1,0:T(8,128)(2,1)S(1)}, bf16[1,512,512]{2,1,0:T(8,128)(2,1)S(1)}, u32[]{:S(2)}, u32[]{:S(2)}) collective-permute-start(bf16[1,512,512]{2,1,0:T(8,128)(2,1)S(1)} %get-tuple-element.37), channel_id=1, source_target_pairs={{0,1},{1,2},{2,3},{3,4},{4,5},{5,6},{6,7},{7,8},{8,9},{9,10},{10,1... | collective-permute-start | bytes 1572872 | tf_op jit(solution)/shard_map/ppermute | solution.py:44
  21.6 6.0 %collective-permute-start.3 = (bf16[1,512,512]{2,1,0:T(8,128)(2,1)S(1)}, bf16[1,512,512]{2,1,0:T(8,128)(2,1)S(1)}, u32[]{:S(2)}, u32[]{:S(2)}) collective-permute-start(bf16[1,512,512]{2,1,0:T(8,128)(2,1)S(1)} %get-tuple-element.38), channel_id=1, source_target_pairs={{1,0},{2,1},{3,2},{4,3},{5,4},{6,5},{7,6},{8,7},{9,8},{10,9},{11,1... | collective-permute-start | bytes 1572872 | tf_op jit(solution)/shard_map/ppermute | solution.py:44
  27.7 0.0 copy-start.1
  27.7 0.0 copy-start.2
  27.7 0.0 copy-start.5
  27.7 0.0 copy-start.6
  27.7 0.0 copy-start.8
  27.7 0.0 copy-start.9
  27.7 0.1 add_convert_fusion.keep_ref
  27.8 0.0 copy-done.10
  27.8 0.0 copy-start.11
  27.8 1.0 matrices.1.matrix_ref
  28.8 0.0 copy-done.1
  28.8 0.0 copy-done.2
  28.8 0.0 copy-done.5
  28.9 0.0 copy-done.6
  28.9 0.0 copy-done.8
  28.9 0.0 copy-done.9
  28.9 1.0 stencils.1
  29.9 6.0 %collective-permute-done.2.above_ref = bf16[1,512,512]{2,1,0:T(8,128)(2,1)S(1)} collective-permute-done((bf16[1,512,512]{2,1,0:T(8,128)(2,1)S(1)}, bf16[1,512,512]{2,1,0:T(8,128)(2,1)S(1)}, u32[]{:S(2)}, u32[]{:S(2)}) %collective-permute-start.2) | collective-permute-done | bytes 524320 | tf_op jit(solution)/shard_map/ppermute | solution.py:44
  35.9 1.2 collective-permute-done.3.below_ref
  37.1 0.0 copy-done.11
  37.1 1.6 %warp.1 = bf16[64,4,16,128]{3,2,1,0:T(8,128)(2,1)S(1)} custom-call(s32[1,2,2]{2,1,0:T(2,128)S(1)} %copy-done.11, bf16[1,512,1024]{2,1,0:T(8,128)(2,1)S(1)} %stage.1.source_ref, bf16[1,512,512]{2,1,0:T(8,128)(2,1)S(1)} %collective-permute-done.2.above_ref, bf16[1,512,512]{2,1,0:T(8,128)(2,1)S(1)} %collective-permute-done.3.below_ref, ...), custom_call_target="tpu_custom_call" | custom-call | tf_op jit(solution)/shard_map/warp/pallas_call | solution.py:299
  38.7 58.8 %all_to_all.10 = bf16[64,4,16,128]{3,2,1,0:T(8,128)(2,1)S(1)} all-to-all(bf16[64,4,16,128]{3,2,1,0:T(8,128)(2,1)S(1)} %warp.1), channel_id=1, replica_groups=mesh['sec'=8,'xy'=64] {'xy'}, dimensions={0} | all-to-all | bytes 2097152 | tf_op jit(solution)/shard_map/all_to_all | solution.py:302
  97.5 0.1 spread.1
  97.6 0.0 copy-start.7
  97.6 20.6 %all_to_all.11.data_ref = bf16[8,33,16,128]{3,2,1,0:T(8,128)(2,1)S(1)} all-to-all(bf16[8,33,16,128]{3,2,1,0:T(8,128)(2,1)S(1)} %spread.1), channel_id=1, replica_groups=mesh['sec'=8,'xy'=64] {'sec'}, dimensions={0} | all-to-all | bytes 2162688 | tf_op jit(solution)/shard_map/all_to_all | solution.py:306
  118.1 0.0 copy-done.7
  118.1 0.0 copy-start.4
  118.2 0.0 copy-start.3
  118.2 0.4 edges.1
  118.6 5.0 %collective-permute-start.4 = (bf16[16,4224]{1,0:T(8,128)(2,1)S(1)}, bf16[16,4224]{1,0:T(8,128)(2,1)S(1)}, u32[]{:S(2)}, u32[]{:S(2)}) collective-permute-start(bf16[16,4224]{1,0:T(8,128)(2,1)S(1)} %get-tuple-element.52), channel_id=1, source_target_pairs={{0,1},{1,2},{2,3},{3,4},{4,5},{5,6},{6,7},{7,8},{8,9},{9,10},{10,1... | collective-permute-start | bytes 405512 | tf_op jit(solution)/shard_map/ppermute | solution.py:44
  123.6 2.9 %collective-permute-start.5 = (bf16[16,4224]{1,0:T(8,128)(2,1)S(1)}, bf16[16,4224]{1,0:T(8,128)(2,1)S(1)}, u32[]{:S(2)}, u32[]{:S(2)}) collective-permute-start(bf16[16,4224]{1,0:T(8,128)(2,1)S(1)} %get-tuple-element.53), channel_id=1, source_target_pairs={{1,0},{2,1},{3,2},{4,3},{5,4},{6,5},{7,6},{8,7},{9,8},{10,9},{11,1... | collective-permute-start | bytes 405512 | tf_op jit(solution)/shard_map/ppermute | solution.py:44
  126.5 0.0 copy-done.4
  126.5 2.7 %interior.1 = (bf16[96,4096]{1,0:T(8,128)(2,1)S(1)}, bf16[32,4224]{1,0:T(8,128)(2,1)S(1)}, bf16[32,4224]{1,0:T(8,128)(2,1)S(1)}) custom-call(f32[3,4224]{1,0:T(4,128)S(1)} %add_convert_fusion.keep_ref, bf16[336,256]{1,0:T(8,128)(2,1)S(1)} %get-tuple-element.54.first_ref, bf16[288,224]{1,0:T(8,128)(2,1)S(1)} %get-tuple-element.55.second_ref, ...), custom_call_target="tpu_custom_call" | custom-call | tf_op jit(solution)/shard_map/interior/pallas_call | solution.py:313
  129.3 0.0 collective-permute-done.4.left_ref
  129.3 1.3 collective-permute-done.5.right_ref
  130.6 0.0 copy-done.3
  130.6 2.0 %rim.1 = bf16[8,16,4096]{2,1,0:T(8,128)(2,1)} custom-call(f32[3,4224]{1,0:T(4,128)S(1)} %add_convert_fusion.keep_ref, bf16[96,128]{1,0:T(8,128)(2,1)S(1)} %get-tuple-element.47.first_ref, bf16[96,128]{1,0:T(8,128)(2,1)S(1)} %get-tuple-element.48.second_ref, bf16[128,128]{1,0:T(8,128)(2,1)S(1)} %copy-done.3, ...), custom_call_target="tpu_custom_call" | custom-call | tf_op jit(solution)/shard_map/rim/pallas_call | solution.py:321
  (2 shorter events, 0.0 us)
Async XLA Ops:
  0.0 14.9 %collective-permute-start = (s32[1,2,2]{2,1,0:T(2,128)}, s32[1,2,2]{2,1,0:T(2,128)S(1)}, u32[]{:S(2)}, u32[]{:S(2)}) collective-permute-start(s32[1,2,2]{2,1,0:T(2,128)} %coarse_ref.1), channel_id=1, source_target_pairs={{1,0},{2,1},{3,2},{4,3},{5,4},{6,5},{7,6},{8,7},{9,8},{10,9},{11,1... | collective-permute-start | bytes 56 | tf_op jit(solution)/shard_map/ppermute | solution.py:44
  11.6 7.8 %collective-permute-start.1 = (s32[1,2,2]{2,1,0:T(2,128)}, s32[1,2,2]{2,1,0:T(2,128)S(1)}, u32[]{:S(2)}, u32[]{:S(2)}) collective-permute-start(s32[1,2,2]{2,1,0:T(2,128)} %coarse_ref.1), channel_id=1, source_target_pairs={{0,1},{1,2},{2,3},{3,4},{4,5},{5,6},{6,7},{7,8},{8,9},{9,10},{10,1... | collective-permute-start | bytes 56 | tf_op jit(solution)/shard_map/ppermute | solution.py:44
  13.6 1.2 copy-start
  14.9 12.9 %copy-start.10 = (f32[1,2,2]{2,1,0:T(2,128)S(1)}, f32[1,2,2]{2,1,0:T(2,128)}, u32[]{:S(2)}) copy-start(f32[1,2,2]{2,1,0:T(2,128)} %fraction_ref) | copy-start | bytes 52
  19.7 16.2 %collective-permute-start.2 = (bf16[1,512,512]{2,1,0:T(8,128)(2,1)S(1)}, bf16[1,512,512]{2,1,0:T(8,128)(2,1)S(1)}, u32[]{:S(2)}, u32[]{:S(2)}) collective-permute-start(bf16[1,512,512]{2,1,0:T(8,128)(2,1)S(1)} %get-tuple-element.37), channel_id=1, source_target_pairs={{0,1},{1,2},{2,3},{3,4},{4,5},{5,6},{6,7},{7,8},{8,9},{9,10},{10,1... | collective-permute-start | bytes 1572872 | tf_op jit(solution)/shard_map/ppermute | solution.py:44
  21.6 15.5 %collective-permute-start.3 = (bf16[1,512,512]{2,1,0:T(8,128)(2,1)S(1)}, bf16[1,512,512]{2,1,0:T(8,128)(2,1)S(1)}, u32[]{:S(2)}, u32[]{:S(2)}) collective-permute-start(bf16[1,512,512]{2,1,0:T(8,128)(2,1)S(1)} %get-tuple-element.38), channel_id=1, source_target_pairs={{1,0},{2,1},{3,2},{4,3},{5,4},{6,5},{7,6},{8,7},{9,8},{10,9},{11,1... | collective-permute-start | bytes 1572872 | tf_op jit(solution)/shard_map/ppermute | solution.py:44
  27.7 1.2 copy-start.1
  27.7 1.2 copy-start.2
  27.7 1.2 copy-start.5
  27.7 1.2 copy-start.6
  27.7 1.2 copy-start.8
  27.7 1.1 copy-start.9
  27.8 9.3 %copy-start.11 = (s32[1,2,2]{2,1,0:T(2,128)S(1)}, s32[1,2,2]{2,1,0:T(2,128)}, u32[]{:S(2)}) copy-start(s32[1,2,2]{2,1,0:T(2,128)} %coarse_ref.1) | copy-start | bytes 52
  97.6 20.6 %copy-start.7 = (bf16[32,128]{1,0:T(8,128)(2,1)S(1)}, bf16[32,128]{1,0:T(8,128)(2,1)}, u32[]{:S(2)}) copy-start(bf16[32,128]{1,0:T(8,128)(2,1)} %constant.37.clone.take_ref) | copy-start | bytes 24580
  118.1 8.4 %copy-start.4 = (bf16[128,128]{1,0:T(8,128)(2,1)S(1)}, bf16[128,128]{1,0:T(8,128)(2,1)}, u32[]{:S(2)}) copy-start(bf16[128,128]{1,0:T(8,128)(2,1)} %constant.38.clone.order_ref) | copy-start | bytes 98308
  118.2 12.5 %copy-start.3 = (bf16[128,128]{1,0:T(8,128)(2,1)S(1)}, bf16[128,128]{1,0:T(8,128)(2,1)}, u32[]{:S(2)}) copy-start(bf16[128,128]{1,0:T(8,128)(2,1)} %constant.39.clone.put_ref) | copy-start | bytes 98308
  118.6 10.7 %collective-permute-start.4 = (bf16[16,4224]{1,0:T(8,128)(2,1)S(1)}, bf16[16,4224]{1,0:T(8,128)(2,1)S(1)}, u32[]{:S(2)}, u32[]{:S(2)}) collective-permute-start(bf16[16,4224]{1,0:T(8,128)(2,1)S(1)} %get-tuple-element.52), channel_id=1, source_target_pairs={{0,1},{1,2},{2,3},{3,4},{4,5},{5,6},{6,7},{7,8},{8,9},{9,10},{10,1... | collective-permute-start | bytes 405512 | tf_op jit(solution)/shard_map/ppermute | solution.py:44
  123.6 7.0 %collective-permute-start.5 = (bf16[16,4224]{1,0:T(8,128)(2,1)S(1)}, bf16[16,4224]{1,0:T(8,128)(2,1)S(1)}, u32[]{:S(2)}, u32[]{:S(2)}) collective-permute-start(bf16[16,4224]{1,0:T(8,128)(2,1)S(1)} %get-tuple-element.53), channel_id=1, source_target_pairs={{1,0},{2,1},{3,2},{4,3},{5,4},{6,5},{7,6},{8,7},{9,8},{10,9},{11,1... | collective-permute-start | bytes 405512 | tf_op jit(solution)/shard_map/ppermute | solution.py:44

commit v9 on v8

--- a/solution.py
+++ b/solution.py
@@ -90,30 +90,46 @@
                 out_ref[0] = source_ref[0, :, column * edge : (column + 1) * edge]
 
 
-def warp_body(coarse_ref, source_ref, above_ref, below_ref, matrix_ref, out_ref):
+def warp_block(matrix_ref, block, picked, out_ref):
+    edge = picked.shape[0]
+    total, chunks, cols, _ = out_ref.shape
+    groups = edge // cols
+    rows_warped = dot(matrix_ref[0, block], picked).astype(BF16)
+    warped = lax.dot_general(
+        matrix_ref[1, block], rows_warped, (((1,), (1,)), ((), ())), preferred_element_type=F32
+    ).astype(BF16)
+    warped = warped.reshape(groups, cols, edge)
+    for chunk in range(chunks):
+        out_ref[block * groups : (block + 1) * groups, chunk] = warped[:, :, chunk * LANES : (chunk + 1) * LANES]
+
+
+def block_offsets(coarse_ref, columns):
+    downs, anchors = offsets(coarse_ref)
+    lane = lax.broadcasted_iota(jnp.int32, downs.shape, 1)
+
+    def at(values, block):
+        return jnp.sum(jnp.where(lane == block, values, 0.0)).astype(jnp.int32)
+
+    return [(at(downs, block), at(anchors, block)) for block in range(columns)]
+
+
+def warp_body(coarse_ref, source_ref, matrix_ref, out_ref):
     _, edge, width = source_ref.shape
     columns = width // edge
-    groups = out_ref.shape[0] // columns
-    chunks, cols = out_ref.shape[1], out_ref.shape[2]
-    downs, anchors = offsets(coarse_ref)
-    lane = lax.broadcasted_iota(jnp.int32, downs.shape, 1)
-    for block in range(columns):
-        down = jnp.sum(jnp.where(lane == block, downs, 0.0)).astype(jnp.int32)
-        anchor = jnp.sum(jnp.where(lane == block, anchors, 0.0)).astype(jnp.int32)
+    for block, (_, anchor) in enumerate(block_offsets(coarse_ref, columns)):
         picked = source_ref[0, :, 0:edge]
         for column in range(1, columns):
             picked = jnp.where(anchor == column, source_ref[0, :, column * edge : (column + 1) * edge], picked)
-        picked = jnp.where(down < 0, above_ref[0], picked)
-        picked = jnp.where(down > 0, below_ref[0], picked)
-        rows_warped = dot(matrix_ref[0, block], picked).astype(BF16)
-        warped = lax.dot_general(
-            matrix_ref[1, block], rows_warped, (((1,), (1,)), ((), ())), preferred_element_type=F32
-        ).astype(BF16)
-        warped = warped.reshape(groups, cols, edge)
-        for chunk in range(chunks):
-            out_ref[block * groups : (block + 1) * groups, chunk] = warped[
-                :, :, chunk * LANES : (chunk + 1) * LANES
-            ]
+        warp_block(matrix_ref, block, picked, out_ref)
+
+
+def moved_body(sign, coarse_ref, moved_ref, matrix_ref, strip_ref, out_ref):
+    out_ref[...] = strip_ref[...]
+    for block, (down, _) in enumerate(block_offsets(coarse_ref, matrix_ref.shape[1])):
+
+        @pl.when(down == sign)
+        def _():
+            warp_block(matrix_ref, block, moved_ref[0], out_ref)
 
 
 def tap_index(out_pixels, in_pixels):
@@ -294,11 +310,13 @@
     after, before = lane < LANES // 2, (lane >= LANES // 2) & (lane < LANES)
     real = ~(after & (at_sec == n_sec - 1)) & ~(before & (at_sec == 0))
     keep = jnp.stack([real, real & (at_xy > 0), real & (at_xy < n_xy - 1)]).astype(F32)
-    above, below, matrix, stencils, keep = lax.optimization_barrier((above, below, matrix, stencils, keep))
-
-    strip = call(warp_body, shaped(n_xy, chunks, cols, LANES), [VMEM] * 5, "warp", 16)(
-        coarse, staged, above, below, matrix
-    )
+    strip_of = shaped(n_xy, chunks, cols, LANES)
+    strip = call(warp_body, strip_of, [VMEM] * 3, "warp", 16)(coarse, staged, matrix)
+    strip, stencils, keep, above = lax.optimization_barrier((strip, stencils, keep, above))
+    for moved, sign, name in ((above, -1, "warp_above"), (below, 1, "warp_below")):
+        strip = call(lambda *refs, sign=sign: moved_body(sign, *refs), strip_of, [VMEM] * 4, name, 16)(
+            coarse, moved, matrix, strip
+        )
     mine = lax.all_to_all(strip, "xy", split_axis=0, concat_axis=0, tiled=True)
     spread = call(spread_body, shaped(n_sec, per_sec + 1, cols, LANES), [VMEM], "spread", 8)(
         mine.reshape(n_xy * chunks, cols, LANES)

time: 133 us -> 132 us (level)
  waiting for transfers between devices: 13 us -> 5.54 us
  blocking collectives: 79.3 us -> 83.9 us
  Pallas kernels: 9.18 us -> 11.1 us
    ppermute x6, waiting for transfers between devices: 13 us -> 5.54 us  [from_behind(): return lax.ppermute(value, axis, shift_pairs(lax.axis_size(axis), steps))]
    all_to_all x1, blocking collectives: 58.8 us -> 62.6 us  [body(): mine = lax.all_to_all(strip, 'xy', split_axis=0, concat_axis=0, tiled=True)]
    pallas_call x1 -> x3, Pallas kernels: 1.59 us -> 3.49 us  [the longest x2 1.91 us: body(): call(lambda *refs, sign=sign: moved_body(sign, *refs), strip_of, [VMEM] *...]
  transfers between devices with their start and end apart: 6 -> 6, of which waited for: 4 -> 3; matrix products, arithmetic and copies ran while one was open for 0% -> 0% of each run, Pallas kernels for 4% -> 6%
where the time goes in v9:
time: 132 us
  blocking collectives  83.9 us (64%)
  starting transfers between devices  29.7 us (22%)
  Pallas kernels  11.1 us (8%)
  waiting for transfers between devices  5.54 us (4%)
    all_to_all x1, blocking collectives, body(): mine = lax.all_to_all(strip, 'xy', split_axis=0, concat_axis=0, tiled=True)  62.6 us
    ppermute x6, starting transfers between devices, from_behind(): return lax.ppermute(value, axis, shift_pairs(lax.axis_size(axis), steps))  29.7 us
    all_to_all x1, blocking collectives, body(): lax.all_to_all(spread, 'sec', split_axis=0, concat_axis=0, tiled=True)  21.3 us
    ppermute x6, waiting for transfers between devices, from_behind(): return lax.ppermute(value, axis, shift_pairs(lax.axis_size(axis), steps))  5.54 us
    pallas_call x1, Pallas kernels, body(): call(interior_body, (shaped(len(inner_out), per_sec * LANES), shaped(len(...  2.74 us
  transfers between devices with their start and end apart: 6, of which 3 were waited for; matrix products, arithmetic and copies ran while one was open for 0% of the time, Pallas kernels for 6%

profile of v9, /device:TPU:24, one launch (start us, length us, event | category | flops | bytes accessed | tf_op | source)
XLA Modules:
  0.0 131.9 jit_solution(574533419410489570)
XLA Ops:
  0.0 3.8 %collective-permute-start.1 = (s32[1,2,2]{2,1,0:T(2,128)}, s32[1,2,2]{2,1,0:T(2,128)S(1)}, u32[]{:S(2)}, u32[]{:S(2)}) collective-permute-start(s32[1,2,2]{2,1,0:T(2,128)} %refs_0_.4), channel_id=1, source_target_pairs={{0,1},{1,2},{2,3},{3,4},{4,5},{5,6},{6,7},{7,8},{8,9},{9,10},{10,1... | collective-permute-start | bytes 56 | tf_op jit(solution)/shard_map/ppermute | solution.py:44
  3.8 9.7 %collective-permute-start = (s32[1,2,2]{2,1,0:T(2,128)}, s32[1,2,2]{2,1,0:T(2,128)S(1)}, u32[]{:S(2)}, u32[]{:S(2)}) collective-permute-start(s32[1,2,2]{2,1,0:T(2,128)} %refs_0_.4), channel_id=1, source_target_pairs={{1,0},{2,1},{3,2},{4,3},{5,4},{6,5},{7,6},{8,7},{9,8},{10,9},{11,1... | collective-permute-start | bytes 56 | tf_op jit(solution)/shard_map/ppermute | solution.py:44
  13.6 0.0 copy-start
  13.6 1.2 copy-done
  14.8 0.1 stage.1.source_ref
  14.9 0.0 copy-start.11
  14.9 0.0 collective-permute-done.1.above_ref
  14.9 0.1 collective-permute-done.below_ref
  15.0 0.3 choose.1
  15.3 1.9 %collective-permute-start.2 = (bf16[1,512,512]{2,1,0:T(8,128)(2,1)S(1)}, bf16[1,512,512]{2,1,0:T(8,128)(2,1)S(1)}, u32[]{:S(2)}, u32[]{:S(2)}) collective-permute-start(bf16[1,512,512]{2,1,0:T(8,128)(2,1)S(1)} %get-tuple-element.43), channel_id=1, source_target_pairs={{0,1},{1,2},{2,3},{3,4},{4,5},{5,6},{6,7},{7,8},{8,9},{9,10},{10,1... | collective-permute-start | bytes 1572872 | tf_op jit(solution)/shard_map/ppermute | solution.py:44
  17.3 6.3 %collective-permute-start.3 = (bf16[1,512,512]{2,1,0:T(8,128)(2,1)S(1)}, bf16[1,512,512]{2,1,0:T(8,128)(2,1)S(1)}, u32[]{:S(2)}, u32[]{:S(2)}) collective-permute-start(bf16[1,512,512]{2,1,0:T(8,128)(2,1)S(1)} %get-tuple-element.47), channel_id=1, source_target_pairs={{1,0},{2,1},{3,2},{4,3},{5,4},{6,5},{7,6},{8,7},{9,8},{10,9},{11,1... | collective-permute-start | bytes 1572872 | tf_op jit(solution)/shard_map/ppermute | solution.py:44
  23.6 0.0 copy-start.7
  23.6 0.1 add_convert_fusion.keep_ref
  23.6 0.0 copy-done.11
  23.7 1.0 matrices.1.matrix_ref.refs_2_
  24.6 0.0 copy-done.7
  24.6 0.0 copy-start.1
  24.7 0.0 copy-start.2
  24.7 0.0 copy-start.5
  24.7 0.0 copy-start.6
  24.7 0.0 copy-start.9
  24.7 0.0 copy-start.10
  24.7 1.6 %warp.1.refs_3_ = bf16[64,4,16,128]{3,2,1,0:T(8,128)(2,1)S(1)} custom-call(s32[1,2,2]{2,1,0:T(2,128)S(1)} %copy-done.7, bf16[1,512,1024]{2,1,0:T(8,128)(2,1)S(1)} %stage.1.source_ref, bf16[2,2,512,512]{3,2,1,0:T(8,128)(2,1)S(1)} %matrices.1.matrix_ref.refs_2_), custom_call_target="tpu_custom_call" | custom-call | tf_op jit(solution)/shard_map/warp/pallas_call | solution.py:314
  26.3 0.0 copy-done.1
  26.3 0.0 copy-done.2
  26.3 0.0 copy-done.5
  26.3 0.0 copy-done.6
  26.4 0.0 copy-done.9
  26.4 0.0 copy-done.10
  26.4 1.0 stencils.1
  27.4 5.2 %collective-permute-done.2.refs_1_ = bf16[1,512,512]{2,1,0:T(8,128)(2,1)S(1)} collective-permute-done((bf16[1,512,512]{2,1,0:T(8,128)(2,1)S(1)}, bf16[1,512,512]{2,1,0:T(8,128)(2,1)S(1)}, u32[]{:S(2)}, u32[]{:S(2)}) %collective-permute-start.2) | collective-permute-done | bytes 524320 | tf_op jit(solution)/shard_map/ppermute | solution.py:44
  32.6 1.0 warp_above.1.refs_3_
  33.6 0.2 collective-permute-done.3.refs_1_
  33.8 1.0 warp_below.1
  34.8 62.6 %all_to_all.10 = bf16[64,4,16,128]{3,2,1,0:T(8,128)(2,1)S(1)} all-to-all(bf16[64,4,16,128]{3,2,1,0:T(8,128)(2,1)S(1)} %warp_below.1), channel_id=1, replica_groups=mesh['sec'=8,'xy'=64] {'xy'}, dimensions={0} | all-to-all | bytes 2097152 | tf_op jit(solution)/shard_map/all_to_all | solution.py:320
  97.4 0.1 spread.1
  97.5 0.0 copy-start.8
  97.5 21.3 %all_to_all.11.data_ref = bf16[8,33,16,128]{3,2,1,0:T(8,128)(2,1)S(1)} all-to-all(bf16[8,33,16,128]{3,2,1,0:T(8,128)(2,1)S(1)} %spread.1), channel_id=1, replica_groups=mesh['sec'=8,'xy'=64] {'sec'}, dimensions={0} | all-to-all | bytes 2162688 | tf_op jit(solution)/shard_map/all_to_all | solution.py:324
  118.8 0.0 copy-done.8
  118.8 0.0 copy-start.4
  118.8 0.0 copy-start.3
  118.8 0.4 edges.1
  119.2 3.4 %collective-permute-start.4 = (bf16[16,4224]{1,0:T(8,128)(2,1)S(1)}, bf16[16,4224]{1,0:T(8,128)(2,1)S(1)}, u32[]{:S(2)}, u32[]{:S(2)}) collective-permute-start(bf16[16,4224]{1,0:T(8,128)(2,1)S(1)} %get-tuple-element.50), channel_id=1, source_target_pairs={{0,1},{1,2},{2,3},{3,4},{4,5},{5,6},{6,7},{7,8},{8,9},{9,10},{10,1... | collective-permute-start | bytes 405512 | tf_op jit(solution)/shard_map/ppermute | solution.py:44
  122.6 4.6 %collective-permute-start.5 = (bf16[16,4224]{1,0:T(8,128)(2,1)S(1)}, bf16[16,4224]{1,0:T(8,128)(2,1)S(1)}, u32[]{:S(2)}, u32[]{:S(2)}) collective-permute-start(bf16[16,4224]{1,0:T(8,128)(2,1)S(1)} %get-tuple-element.51), channel_id=1, source_target_pairs={{1,0},{2,1},{3,2},{4,3},{5,4},{6,5},{7,6},{8,7},{9,8},{10,9},{11,1... | collective-permute-start | bytes 405512 | tf_op jit(solution)/shard_map/ppermute | solution.py:44
  127.2 0.0 copy-done.4
  127.2 2.7 %interior.1 = (bf16[96,4096]{1,0:T(8,128)(2,1)S(1)}, bf16[32,4224]{1,0:T(8,128)(2,1)S(1)}, bf16[32,4224]{1,0:T(8,128)(2,1)S(1)}) custom-call(f32[3,4224]{1,0:T(4,128)S(1)} %add_convert_fusion.keep_ref, bf16[336,256]{1,0:T(8,128)(2,1)S(1)} %get-tuple-element.52.first_ref, bf16[288,224]{1,0:T(8,128)(2,1)S(1)} %get-tuple-element.53.second_ref, ...), custom_call_target="tpu_custom_call" | custom-call | tf_op jit(solution)/shard_map/interior/pallas_call | solution.py:331
  129.9 0.0 collective-permute-done.4.left_ref
  129.9 0.0 collective-permute-done.5.right_ref
  129.9 0.0 copy-done.3
  130.0 2.0 %rim.1 = bf16[8,16,4096]{2,1,0:T(8,128)(2,1)} custom-call(f32[3,4224]{1,0:T(4,128)S(1)} %add_convert_fusion.keep_ref, bf16[96,128]{1,0:T(8,128)(2,1)S(1)} %get-tuple-element.45.first_ref, bf16[96,128]{1,0:T(8,128)(2,1)S(1)} %get-tuple-element.46.second_ref, bf16[128,128]{1,0:T(8,128)(2,1)S(1)} %copy-done.3, ...), custom_call_target="tpu_custom_call" | custom-call | tf_op jit(solution)/shard_map/rim/pallas_call | solution.py:339
  (2 shorter events, 0.0 us)
Async XLA Ops:
  0.0 14.9 %collective-permute-start.1 = (s32[1,2,2]{2,1,0:T(2,128)}, s32[1,2,2]{2,1,0:T(2,128)S(1)}, u32[]{:S(2)}, u32[]{:S(2)}) collective-permute-start(s32[1,2,2]{2,1,0:T(2,128)} %refs_0_.4), channel_id=1, source_target_pairs={{0,1},{1,2},{2,3},{3,4},{4,5},{5,6},{6,7},{7,8},{8,9},{9,10},{10,1... | collective-permute-start | bytes 56 | tf_op jit(solution)/shard_map/ppermute | solution.py:44
  3.8 11.2 %collective-permute-start = (s32[1,2,2]{2,1,0:T(2,128)}, s32[1,2,2]{2,1,0:T(2,128)S(1)}, u32[]{:S(2)}, u32[]{:S(2)}) collective-permute-start(s32[1,2,2]{2,1,0:T(2,128)} %refs_0_.4), channel_id=1, source_target_pairs={{1,0},{2,1},{3,2},{4,3},{5,4},{6,5},{7,6},{8,7},{9,8},{10,9},{11,1... | collective-permute-start | bytes 56 | tf_op jit(solution)/shard_map/ppermute | solution.py:44
  13.6 1.2 copy-start
  14.9 8.8 %copy-start.11 = (f32[1,2,2]{2,1,0:T(2,128)S(1)}, f32[1,2,2]{2,1,0:T(2,128)}, u32[]{:S(2)}) copy-start(f32[1,2,2]{2,1,0:T(2,128)} %fraction_ref) | copy-start | bytes 52
  15.3 17.3 %collective-permute-start.2 = (bf16[1,512,512]{2,1,0:T(8,128)(2,1)S(1)}, bf16[1,512,512]{2,1,0:T(8,128)(2,1)S(1)}, u32[]{:S(2)}, u32[]{:S(2)}) collective-permute-start(bf16[1,512,512]{2,1,0:T(8,128)(2,1)S(1)} %get-tuple-element.43), channel_id=1, source_target_pairs={{0,1},{1,2},{2,3},{3,4},{4,5},{5,6},{6,7},{7,8},{8,9},{9,10},{10,1... | collective-permute-start | bytes 1572872 | tf_op jit(solution)/shard_map/ppermute | solution.py:44
  17.3 16.6 %collective-permute-start.3 = (bf16[1,512,512]{2,1,0:T(8,128)(2,1)S(1)}, bf16[1,512,512]{2,1,0:T(8,128)(2,1)S(1)}, u32[]{:S(2)}, u32[]{:S(2)}) collective-permute-start(bf16[1,512,512]{2,1,0:T(8,128)(2,1)S(1)} %get-tuple-element.47), channel_id=1, source_target_pairs={{1,0},{2,1},{3,2},{4,3},{5,4},{6,5},{7,6},{8,7},{9,8},{10,9},{11,1... | collective-permute-start | bytes 1572872 | tf_op jit(solution)/shard_map/ppermute | solution.py:44
  23.6 1.1 copy-start.7
  24.6 1.7 %copy-start.1 = (s32[112,128]{1,0:T(8,128)S(1)}, s32[112,128]{1,0:T(8,128)}, u32[]{:S(2)}) copy-start(s32[112,128]{1,0:T(8,128)} %constant.33.clone.refs_0_) | copy-start | bytes 172036
  24.7 1.7 %copy-start.2 = (s32[96,112]{1,0:T(8,128)S(1)}, s32[96,112]{1,0:T(8,128)}, u32[]{:S(2)}) copy-start(s32[96,112]{1,0:T(8,128)} %constant.34.clone.refs_1_) | copy-start | bytes 129028
  24.7 1.7 %copy-start.5 = (s32[32,64]{1,0:T(8,128)S(1)}, s32[32,64]{1,0:T(8,128)}, u32[]{:S(2)}) copy-start(s32[32,64]{1,0:T(8,128)} %constant.36.clone.refs_3_) | copy-start | bytes 24580
  24.7 1.7 %copy-start.6 = (s32[32,64]{1,0:T(8,128)S(1)}, s32[32,64]{1,0:T(8,128)}, u32[]{:S(2)}) copy-start(s32[32,64]{1,0:T(8,128)} %constant.35.clone.refs_2_) | copy-start | bytes 24580
  24.7 1.7 %copy-start.9 = (f32[3,3,3]{2,1,0:T(4,128)S(1)}, f32[3,3,3]{2,1,0:T(4,128)}, u32[]{:S(2)}) copy-start(f32[3,3,3]{2,1,0:T(4,128)} %one_ref) | copy-start | bytes 328
  24.7 1.7 %copy-start.10 = (f32[3,3,3]{2,1,0:T(4,128)S(1)}, f32[3,3,3]{2,1,0:T(4,128)}, u32[]{:S(2)}) copy-start(f32[3,3,3]{2,1,0:T(4,128)} %two_ref) | copy-start | bytes 328
  97.5 21.3 %copy-start.8 = (bf16[32,128]{1,0:T(8,128)(2,1)S(1)}, bf16[32,128]{1,0:T(8,128)(2,1)}, u32[]{:S(2)}) copy-start(bf16[32,128]{1,0:T(8,128)(2,1)} %constant.37.clone.take_ref) | copy-start | bytes 24580
  118.8 8.4 %copy-start.4 = (bf16[128,128]{1,0:T(8,128)(2,1)S(1)}, bf16[128,128]{1,0:T(8,128)(2,1)}, u32[]{:S(2)}) copy-start(bf16[128,128]{1,0:T(8,128)(2,1)} %constant.38.clone.order_ref) | copy-start | bytes 98308
  118.8 11.1 %copy-start.3 = (bf16[128,128]{1,0:T(8,128)(2,1)S(1)}, bf16[128,128]{1,0:T(8,128)(2,1)}, u32[]{:S(2)}) copy-start(bf16[128,128]{1,0:T(8,128)(2,1)} %constant.39.clone.put_ref) | copy-start | bytes 98308
  119.2 10.7 %collective-permute-start.4 = (bf16[16,4224]{1,0:T(8,128)(2,1)S(1)}, bf16[16,4224]{1,0:T(8,128)(2,1)S(1)}, u32[]{:S(2)}, u32[]{:S(2)}) collective-permute-start(bf16[16,4224]{1,0:T(8,128)(2,1)S(1)} %get-tuple-element.50), channel_id=1, source_target_pairs={{0,1},{1,2},{2,3},{3,4},{4,5},{5,6},{6,7},{7,8},{8,9},{9,10},{10,1... | collective-permute-start | bytes 405512 | tf_op jit(solution)/shard_map/ppermute | solution.py:44
  122.6 7.3 %collective-permute-start.5 = (bf16[16,4224]{1,0:T(8,128)(2,1)S(1)}, bf16[16,4224]{1,0:T(8,128)(2,1)S(1)}, u32[]{:S(2)}, u32[]{:S(2)}) collective-permute-start(bf16[16,4224]{1,0:T(8,128)(2,1)S(1)} %get-tuple-element.51), channel_id=1, source_target_pairs={{1,0},{2,1},{3,2},{4,3},{5,4},{6,5},{7,6},{8,7},{9,8},{10,9},{11,1... | collective-permute-start | bytes 405512 | tf_op jit(solution)/shard_map/ppermute | solution.py:44

commit v10 on v9

--- a/solution.py
+++ b/solution.py
@@ -152,7 +152,8 @@
 
 
 def stencils_body(one_ref, two_ref, *refs):
-    indices, outs = refs[:4], refs[4:]
+    half = len(refs) // 2
+    indices, outs = refs[:half], refs[half:]
     for place, (index_ref, out_ref) in enumerate(zip(indices, outs)):
         stencil_matrix(index_ref[...], one_ref if place % 2 == 0 else two_ref, out_ref)
 
@@ -214,37 +215,47 @@
     out_ref[...] = total[:, lanes:].astype(BF16)
 
 
-def rim_body(keep_ref, first_ref, second_ref, put_ref, left_ref, right_ref, passed_ref, aligned_ref, inner_ref, out_ref, volume_ref, pass_ref, done_ref, sems):
-    lanes = LANES
-    sections = out_ref.shape[0]
-    rim, length = aligned_ref.shape
-    side = left_ref.shape[0]
-    for start in (0, rim + 2 * side):
-        volume_ref[start : start + rim] = aligned_ref[...]
-        volume_ref[start + rim : start + rim + side] = left_ref[...]
-        volume_ref[start + rim + side : start + rim + 2 * side] = right_ref[...]
+def rim_rows(which, keep_ref, first_ref, second_ref, halo_ref, passed_ref, aligned_ref, volume_ref, pass_ref):
+    sections = halo_ref.shape[0] // HALO
+    side = halo_ref.shape[0]
+    own = slice(which * side, (which + 1) * side)
+    aligned = aligned_ref[own]
+    for start in (0, 2 * side):
+        volume_ref[start : start + side] = aligned
+        volume_ref[start + side : start + 2 * side] = halo_ref[...]
     rows = first_ref.shape[0] // 3
     passed = jnp.maximum(shifted_sum(first_ref, volume_ref[...], rows), 0.0)
-    passed = [
-        inside(keep_ref, 1, passed[0:sections]),
-        inside(keep_ref, 0, passed[sections : rows - sections]),
-        inside(keep_ref, 2, passed[rows - sections :]),
-    ]
-    passed = jnp.concatenate(passed, axis=0).astype(BF16)
-    inner = passed_ref.shape[0]
-    for start in (0, inner + rows):
-        pass_ref[start : start + inner] = passed_ref[...]
-        pass_ref[start + inner : start + inner + rows] = passed
-    second = shifted_sum(second_ref, pass_ref[...], rim)
-    total = (second + aligned_ref[...].astype(F32))[:, lanes:].astype(BF16)
-    pieces = sems.shape[0]
-    width = total.shape[1] // pieces
-    copies = []
+    low = inside(keep_ref, 0 if which else 1, passed[0:sections])
+    high = inside(keep_ref, 2 if which else 0, passed[sections:])
+    passed = jnp.concatenate([low, high], axis=0).astype(BF16)
+    for start in (0, side + rows):
+        pass_ref[start : start + side] = passed_ref[own]
+        pass_ref[start + side : start + side + rows] = passed
+    second = shifted_sum(second_ref, pass_ref[...], side)
+    return (second + aligned.astype(F32))[:, LANES:].astype(BF16)
+
+
+def left_body(keep_ref, first_ref, second_ref, put_ref, halo_ref, passed_ref, aligned_ref, inner_ref, out_ref, volume_ref, pass_ref):
+    total = rim_rows(0, keep_ref, first_ref, second_ref, halo_ref, passed_ref, aligned_ref, volume_ref, pass_ref)
+    rows_out = jnp.concatenate([total, inner_ref[...]], axis=0)
+    out_ref[...] = dot(put_ref[...], rows_out).astype(BF16).reshape(out_ref.shape)
+
+
+def right_body(keep_ref, first_ref, second_ref, put_ref, halo_ref, passed_ref, aligned_ref, inner_ref, out_ref, volume_ref, pass_ref, done_ref, sems):
+    sections, cols, length = out_ref.shape
+    half = cols // 2
+    pieces = sems.shape[0] - 1
+    copies = [pltpu.make_async_copy(inner_ref.at[:, 0:half], out_ref.at[:, 0:half], sems.at[pieces])]
+    copies[0].start()
+    total = rim_rows(1, keep_ref, first_ref, second_ref, halo_ref, passed_ref, aligned_ref, volume_ref, pass_ref)
+    width = length // pieces
     for piece in range(pieces):
         where = slice(piece * width, (piece + 1) * width)
-        rows_out = jnp.concatenate([total[:, where], inner_ref[:, where]], axis=0)
-        done_ref[:, :, where] = dot(put_ref[...], rows_out).astype(BF16).reshape(sections, -1, width)
-        copies.append(pltpu.make_async_copy(done_ref.at[:, :, where], out_ref.at[:, :, where], sems.at[piece]))
+        placed = dot(put_ref[...], total[:, where]).astype(BF16).reshape(sections, half, width)
+        done_ref[:, :, where] = placed + inner_ref[:, half:, where]
+        copies.append(
+            pltpu.make_async_copy(done_ref.at[:, :, where], out_ref.at[:, half:, where], sems.at[piece])
+        )
         copies[-1].start()
     for copy in copies:
         copy.wait()
@@ -283,22 +294,20 @@
 
     last = cols - 1
     natural = pixels(*range(cols))
-    near = pixels(1, 2, last - 2, last - 1)
-    rim = pixels(0, 1, last - 1, last)
-    inner_pass = near + pixels(*range(3, last - 2))
-    rim_in = rim + pixels(-2, -1) + pixels(last + 1, last + 2)
-    rim_pass = by_column(-1, 0, last, last + 1)
+    near = pixels(1, 2), pixels(last - 2, last - 1)
+    rim = pixels(0, 1), pixels(last - 1, last)
+    beyond = pixels(-2, -1), pixels(last + 1, last + 2)
+    rim_pass = by_column(-1, 0), by_column(last, last + 1)
+    inner_pass = near[0] + near[1] + pixels(*range(3, last - 2))
     inner_out = pixels(*range(HALO, cols - HALO))
-    indices = [
-        tap_index(inner_pass, natural),
-        tap_index(inner_out, inner_pass),
-        tap_index(rim_pass, rim_in),
-        tap_index(rim, near + rim_pass),
-    ]
+    indices = [tap_index(inner_pass, natural), tap_index(inner_out, inner_pass)]
+    for which in range(2):
+        indices.append(tap_index(rim_pass[which], rim[which] + beyond[which]))
+        indices.append(tap_index(rim[which], near[which] + rim_pass[which]))
     stencils = call(
         stencils_body,
         tuple(shaped(3 * index.shape[0], 2 * index.shape[1]) for index in indices),
-        [SMEM, SMEM] + [VMEM] * 4,
+        [SMEM, SMEM] + [VMEM] * len(indices),
         "stencils",
         8,
     )(kernel_one, kernel_two, *map(jnp.asarray, indices))
@@ -328,28 +337,23 @@
         edges_body, (shaped(n_sec * HALO, length),) * 2, [VMEM, VMEM], "edges", 8
     )(data, one_hot(pixels(0, 1) + pixels(last - 1, last), natural))
     left, right = from_behind(lasts, "xy", 1), from_behind(firsts, "xy", -1)
+    side = n_sec * HALO
     inner, passed, aligned = call(
         interior_body,
-        (shaped(len(inner_out), per_sec * LANES), shaped(len(near), length), shaped(len(rim), length)),
+        (shaped(len(inner_out), per_sec * LANES), shaped(2 * side, length), shaped(2 * side, length)),
         [VMEM] * 5,
         "interior",
         32,
         [pltpu.VMEM((2 * len(natural), length), BF16), pltpu.VMEM((2 * len(inner_pass), length), BF16)],
-    )(keep, stencils[0], stencils[1], one_hot(rim + inner_out, natural), data)
-    return call(
-        rim_body,
-        out,
-        [VMEM] * 9,
-        "rim",
-        32,
-        [
-            pltpu.VMEM((2 * len(rim_in), length), BF16),
-            pltpu.VMEM((2 * (len(near) + len(rim_pass)), length), BF16),
-            pltpu.VMEM(out.shape, BF16),
-            pltpu.SemaphoreType.DMA((4,)),
-        ],
-        ANY,
-    )(keep, stencils[2], stencils[3], one_hot(natural, rim + inner_out), left, right, passed, aligned, inner)
+    )(keep, stencils[0], stencils[1], one_hot(rim[0] + rim[1] + inner_out, natural), data)
+    scratch = [pltpu.VMEM((4 * side, length), BF16)] * 2
+    placed = call(left_body, out, [VMEM] * 8, "left", 24, scratch)(
+        keep, stencils[2], stencils[3], one_hot(natural, rim[0] + inner_out), left, passed, aligned, inner
+    )
+    scratch = scratch + [pltpu.VMEM((n_sec, cols // 2, per_sec * LANES), BF16), pltpu.SemaphoreType.DMA((5,))]
+    return call(right_body, out, [VMEM] * 8, "right", 24, scratch, ANY)(
+        keep, stencils[4], stencils[5], one_hot(pixels(*range(cols // 2, cols)), rim[1]), right, passed, aligned, placed
+    )
 
 
 def solution(mesh):

time: 132 us -> 132 us (level)
    pallas_call x2 -> x3, Pallas kernels: 4.7 us -> 5.36 us  [the longest x1 2.77 us: body(): call(interior_body, (shaped(len(inner_out), per_sec * LANES), shaped(2 *...]
where the time goes in v10:
time: 132 us; the launch traced here: 131 us
  blocking collectives  83.4 us (63%)
  starting transfers between devices  29.7 us (22%)
  Pallas kernels  10.9 us (8%)
  waiting for transfers between devices  5.49 us (4%)
    all_to_all x1, blocking collectives, body(): mine = lax.all_to_all(strip, 'xy', split_axis=0, concat_axis=0, tiled=True)  62.9 us
    ppermute x6, starting transfers between devices, from_behind(): return lax.ppermute(value, axis, shift_pairs(lax.axis_size(axis), steps))  29.7 us
    all_to_all x1, blocking collectives, body(): lax.all_to_all(spread, 'sec', split_axis=0, concat_axis=0, tiled=True)  20.5 us
    ppermute x6, waiting for transfers between devices, from_behind(): return lax.ppermute(value, axis, shift_pairs(lax.axis_size(axis), steps))  5.49 us
    pallas_call x1, Pallas kernels, body(): call(interior_body, (shaped(len(inner_out), per_sec * LANES), shaped(2 *...  2.77 us
  transfers between devices with their start and end apart: 6, of which 3 were waited for; matrix products, arithmetic and copies ran while one was open for 0% of the time, Pallas kernels for 6%

profile of v10, /device:TPU:24, one launch (start us, length us, event | category | flops | bytes accessed | tf_op | source)
XLA Modules:
  0.0 131.3 jit_solution(16681725192387519416)
XLA Ops:
  0.0 3.8 %collective-permute-start.1 = (s32[1,2,2]{2,1,0:T(2,128)}, s32[1,2,2]{2,1,0:T(2,128)S(1)}, u32[]{:S(2)}, u32[]{:S(2)}) collective-permute-start(s32[1,2,2]{2,1,0:T(2,128)} %refs_0_.4), channel_id=1, source_target_pairs={{0,1},{1,2},{2,3},{3,4},{4,5},{5,6},{6,7},{7,8},{8,9},{9,10},{10,1... | collective-permute-start | bytes 56 | tf_op jit(solution)/shard_map/ppermute | solution.py:44
  3.8 9.7 %collective-permute-start = (s32[1,2,2]{2,1,0:T(2,128)}, s32[1,2,2]{2,1,0:T(2,128)S(1)}, u32[]{:S(2)}, u32[]{:S(2)}) collective-permute-start(s32[1,2,2]{2,1,0:T(2,128)} %refs_0_.4), channel_id=1, source_target_pairs={{1,0},{2,1},{3,2},{4,3},{5,4},{6,5},{7,6},{8,7},{9,8},{10,9},{11,1... | collective-permute-start | bytes 56 | tf_op jit(solution)/shard_map/ppermute | solution.py:44
  13.6 0.0 copy-start
  13.6 1.2 copy-done
  14.8 0.1 stage.1.source_ref
  14.9 0.0 copy-start.14
  14.9 0.0 collective-permute-done.1.above_ref
  14.9 0.1 collective-permute-done.below_ref
  15.0 0.3 choose.1
  15.3 1.9 %collective-permute-start.2 = (bf16[1,512,512]{2,1,0:T(8,128)(2,1)S(1)}, bf16[1,512,512]{2,1,0:T(8,128)(2,1)S(1)}, u32[]{:S(2)}, u32[]{:S(2)}) collective-permute-start(bf16[1,512,512]{2,1,0:T(8,128)(2,1)S(1)} %get-tuple-element.49), channel_id=1, source_target_pairs={{0,1},{1,2},{2,3},{3,4},{4,5},{5,6},{6,7},{7,8},{8,9},{9,10},{10,1... | collective-permute-start | bytes 1572872 | tf_op jit(solution)/shard_map/ppermute | solution.py:44
  17.3 6.3 %collective-permute-start.3 = (bf16[1,512,512]{2,1,0:T(8,128)(2,1)S(1)}, bf16[1,512,512]{2,1,0:T(8,128)(2,1)S(1)}, u32[]{:S(2)}, u32[]{:S(2)}) collective-permute-start(bf16[1,512,512]{2,1,0:T(8,128)(2,1)S(1)} %get-tuple-element.53), channel_id=1, source_target_pairs={{1,0},{2,1},{3,2},{4,3},{5,4},{6,5},{7,6},{8,7},{9,8},{10,9},{11,1... | collective-permute-start | bytes 1572872 | tf_op jit(solution)/shard_map/ppermute | solution.py:44
  23.6 0.0 copy-start.6
  23.6 0.1 add_convert_fusion.keep_ref
  23.6 0.0 copy-done.14
  23.7 1.0 matrices.1.matrix_ref.refs_2_
  24.6 0.0 copy-done.6
  24.6 0.0 copy-start.1
  24.7 0.0 copy-start.2
  24.7 0.0 copy-start.8
  24.7 0.0 copy-start.9
  24.7 0.0 copy-start.10
  24.7 0.0 copy-start.11
  24.7 0.0 copy-start.12
  24.7 0.0 copy-start.13
  24.8 1.6 %warp.1.refs_3_ = bf16[64,4,16,128]{3,2,1,0:T(8,128)(2,1)S(1)} custom-call(s32[1,2,2]{2,1,0:T(2,128)S(1)} %copy-done.6, bf16[1,512,1024]{2,1,0:T(8,128)(2,1)S(1)} %stage.1.source_ref, bf16[2,2,512,512]{3,2,1,0:T(8,128)(2,1)S(1)} %matrices.1.matrix_ref.refs_2_), custom_call_target="tpu_custom_call" | custom-call | tf_op jit(solution)/shard_map/warp/pallas_call | solution.py:323
  26.3 0.0 copy-done.1
  26.4 0.0 copy-done.2
  26.4 0.0 copy-done.8
  26.4 0.0 copy-done.9
  26.4 0.0 copy-done.10
  26.4 0.0 copy-done.11
  26.4 0.0 copy-done.12
  26.4 0.0 copy-done.13
  26.4 1.0 stencils.1
  27.5 5.2 %collective-permute-done.2.refs_1_ = bf16[1,512,512]{2,1,0:T(8,128)(2,1)S(1)} collective-permute-done((bf16[1,512,512]{2,1,0:T(8,128)(2,1)S(1)}, bf16[1,512,512]{2,1,0:T(8,128)(2,1)S(1)}, u32[]{:S(2)}, u32[]{:S(2)}) %collective-permute-start.2) | collective-permute-done | bytes 524320 | tf_op jit(solution)/shard_map/ppermute | solution.py:44
  32.6 1.0 warp_above.1.refs_3_
  33.6 0.2 collective-permute-done.3.refs_1_
  33.8 0.1 warp_below.1
  34.0 62.9 %all_to_all.10 = bf16[64,4,16,128]{3,2,1,0:T(8,128)(2,1)S(1)} all-to-all(bf16[64,4,16,128]{3,2,1,0:T(8,128)(2,1)S(1)} %warp_below.1), channel_id=1, replica_groups=mesh['sec'=8,'xy'=64] {'xy'}, dimensions={0} | all-to-all | bytes 2097152 | tf_op jit(solution)/shard_map/all_to_all | solution.py:329
  96.8 0.1 spread.1
  96.9 0.0 copy-start.7
  96.9 20.5 %all_to_all.11.data_ref = bf16[8,33,16,128]{3,2,1,0:T(8,128)(2,1)S(1)} all-to-all(bf16[8,33,16,128]{3,2,1,0:T(8,128)(2,1)S(1)} %spread.1), channel_id=1, replica_groups=mesh['sec'=8,'xy'=64] {'sec'}, dimensions={0} | all-to-all | bytes 2162688 | tf_op jit(solution)/shard_map/all_to_all | solution.py:333
  117.5 0.0 copy-done.7
  117.5 0.0 copy-start.4
  117.5 0.0 copy-start.3
  117.5 0.4 edges.1
  117.9 4.7 %collective-permute-start.5 = (bf16[16,4224]{1,0:T(8,128)(2,1)S(1)}, bf16[16,4224]{1,0:T(8,128)(2,1)S(1)}, u32[]{:S(2)}, u32[]{:S(2)}) collective-permute-start(bf16[16,4224]{1,0:T(8,128)(2,1)S(1)} %get-tuple-element.63), channel_id=1, source_target_pairs={{0,1},{1,2},{2,3},{3,4},{4,5},{5,6},{6,7},{7,8},{8,9},{9,10},{10,1... | collective-permute-start | bytes 405512 | tf_op jit(solution)/shard_map/ppermute | solution.py:44
  122.6 3.3 %collective-permute-start.4 = (bf16[16,4224]{1,0:T(8,128)(2,1)S(1)}, bf16[16,4224]{1,0:T(8,128)(2,1)S(1)}, u32[]{:S(2)}, u32[]{:S(2)}) collective-permute-start(bf16[16,4224]{1,0:T(8,128)(2,1)S(1)} %get-tuple-element.56), channel_id=1, source_target_pairs={{1,0},{2,1},{3,2},{4,3},{5,4},{6,5},{7,6},{8,7},{9,8},{10,9},{11,1... | collective-permute-start | bytes 405512 | tf_op jit(solution)/shard_map/ppermute | solution.py:44
  125.9 0.0 copy-done.4
  125.9 2.8 %interior.1 = (bf16[96,4096]{1,0:T(8,128)(2,1)S(1)}, bf16[32,4224]{1,0:T(8,128)(2,1)S(1)}, bf16[32,4224]{1,0:T(8,128)(2,1)S(1)}) custom-call(f32[3,4224]{1,0:T(4,128)S(1)} %add_convert_fusion.keep_ref, bf16[336,256]{1,0:T(8,128)(2,1)S(1)} %get-tuple-element.57.first_ref, bf16[288,224]{1,0:T(8,128)(2,1)S(1)} %get-tuple-element.58.second_ref, ...), custom_call_target="tpu_custom_call" | custom-call | tf_op jit(solution)/shard_map/interior/pallas_call | solution.py:341
  128.6 0.0 collective-permute-done.5.halo_ref
  128.7 0.0 copy-done.3
  128.7 0.0 copy-start.5
  128.7 1.0 left.1.inner_ref
  129.7 0.0 collective-permute-done.4.halo_ref
  129.7 0.0 copy-done.5
  129.7 1.6 %right.1 = bf16[8,16,4096]{2,1,0:T(8,128)(2,1)} custom-call(f32[3,4224]{1,0:T(4,128)S(1)} %add_convert_fusion.keep_ref, bf16[48,64]{1,0:T(8,128)(2,1)S(1)} %get-tuple-element.51.first_ref, bf16[48,64]{1,0:T(8,128)(2,1)S(1)} %get-tuple-element.52.second_ref, bf16[64,16]{1,0:T(8,128)(2,1)S(1)} %copy-done.5, ...), custom_call_target="tpu_custom_call" | custom-call | tf_op jit(solution)/shard_map/right/pallas_call | solution.py:354
  (2 shorter events, 0.0 us)
Async XLA Ops:
  0.0 14.9 %collective-permute-start.1 = (s32[1,2,2]{2,1,0:T(2,128)}, s32[1,2,2]{2,1,0:T(2,128)S(1)}, u32[]{:S(2)}, u32[]{:S(2)}) collective-permute-start(s32[1,2,2]{2,1,0:T(2,128)} %refs_0_.4), channel_id=1, source_target_pairs={{0,1},{1,2},{2,3},{3,4},{4,5},{5,6},{6,7},{7,8},{8,9},{9,10},{10,1... | collective-permute-start | bytes 56 | tf_op jit(solution)/shard_map/ppermute | solution.py:44
  3.8 11.2 %collective-permute-start = (s32[1,2,2]{2,1,0:T(2,128)}, s32[1,2,2]{2,1,0:T(2,128)S(1)}, u32[]{:S(2)}, u32[]{:S(2)}) collective-permute-start(s32[1,2,2]{2,1,0:T(2,128)} %refs_0_.4), channel_id=1, source_target_pairs={{1,0},{2,1},{3,2},{4,3},{5,4},{6,5},{7,6},{8,7},{9,8},{10,9},{11,1... | collective-permute-start | bytes 56 | tf_op jit(solution)/shard_map/ppermute | solution.py:44
  13.6 1.2 copy-start
  14.9 8.8 %copy-start.14 = (f32[1,2,2]{2,1,0:T(2,128)S(1)}, f32[1,2,2]{2,1,0:T(2,128)}, u32[]{:S(2)}) copy-start(f32[1,2,2]{2,1,0:T(2,128)} %fraction_ref) | copy-start | bytes 52
  15.3 17.3 %collective-permute-start.2 = (bf16[1,512,512]{2,1,0:T(8,128)(2,1)S(1)}, bf16[1,512,512]{2,1,0:T(8,128)(2,1)S(1)}, u32[]{:S(2)}, u32[]{:S(2)}) collective-permute-start(bf16[1,512,512]{2,1,0:T(8,128)(2,1)S(1)} %get-tuple-element.49), channel_id=1, source_target_pairs={{0,1},{1,2},{2,3},{3,4},{4,5},{5,6},{6,7},{7,8},{8,9},{9,10},{10,1... | collective-permute-start | bytes 1572872 | tf_op jit(solution)/shard_map/ppermute | solution.py:44
  17.3 16.6 %collective-permute-start.3 = (bf16[1,512,512]{2,1,0:T(8,128)(2,1)S(1)}, bf16[1,512,512]{2,1,0:T(8,128)(2,1)S(1)}, u32[]{:S(2)}, u32[]{:S(2)}) collective-permute-start(bf16[1,512,512]{2,1,0:T(8,128)(2,1)S(1)} %get-tuple-element.53), channel_id=1, source_target_pairs={{1,0},{2,1},{3,2},{4,3},{5,4},{6,5},{7,6},{8,7},{9,8},{10,9},{11,1... | collective-permute-start | bytes 1572872 | tf_op jit(solution)/shard_map/ppermute | solution.py:44
  23.6 1.1 copy-start.6
  24.6 1.7 %copy-start.1 = (s32[112,128]{1,0:T(8,128)S(1)}, s32[112,128]{1,0:T(8,128)}, u32[]{:S(2)}) copy-start(s32[112,128]{1,0:T(8,128)} %constant.39.clone.refs_0_) | copy-start | bytes 172036
  24.7 1.7 %copy-start.2 = (s32[96,112]{1,0:T(8,128)S(1)}, s32[96,112]{1,0:T(8,128)}, u32[]{:S(2)}) copy-start(s32[96,112]{1,0:T(8,128)} %constant.40.clone.refs_1_) | copy-start | bytes 129028
  24.7 1.7 %copy-start.8 = (s32[16,32]{1,0:T(8,128)S(1)}, s32[16,32]{1,0:T(8,128)}, u32[]{:S(2)}) copy-start(s32[16,32]{1,0:T(8,128)} %constant.44.clone.refs_5_) | copy-start | bytes 6148
  24.7 1.7 %copy-start.9 = (s32[16,32]{1,0:T(8,128)S(1)}, s32[16,32]{1,0:T(8,128)}, u32[]{:S(2)}) copy-start(s32[16,32]{1,0:T(8,128)} %constant.43.clone.refs_4_) | copy-start | bytes 6148
  24.7 1.7 %copy-start.10 = (s32[16,32]{1,0:T(8,128)S(1)}, s32[16,32]{1,0:T(8,128)}, u32[]{:S(2)}) copy-start(s32[16,32]{1,0:T(8,128)} %constant.42.clone.refs_3_) | copy-start | bytes 6148
  24.7 1.7 %copy-start.11 = (s32[16,32]{1,0:T(8,128)S(1)}, s32[16,32]{1,0:T(8,128)}, u32[]{:S(2)}) copy-start(s32[16,32]{1,0:T(8,128)} %constant.41.clone.refs_2_) | copy-start | bytes 6148
  24.7 1.7 %copy-start.12 = (f32[3,3,3]{2,1,0:T(4,128)S(1)}, f32[3,3,3]{2,1,0:T(4,128)}, u32[]{:S(2)}) copy-start(f32[3,3,3]{2,1,0:T(4,128)} %one_ref) | copy-start | bytes 328
  24.7 1.7 %copy-start.13 = (f32[3,3,3]{2,1,0:T(4,128)S(1)}, f32[3,3,3]{2,1,0:T(4,128)}, u32[]{:S(2)}) copy-start(f32[3,3,3]{2,1,0:T(4,128)} %two_ref) | copy-start | bytes 328
  96.9 20.6 %copy-start.7 = (bf16[32,128]{1,0:T(8,128)(2,1)S(1)}, bf16[32,128]{1,0:T(8,128)(2,1)}, u32[]{:S(2)}) copy-start(bf16[32,128]{1,0:T(8,128)(2,1)} %constant.45.clone.take_ref) | copy-start | bytes 24580
  117.5 8.4 %copy-start.4 = (bf16[128,128]{1,0:T(8,128)(2,1)S(1)}, bf16[128,128]{1,0:T(8,128)(2,1)}, u32[]{:S(2)}) copy-start(bf16[128,128]{1,0:T(8,128)(2,1)} %constant.46.clone.order_ref) | copy-start | bytes 98308
  117.5 11.2 %copy-start.3 = (bf16[128,112]{1,0:T(8,128)(2,1)S(1)}, bf16[128,112]{1,0:T(8,128)(2,1)}, u32[]{:S(2)}) copy-start(bf16[128,112]{1,0:T(8,128)(2,1)} %constant.47.clone.put_ref) | copy-start | bytes 86020
  117.9 10.8 %collective-permute-start.5 = (bf16[16,4224]{1,0:T(8,128)(2,1)S(1)}, bf16[16,4224]{1,0:T(8,128)(2,1)S(1)}, u32[]{:S(2)}, u32[]{:S(2)}) collective-permute-start(bf16[16,4224]{1,0:T(8,128)(2,1)S(1)} %get-tuple-element.63), channel_id=1, source_target_pairs={{0,1},{1,2},{2,3},{3,4},{4,5},{5,6},{6,7},{7,8},{8,9},{9,10},{10,1... | collective-permute-start | bytes 405512 | tf_op jit(solution)/shard_map/ppermute | solution.py:44
  122.6 7.1 %collective-permute-start.4 = (bf16[16,4224]{1,0:T(8,128)(2,1)S(1)}, bf16[16,4224]{1,0:T(8,128)(2,1)S(1)}, u32[]{:S(2)}, u32[]{:S(2)}) collective-permute-start(bf16[16,4224]{1,0:T(8,128)(2,1)S(1)} %get-tuple-element.56), channel_id=1, source_target_pairs={{1,0},{2,1},{3,2},{4,3},{5,4},{6,5},{7,6},{8,7},{9,8},{10,9},{11,1... | collective-permute-start | bytes 405512 | tf_op jit(solution)/shard_map/ppermute | solution.py:44
  128.7 1.0 copy-start.5

commit v11 on v10

--- a/solution.py
+++ b/solution.py
@@ -237,22 +237,22 @@
 
 def left_body(keep_ref, first_ref, second_ref, put_ref, halo_ref, passed_ref, aligned_ref, inner_ref, out_ref, volume_ref, pass_ref):
     total = rim_rows(0, keep_ref, first_ref, second_ref, halo_ref, passed_ref, aligned_ref, volume_ref, pass_ref)
-    rows_out = jnp.concatenate([total, inner_ref[...]], axis=0)
+    rows_out = jnp.concatenate([total, inner_ref[0 : inner_ref.shape[0] // 2]], axis=0)
     out_ref[...] = dot(put_ref[...], rows_out).astype(BF16).reshape(out_ref.shape)
 
 
-def right_body(keep_ref, first_ref, second_ref, put_ref, halo_ref, passed_ref, aligned_ref, inner_ref, out_ref, volume_ref, pass_ref, done_ref, sems):
+def right_body(keep_ref, first_ref, second_ref, put_ref, halo_ref, passed_ref, aligned_ref, inner_ref, lower_ref, out_ref, volume_ref, pass_ref, done_ref, sems):
     sections, cols, length = out_ref.shape
     half = cols // 2
     pieces = sems.shape[0] - 1
-    copies = [pltpu.make_async_copy(inner_ref.at[:, 0:half], out_ref.at[:, 0:half], sems.at[pieces])]
+    copies = [pltpu.make_async_copy(lower_ref, out_ref.at[:, 0:half], sems.at[pieces])]
     copies[0].start()
     total = rim_rows(1, keep_ref, first_ref, second_ref, halo_ref, passed_ref, aligned_ref, volume_ref, pass_ref)
     width = length // pieces
     for piece in range(pieces):
         where = slice(piece * width, (piece + 1) * width)
-        placed = dot(put_ref[...], total[:, where]).astype(BF16).reshape(sections, half, width)
-        done_ref[:, :, where] = placed + inner_ref[:, half:, where]
+        rows_out = jnp.concatenate([total[:, where], inner_ref[inner_ref.shape[0] // 2 :, where]], axis=0)
+        done_ref[:, :, where] = dot(put_ref[...], rows_out).astype(BF16).reshape(sections, half, width)
         copies.append(
             pltpu.make_async_copy(done_ref.at[:, :, where], out_ref.at[:, half:, where], sems.at[piece])
         )
@@ -299,7 +299,7 @@
     beyond = pixels(-2, -1), pixels(last + 1, last + 2)
     rim_pass = by_column(-1, 0), by_column(last, last + 1)
     inner_pass = near[0] + near[1] + pixels(*range(3, last - 2))
-    inner_out = pixels(*range(HALO, cols - HALO))
+    inner_out = pixels(*range(HALO, cols // 2)) + pixels(*range(cols // 2, cols - HALO))
     indices = [tap_index(inner_pass, natural), tap_index(inner_out, inner_pass)]
     for which in range(2):
         indices.append(tap_index(rim_pass[which], rim[which] + beyond[which]))
@@ -347,12 +347,15 @@
         [pltpu.VMEM((2 * len(natural), length), BF16), pltpu.VMEM((2 * len(inner_pass), length), BF16)],
     )(keep, stencils[0], stencils[1], one_hot(rim[0] + rim[1] + inner_out, natural), data)
     scratch = [pltpu.VMEM((4 * side, length), BF16)] * 2
-    placed = call(left_body, out, [VMEM] * 8, "left", 24, scratch)(
-        keep, stencils[2], stencils[3], one_hot(natural, rim[0] + inner_out), left, passed, aligned, inner
-    )
-    scratch = scratch + [pltpu.VMEM((n_sec, cols // 2, per_sec * LANES), BF16), pltpu.SemaphoreType.DMA((5,))]
-    return call(right_body, out, [VMEM] * 8, "right", 24, scratch, ANY)(
-        keep, stencils[4], stencils[5], one_hot(pixels(*range(cols // 2, cols)), rim[1]), right, passed, aligned, placed
+    lower, upper = pixels(*range(cols // 2)), pixels(*range(cols // 2, cols))
+    middle = len(inner_out) // 2
+    part = shaped(n_sec, cols // 2, per_sec * LANES)
+    done = call(left_body, part, [VMEM] * 8, "left", 24, scratch)(
+        keep, stencils[2], stencils[3], one_hot(lower, rim[0] + inner_out[:middle]), left, passed, aligned, inner
+    )
+    scratch = scratch + [pltpu.VMEM(part.shape, BF16), pltpu.SemaphoreType.DMA((5,))]
+    return call(right_body, out, [VMEM] * 9, "right", 24, scratch, ANY)(
+        keep, stencils[4], stencils[5], one_hot(upper, rim[1] + inner_out[middle:]), right, passed, aligned, inner, done
     )
 
 

time: 132 us -> 133 us (level)
  no operation moved by 1% of the time
where the time goes in v11:
time: 133 us; the launch traced here: 132 us
  blocking collectives  83.5 us (63%)
  starting transfers between devices  29.7 us (22%)
  Pallas kernels  10.8 us (8%)
  waiting for transfers between devices  6.32 us (5%)
    all_to_all x1, blocking collectives, body(): mine = lax.all_to_all(strip, 'xy', split_axis=0, concat_axis=0, tiled=True)  62.6 us
    ppermute x6, starting transfers between devices, from_behind(): return lax.ppermute(value, axis, shift_pairs(lax.axis_size(axis), steps))  29.7 us
    all_to_all x1, blocking collectives, body(): lax.all_to_all(spread, 'sec', split_axis=0, concat_axis=0, tiled=True)  20.9 us
    ppermute x6, waiting for transfers between devices, from_behind(): return lax.ppermute(value, axis, shift_pairs(lax.axis_size(axis), steps))  6.32 us
    pallas_call x1, Pallas kernels, body(): call(interior_body, (shaped(len(inner_out), per_sec * LANES), shaped(2 *...  2.78 us
  transfers between devices with their start and end apart: 6, of which 3 were waited for; matrix products, arithmetic and copies ran while one was open for 0% of the time, Pallas kernels for 6%

profile of v11, /device:TPU:24, one launch (start us, length us, event | category | flops | bytes accessed | tf_op | source)
XLA Modules:
  0.0 132.1 jit_solution(8417269235677787996)
XLA Ops:
  0.0 3.8 %collective-permute-start.1 = (s32[1,2,2]{2,1,0:T(2,128)}, s32[1,2,2]{2,1,0:T(2,128)S(1)}, u32[]{:S(2)}, u32[]{:S(2)}) collective-permute-start(s32[1,2,2]{2,1,0:T(2,128)} %refs_0_.4), channel_id=1, source_target_pairs={{0,1},{1,2},{2,3},{3,4},{4,5},{5,6},{6,7},{7,8},{8,9},{9,10},{10,1... | collective-permute-start | bytes 56 | tf_op jit(solution)/shard_map/ppermute | solution.py:44
  3.8 9.7 %collective-permute-start = (s32[1,2,2]{2,1,0:T(2,128)}, s32[1,2,2]{2,1,0:T(2,128)S(1)}, u32[]{:S(2)}, u32[]{:S(2)}) collective-permute-start(s32[1,2,2]{2,1,0:T(2,128)} %refs_0_.4), channel_id=1, source_target_pairs={{1,0},{2,1},{3,2},{4,3},{5,4},{6,5},{7,6},{8,7},{9,8},{10,9},{11,1... | collective-permute-start | bytes 56 | tf_op jit(solution)/shard_map/ppermute | solution.py:44
  13.6 0.0 copy-start
  13.6 1.2 copy-done
  14.8 0.1 stage.1.source_ref
  14.9 0.0 copy-start.14
  14.9 0.0 collective-permute-done.1.above_ref
  14.9 0.1 collective-permute-done.below_ref
  15.0 0.3 choose.1
  15.3 1.9 %collective-permute-start.2 = (bf16[1,512,512]{2,1,0:T(8,128)(2,1)S(1)}, bf16[1,512,512]{2,1,0:T(8,128)(2,1)S(1)}, u32[]{:S(2)}, u32[]{:S(2)}) collective-permute-start(bf16[1,512,512]{2,1,0:T(8,128)(2,1)S(1)} %get-tuple-element.49), channel_id=1, source_target_pairs={{0,1},{1,2},{2,3},{3,4},{4,5},{5,6},{6,7},{7,8},{8,9},{9,10},{10,1... | collective-permute-start | bytes 1572872 | tf_op jit(solution)/shard_map/ppermute | solution.py:44
  17.3 6.3 %collective-permute-start.3 = (bf16[1,512,512]{2,1,0:T(8,128)(2,1)S(1)}, bf16[1,512,512]{2,1,0:T(8,128)(2,1)S(1)}, u32[]{:S(2)}, u32[]{:S(2)}) collective-permute-start(bf16[1,512,512]{2,1,0:T(8,128)(2,1)S(1)} %get-tuple-element.53), channel_id=1, source_target_pairs={{1,0},{2,1},{3,2},{4,3},{5,4},{6,5},{7,6},{8,7},{9,8},{10,9},{11,1... | collective-permute-start | bytes 1572872 | tf_op jit(solution)/shard_map/ppermute | solution.py:44
  23.6 0.0 copy-start.6
  23.6 0.1 add_convert_fusion.keep_ref
  23.6 0.0 copy-done.14
  23.7 1.0 matrices.1.matrix_ref.refs_2_
  24.6 0.0 copy-done.6
  24.6 0.0 copy-start.1
  24.7 0.0 copy-start.2
  24.7 0.0 copy-start.8
  24.7 0.0 copy-start.9
  24.7 0.0 copy-start.10
  24.7 0.0 copy-start.11
  24.7 0.0 copy-start.12
  24.7 0.0 copy-start.13
  24.8 1.6 %warp.1.refs_3_ = bf16[64,4,16,128]{3,2,1,0:T(8,128)(2,1)S(1)} custom-call(s32[1,2,2]{2,1,0:T(2,128)S(1)} %copy-done.6, bf16[1,512,1024]{2,1,0:T(8,128)(2,1)S(1)} %stage.1.source_ref, bf16[2,2,512,512]{3,2,1,0:T(8,128)(2,1)S(1)} %matrices.1.matrix_ref.refs_2_), custom_call_target="tpu_custom_call" | custom-call | tf_op jit(solution)/shard_map/warp/pallas_call | solution.py:323
  26.3 0.0 copy-done.1
  26.4 0.0 copy-done.2
  26.4 0.0 copy-done.8
  26.4 0.0 copy-done.9
  26.4 0.0 copy-done.10
  26.4 0.0 copy-done.11
  26.4 0.0 copy-done.12
  26.4 0.0 copy-done.13
  26.4 1.0 stencils.1
  27.5 5.2 %collective-permute-done.2.refs_1_ = bf16[1,512,512]{2,1,0:T(8,128)(2,1)S(1)} collective-permute-done((bf16[1,512,512]{2,1,0:T(8,128)(2,1)S(1)}, bf16[1,512,512]{2,1,0:T(8,128)(2,1)S(1)}, u32[]{:S(2)}, u32[]{:S(2)}) %collective-permute-start.2) | collective-permute-done | bytes 524320 | tf_op jit(solution)/shard_map/ppermute | solution.py:44
  32.6 0.1 warp_above.1.refs_3_
  32.8 1.0 collective-permute-done.3.refs_1_
  33.8 1.0 warp_below.1
  34.8 62.6 %all_to_all.10 = bf16[64,4,16,128]{3,2,1,0:T(8,128)(2,1)S(1)} all-to-all(bf16[64,4,16,128]{3,2,1,0:T(8,128)(2,1)S(1)} %warp_below.1), channel_id=1, replica_groups=mesh['sec'=8,'xy'=64] {'xy'}, dimensions={0} | all-to-all | bytes 2097152 | tf_op jit(solution)/shard_map/all_to_all | solution.py:329
  97.4 0.1 spread.1
  97.5 0.0 copy-start.7
  97.5 20.9 %all_to_all.11.data_ref = bf16[8,33,16,128]{3,2,1,0:T(8,128)(2,1)S(1)} all-to-all(bf16[8,33,16,128]{3,2,1,0:T(8,128)(2,1)S(1)} %spread.1), channel_id=1, replica_groups=mesh['sec'=8,'xy'=64] {'sec'}, dimensions={0} | all-to-all | bytes 2162688 | tf_op jit(solution)/shard_map/all_to_all | solution.py:333
  118.4 0.0 copy-done.7
  118.4 0.0 copy-start.3
  118.4 0.0 copy-start.5
  118.4 0.4 edges.1
  118.8 3.6 %collective-permute-start.5 = (bf16[16,4224]{1,0:T(8,128)(2,1)S(1)}, bf16[16,4224]{1,0:T(8,128)(2,1)S(1)}, u32[]{:S(2)}, u32[]{:S(2)}) collective-permute-start(bf16[16,4224]{1,0:T(8,128)(2,1)S(1)} %get-tuple-element.64), channel_id=1, source_target_pairs={{0,1},{1,2},{2,3},{3,4},{4,5},{5,6},{6,7},{7,8},{8,9},{9,10},{10,1... | collective-permute-start | bytes 405512 | tf_op jit(solution)/shard_map/ppermute | solution.py:44
  122.4 4.4 %collective-permute-start.4 = (bf16[16,4224]{1,0:T(8,128)(2,1)S(1)}, bf16[16,4224]{1,0:T(8,128)(2,1)S(1)}, u32[]{:S(2)}, u32[]{:S(2)}) collective-permute-start(bf16[16,4224]{1,0:T(8,128)(2,1)S(1)} %get-tuple-element.56), channel_id=1, source_target_pairs={{1,0},{2,1},{3,2},{4,3},{5,4},{6,5},{7,6},{8,7},{9,8},{10,9},{11,1... | collective-permute-start | bytes 405512 | tf_op jit(solution)/shard_map/ppermute | solution.py:44
  126.8 0.0 copy-done.3
  126.8 2.8 %interior.1 = (bf16[96,4096]{1,0:T(8,128)(2,1)S(1)}, bf16[32,4224]{1,0:T(8,128)(2,1)S(1)}, bf16[32,4224]{1,0:T(8,128)(2,1)S(1)}) custom-call(f32[3,4224]{1,0:T(4,128)S(1)} %add_convert_fusion.keep_ref, bf16[336,256]{1,0:T(8,128)(2,1)S(1)} %get-tuple-element.57.first_ref, bf16[288,224]{1,0:T(8,128)(2,1)S(1)} %get-tuple-element.58.second_ref, ...), custom_call_target="tpu_custom_call" | custom-call | tf_op jit(solution)/shard_map/interior/pallas_call | solution.py:341
  129.6 0.0 copy-start.4
  129.6 0.0 collective-permute-done.5.halo_ref
  129.6 0.0 copy-done.5
  129.6 0.9 left.1.lower_ref
  130.5 0.0 collective-permute-done.4.halo_ref
  130.5 0.0 copy-done.4
  130.5 1.6 %right.1 = bf16[8,16,4096]{2,1,0:T(8,128)(2,1)} custom-call(f32[3,4224]{1,0:T(4,128)S(1)} %add_convert_fusion.keep_ref, bf16[48,64]{1,0:T(8,128)(2,1)S(1)} %get-tuple-element.51.first_ref, bf16[48,64]{1,0:T(8,128)(2,1)S(1)} %get-tuple-element.52.second_ref, bf16[64,64]{1,0:T(8,128)(2,1)S(1)} %copy-done.4, ...), custom_call_target="tpu_custom_call" | custom-call | tf_op jit(solution)/shard_map/right/pallas_call | solution.py:357
  (2 shorter events, 0.0 us)
Async XLA Ops:
  0.0 14.9 %collective-permute-start.1 = (s32[1,2,2]{2,1,0:T(2,128)}, s32[1,2,2]{2,1,0:T(2,128)S(1)}, u32[]{:S(2)}, u32[]{:S(2)}) collective-permute-start(s32[1,2,2]{2,1,0:T(2,128)} %refs_0_.4), channel_id=1, source_target_pairs={{0,1},{1,2},{2,3},{3,4},{4,5},{5,6},{6,7},{7,8},{8,9},{9,10},{10,1... | collective-permute-start | bytes 56 | tf_op jit(solution)/shard_map/ppermute | solution.py:44
  3.8 11.2 %collective-permute-start = (s32[1,2,2]{2,1,0:T(2,128)}, s32[1,2,2]{2,1,0:T(2,128)S(1)}, u32[]{:S(2)}, u32[]{:S(2)}) collective-permute-start(s32[1,2,2]{2,1,0:T(2,128)} %refs_0_.4), channel_id=1, source_target_pairs={{1,0},{2,1},{3,2},{4,3},{5,4},{6,5},{7,6},{8,7},{9,8},{10,9},{11,1... | collective-permute-start | bytes 56 | tf_op jit(solution)/shard_map/ppermute | solution.py:44
  13.6 1.2 copy-start
  14.9 8.8 %copy-start.14 = (f32[1,2,2]{2,1,0:T(2,128)S(1)}, f32[1,2,2]{2,1,0:T(2,128)}, u32[]{:S(2)}) copy-start(f32[1,2,2]{2,1,0:T(2,128)} %fraction_ref) | copy-start | bytes 52
  15.3 17.3 %collective-permute-start.2 = (bf16[1,512,512]{2,1,0:T(8,128)(2,1)S(1)}, bf16[1,512,512]{2,1,0:T(8,128)(2,1)S(1)}, u32[]{:S(2)}, u32[]{:S(2)}) collective-permute-start(bf16[1,512,512]{2,1,0:T(8,128)(2,1)S(1)} %get-tuple-element.49), channel_id=1, source_target_pairs={{0,1},{1,2},{2,3},{3,4},{4,5},{5,6},{6,7},{7,8},{8,9},{9,10},{10,1... | collective-permute-start | bytes 1572872 | tf_op jit(solution)/shard_map/ppermute | solution.py:44
  17.3 16.6 %collective-permute-start.3 = (bf16[1,512,512]{2,1,0:T(8,128)(2,1)S(1)}, bf16[1,512,512]{2,1,0:T(8,128)(2,1)S(1)}, u32[]{:S(2)}, u32[]{:S(2)}) collective-permute-start(bf16[1,512,512]{2,1,0:T(8,128)(2,1)S(1)} %get-tuple-element.53), channel_id=1, source_target_pairs={{1,0},{2,1},{3,2},{4,3},{5,4},{6,5},{7,6},{8,7},{9,8},{10,9},{11,1... | collective-permute-start | bytes 1572872 | tf_op jit(solution)/shard_map/ppermute | solution.py:44
  23.6 1.1 copy-start.6
  24.6 1.7 %copy-start.1 = (s32[112,128]{1,0:T(8,128)S(1)}, s32[112,128]{1,0:T(8,128)}, u32[]{:S(2)}) copy-start(s32[112,128]{1,0:T(8,128)} %constant.39.clone.refs_0_) | copy-start | bytes 172036
  24.7 1.7 %copy-start.2 = (s32[96,112]{1,0:T(8,128)S(1)}, s32[96,112]{1,0:T(8,128)}, u32[]{:S(2)}) copy-start(s32[96,112]{1,0:T(8,128)} %constant.40.clone.refs_1_) | copy-start | bytes 129028
  24.7 1.7 %copy-start.8 = (s32[16,32]{1,0:T(8,128)S(1)}, s32[16,32]{1,0:T(8,128)}, u32[]{:S(2)}) copy-start(s32[16,32]{1,0:T(8,128)} %constant.44.clone.refs_5_) | copy-start | bytes 6148
  24.7 1.7 %copy-start.9 = (s32[16,32]{1,0:T(8,128)S(1)}, s32[16,32]{1,0:T(8,128)}, u32[]{:S(2)}) copy-start(s32[16,32]{1,0:T(8,128)} %constant.43.clone.refs_4_) | copy-start | bytes 6148
  24.7 1.7 %copy-start.10 = (s32[16,32]{1,0:T(8,128)S(1)}, s32[16,32]{1,0:T(8,128)}, u32[]{:S(2)}) copy-start(s32[16,32]{1,0:T(8,128)} %constant.42.clone.refs_3_) | copy-start | bytes 6148
  24.7 1.7 %copy-start.11 = (s32[16,32]{1,0:T(8,128)S(1)}, s32[16,32]{1,0:T(8,128)}, u32[]{:S(2)}) copy-start(s32[16,32]{1,0:T(8,128)} %constant.41.clone.refs_2_) | copy-start | bytes 6148
  24.7 1.7 %copy-start.12 = (f32[3,3,3]{2,1,0:T(4,128)S(1)}, f32[3,3,3]{2,1,0:T(4,128)}, u32[]{:S(2)}) copy-start(f32[3,3,3]{2,1,0:T(4,128)} %one_ref) | copy-start | bytes 328
  24.7 1.7 %copy-start.13 = (f32[3,3,3]{2,1,0:T(4,128)S(1)}, f32[3,3,3]{2,1,0:T(4,128)}, u32[]{:S(2)}) copy-start(f32[3,3,3]{2,1,0:T(4,128)} %two_ref) | copy-start | bytes 328
  97.5 20.9 %copy-start.7 = (bf16[32,128]{1,0:T(8,128)(2,1)S(1)}, bf16[32,128]{1,0:T(8,128)(2,1)}, u32[]{:S(2)}) copy-start(bf16[32,128]{1,0:T(8,128)(2,1)} %constant.45.clone.take_ref) | copy-start | bytes 24580
  118.4 8.4 %copy-start.3 = (bf16[128,128]{1,0:T(8,128)(2,1)S(1)}, bf16[128,128]{1,0:T(8,128)(2,1)}, u32[]{:S(2)}) copy-start(bf16[128,128]{1,0:T(8,128)(2,1)} %constant.46.clone.order_ref) | copy-start | bytes 98308
  118.4 11.2 %copy-start.5 = (bf16[64,64]{1,0:T(8,128)(2,1)S(1)}, bf16[64,64]{1,0:T(8,128)(2,1)}, u32[]{:S(2)}) copy-start(bf16[64,64]{1,0:T(8,128)(2,1)} %constant.47.clone.put_ref) | copy-start | bytes 24580
  118.8 10.8 %collective-permute-start.5 = (bf16[16,4224]{1,0:T(8,128)(2,1)S(1)}, bf16[16,4224]{1,0:T(8,128)(2,1)S(1)}, u32[]{:S(2)}, u32[]{:S(2)}) collective-permute-start(bf16[16,4224]{1,0:T(8,128)(2,1)S(1)} %get-tuple-element.64), channel_id=1, source_target_pairs={{0,1},{1,2},{2,3},{3,4},{4,5},{5,6},{6,7},{7,8},{8,9},{9,10},{10,1... | collective-permute-start | bytes 405512 | tf_op jit(solution)/shard_map/ppermute | solution.py:44
  122.4 8.1 %collective-permute-start.4 = (bf16[16,4224]{1,0:T(8,128)(2,1)S(1)}, bf16[16,4224]{1,0:T(8,128)(2,1)S(1)}, u32[]{:S(2)}, u32[]{:S(2)}) collective-permute-start(bf16[16,4224]{1,0:T(8,128)(2,1)S(1)} %get-tuple-element.56), channel_id=1, source_target_pairs={{1,0},{2,1},{3,2},{4,3},{5,4},{6,5},{7,6},{8,7},{9,8},{10,9},{11,1... | collective-permute-start | bytes 405512 | tf_op jit(solution)/shard_map/ppermute | solution.py:44
  129.6 0.9 copy-start.4

commit v12 on v11

--- a/solution.py
+++ b/solution.py
@@ -336,7 +336,7 @@
     firsts, lasts = call(
         edges_body, (shaped(n_sec * HALO, length),) * 2, [VMEM, VMEM], "edges", 8
     )(data, one_hot(pixels(0, 1) + pixels(last - 1, last), natural))
-    left, right = from_behind(lasts, "xy", 1), from_behind(firsts, "xy", -1)
+    left = from_behind(lasts, "xy", 1)
     side = n_sec * HALO
     inner, passed, aligned = call(
         interior_body,
@@ -346,6 +346,8 @@
         32,
         [pltpu.VMEM((2 * len(natural), length), BF16), pltpu.VMEM((2 * len(inner_pass), length), BF16)],
     )(keep, stencils[0], stencils[1], one_hot(rim[0] + rim[1] + inner_out, natural), data)
+    firsts, inner = lax.optimization_barrier((firsts, inner))
+    right = from_behind(firsts, "xy", -1)
     scratch = [pltpu.VMEM((4 * side, length), BF16)] * 2
     lower, upper = pixels(*range(cols // 2)), pixels(*range(cols // 2, cols))
     middle = len(inner_out) // 2

time: 133 us -> 135 us (1.015)
  waiting for transfers between devices: 6.32 us -> 7.69 us
    ppermute x6, waiting for transfers between devices: 6.32 us -> 7.69 us  [from_behind(): return lax.ppermute(value, axis, shift_pairs(lax.axis_size(axis), steps))]
  transfers between devices with their start and end apart: 6 -> 6, of which waited for: 3 -> 4; matrix products, arithmetic and copies ran while one was open for 0% -> 0% of each run, Pallas kernels for 6% -> 6%
where the time goes in v12:
time: 135 us; the launch traced here: 134 us
  blocking collectives  83.3 us (62%)
  starting transfers between devices  29.7 us (22%)
  Pallas kernels  11.7 us (9%)
  waiting for transfers between devices  7.69 us (6%)
    all_to_all x1, blocking collectives, body(): mine = lax.all_to_all(strip, 'xy', split_axis=0, concat_axis=0, tiled=True)  63 us
    ppermute x6, starting transfers between devices, from_behind(): return lax.ppermute(value, axis, shift_pairs(lax.axis_size(axis), steps))  29.7 us
    all_to_all x1, blocking collectives, body(): lax.all_to_all(spread, 'sec', split_axis=0, concat_axis=0, tiled=True)  20.3 us
    ppermute x6, waiting for transfers between devices, from_behind(): return lax.ppermute(value, axis, shift_pairs(lax.axis_size(axis), steps))  7.69 us
    pallas_call x1, Pallas kernels, body(): call(interior_body, (shaped(len(inner_out), per_sec * LANES), shaped(2 *...  2.77 us
  transfers between devices with their start and end apart: 6, of which 4 were waited for; matrix products, arithmetic and copies ran while one was open for 0% of the time, Pallas kernels for 6%

profile of v12, /device:TPU:24, one launch (start us, length us, event | category | flops | bytes accessed | tf_op | source)
XLA Modules:
  0.0 134.1 jit_solution(3166274872495343259)
XLA Ops:
  0.0 3.8 %collective-permute-start.1 = (s32[1,2,2]{2,1,0:T(2,128)}, s32[1,2,2]{2,1,0:T(2,128)S(1)}, u32[]{:S(2)}, u32[]{:S(2)}) collective-permute-start(s32[1,2,2]{2,1,0:T(2,128)} %refs_0_.4), channel_id=1, source_target_pairs={{0,1},{1,2},{2,3},{3,4},{4,5},{5,6},{6,7},{7,8},{8,9},{9,10},{10,1... | collective-permute-start | bytes 56 | tf_op jit(solution)/shard_map/ppermute | solution.py:44
  3.8 9.7 %collective-permute-start = (s32[1,2,2]{2,1,0:T(2,128)}, s32[1,2,2]{2,1,0:T(2,128)S(1)}, u32[]{:S(2)}, u32[]{:S(2)}) collective-permute-start(s32[1,2,2]{2,1,0:T(2,128)} %refs_0_.4), channel_id=1, source_target_pairs={{1,0},{2,1},{3,2},{4,3},{5,4},{6,5},{7,6},{8,7},{9,8},{10,9},{11,1... | collective-permute-start | bytes 56 | tf_op jit(solution)/shard_map/ppermute | solution.py:44
  13.6 0.0 copy-start
  13.6 1.2 copy-done
  14.8 0.1 stage.1.source_ref
  14.9 0.0 copy-start.14
  14.9 0.0 collective-permute-done.1.above_ref
  14.9 0.1 collective-permute-done.below_ref
  15.0 0.3 choose.1
  15.3 1.9 %collective-permute-start.2 = (bf16[1,512,512]{2,1,0:T(8,128)(2,1)S(1)}, bf16[1,512,512]{2,1,0:T(8,128)(2,1)S(1)}, u32[]{:S(2)}, u32[]{:S(2)}) collective-permute-start(bf16[1,512,512]{2,1,0:T(8,128)(2,1)S(1)} %get-tuple-element.51), channel_id=1, source_target_pairs={{0,1},{1,2},{2,3},{3,4},{4,5},{5,6},{6,7},{7,8},{8,9},{9,10},{10,1... | collective-permute-start | bytes 1572872 | tf_op jit(solution)/shard_map/ppermute | solution.py:44
  17.3 6.3 %collective-permute-start.3 = (bf16[1,512,512]{2,1,0:T(8,128)(2,1)S(1)}, bf16[1,512,512]{2,1,0:T(8,128)(2,1)S(1)}, u32[]{:S(2)}, u32[]{:S(2)}) collective-permute-start(bf16[1,512,512]{2,1,0:T(8,128)(2,1)S(1)} %get-tuple-element.55), channel_id=1, source_target_pairs={{1,0},{2,1},{3,2},{4,3},{5,4},{6,5},{7,6},{8,7},{9,8},{10,9},{11,1... | collective-permute-start | bytes 1572872 | tf_op jit(solution)/shard_map/ppermute | solution.py:44
  23.6 0.0 copy-start.6
  23.6 0.1 add_convert_fusion.keep_ref
  23.6 0.0 copy-done.14
  23.7 1.0 matrices.1.matrix_ref.refs_2_
  24.6 0.0 copy-done.6
  24.6 0.0 copy-start.1
  24.7 0.0 copy-start.2
  24.7 0.0 copy-start.8
  24.7 0.0 copy-start.9
  24.7 0.0 copy-start.10
  24.7 0.0 copy-start.11
  24.7 0.0 copy-start.12
  24.7 0.0 copy-start.13
  24.8 1.6 %warp.1.refs_3_ = bf16[64,4,16,128]{3,2,1,0:T(8,128)(2,1)S(1)} custom-call(s32[1,2,2]{2,1,0:T(2,128)S(1)} %copy-done.6, bf16[1,512,1024]{2,1,0:T(8,128)(2,1)S(1)} %stage.1.source_ref, bf16[2,2,512,512]{3,2,1,0:T(8,128)(2,1)S(1)} %matrices.1.matrix_ref.refs_2_), custom_call_target="tpu_custom_call" | custom-call | tf_op jit(solution)/shard_map/warp/pallas_call | solution.py:323
  26.3 0.0 copy-done.1
  26.4 0.0 copy-done.2
  26.4 0.0 copy-done.8
  26.4 0.0 copy-done.9
  26.4 0.0 copy-done.10
  26.4 0.0 copy-done.11
  26.4 0.0 copy-done.12
  26.4 0.0 copy-done.13
  26.4 1.0 stencils.1
  27.5 5.2 %collective-permute-done.2.refs_1_ = bf16[1,512,512]{2,1,0:T(8,128)(2,1)S(1)} collective-permute-done((bf16[1,512,512]{2,1,0:T(8,128)(2,1)S(1)}, bf16[1,512,512]{2,1,0:T(8,128)(2,1)S(1)}, u32[]{:S(2)}, u32[]{:S(2)}) %collective-permute-start.2) | collective-permute-done | bytes 524320 | tf_op jit(solution)/shard_map/ppermute | solution.py:44
  32.6 1.0 warp_above.1.refs_3_
  33.6 0.2 collective-permute-done.3.refs_1_
  33.8 1.0 warp_below.1
  34.8 63.0 %all_to_all.10 = bf16[64,4,16,128]{3,2,1,0:T(8,128)(2,1)S(1)} all-to-all(bf16[64,4,16,128]{3,2,1,0:T(8,128)(2,1)S(1)} %warp_below.1), channel_id=1, replica_groups=mesh['sec'=8,'xy'=64] {'xy'}, dimensions={0} | all-to-all | bytes 2097152 | tf_op jit(solution)/shard_map/all_to_all | solution.py:329
  97.8 0.1 spread.1
  97.9 0.0 copy-start.7
  97.9 20.3 %all_to_all.11.data_ref = bf16[8,33,16,128]{3,2,1,0:T(8,128)(2,1)S(1)} all-to-all(bf16[8,33,16,128]{3,2,1,0:T(8,128)(2,1)S(1)} %spread.1), channel_id=1, replica_groups=mesh['sec'=8,'xy'=64] {'sec'}, dimensions={0} | all-to-all | bytes 2162688 | tf_op jit(solution)/shard_map/all_to_all | solution.py:333
  118.2 0.0 copy-done.7
  118.2 0.0 copy-start.3
  118.2 0.0 copy-start.5
  118.2 0.4 edges.1
  118.6 4.0 %collective-permute-start.5 = (bf16[16,4224]{1,0:T(8,128)(2,1)S(1)}, bf16[16,4224]{1,0:T(8,128)(2,1)S(1)}, u32[]{:S(2)}, u32[]{:S(2)}) collective-permute-start(bf16[16,4224]{1,0:T(8,128)(2,1)S(1)} %get-tuple-element.68), channel_id=1, source_target_pairs={{0,1},{1,2},{2,3},{3,4},{4,5},{5,6},{6,7},{7,8},{8,9},{9,10},{10,1... | collective-permute-start | bytes 405512 | tf_op jit(solution)/shard_map/ppermute | solution.py:44
  122.6 0.0 copy-done.3
  122.6 2.8 %interior.1 = (bf16[96,4096]{1,0:T(8,128)(2,1)S(1)}, bf16[32,4224]{1,0:T(8,128)(2,1)S(1)}, bf16[32,4224]{1,0:T(8,128)(2,1)S(1)}) custom-call(f32[3,4224]{1,0:T(4,128)S(1)} %add_convert_fusion.keep_ref, bf16[336,256]{1,0:T(8,128)(2,1)S(1)} %get-tuple-element.59.first_ref, bf16[288,224]{1,0:T(8,128)(2,1)S(1)} %get-tuple-element.60.second_ref, ...), custom_call_target="tpu_custom_call" | custom-call | tf_op jit(solution)/shard_map/interior/pallas_call | solution.py:341
  125.4 0.0 copy-start.4
  125.4 3.9 %collective-permute-start.4 = (bf16[16,4224]{1,0:T(8,128)(2,1)S(1)}, bf16[16,4224]{1,0:T(8,128)(2,1)S(1)}, u32[]{:S(2)}, u32[]{:S(2)}) collective-permute-start(bf16[16,4224]{1,0:T(8,128)(2,1)S(1)} %get-tuple-element.62), channel_id=1, source_target_pairs={{1,0},{2,1},{3,2},{4,3},{5,4},{6,5},{7,6},{8,7},{9,8},{10,9},{11,1... | collective-permute-start | bytes 405512 | tf_op jit(solution)/shard_map/ppermute | solution.py:44
  129.3 0.0 collective-permute-done.5.halo_ref
  129.3 0.0 copy-done.5
  129.4 0.9 left.1.lower_ref
  130.2 2.2 %collective-permute-done.4.halo_ref = bf16[16,4224]{1,0:T(8,128)(2,1)S(1)} collective-permute-done((bf16[16,4224]{1,0:T(8,128)(2,1)S(1)}, bf16[16,4224]{1,0:T(8,128)(2,1)S(1)}, u32[]{:S(2)}, u32[]{:S(2)}) %collective-permute-start.4) | collective-permute-done | bytes 135200 | tf_op jit(solution)/shard_map/ppermute | solution.py:44
  132.4 0.0 copy-done.4
  132.4 1.6 %right.1 = bf16[8,16,4096]{2,1,0:T(8,128)(2,1)} custom-call(f32[3,4224]{1,0:T(4,128)S(1)} %add_convert_fusion.keep_ref, bf16[48,64]{1,0:T(8,128)(2,1)S(1)} %get-tuple-element.53.first_ref, bf16[48,64]{1,0:T(8,128)(2,1)S(1)} %get-tuple-element.54.second_ref, bf16[64,64]{1,0:T(8,128)(2,1)S(1)} %copy-done.4, ...), custom_call_target="tpu_custom_call" | custom-call | tf_op jit(solution)/shard_map/right/pallas_call | solution.py:359
  (2 shorter events, 0.0 us)
Async XLA Ops:
  0.0 14.9 %collective-permute-start.1 = (s32[1,2,2]{2,1,0:T(2,128)}, s32[1,2,2]{2,1,0:T(2,128)S(1)}, u32[]{:S(2)}, u32[]{:S(2)}) collective-permute-start(s32[1,2,2]{2,1,0:T(2,128)} %refs_0_.4), channel_id=1, source_target_pairs={{0,1},{1,2},{2,3},{3,4},{4,5},{5,6},{6,7},{7,8},{8,9},{9,10},{10,1... | collective-permute-start | bytes 56 | tf_op jit(solution)/shard_map/ppermute | solution.py:44
  3.8 11.2 %collective-permute-start = (s32[1,2,2]{2,1,0:T(2,128)}, s32[1,2,2]{2,1,0:T(2,128)S(1)}, u32[]{:S(2)}, u32[]{:S(2)}) collective-permute-start(s32[1,2,2]{2,1,0:T(2,128)} %refs_0_.4), channel_id=1, source_target_pairs={{1,0},{2,1},{3,2},{4,3},{5,4},{6,5},{7,6},{8,7},{9,8},{10,9},{11,1... | collective-permute-start | bytes 56 | tf_op jit(solution)/shard_map/ppermute | solution.py:44
  13.6 1.2 copy-start
  14.9 8.8 %copy-start.14 = (f32[1,2,2]{2,1,0:T(2,128)S(1)}, f32[1,2,2]{2,1,0:T(2,128)}, u32[]{:S(2)}) copy-start(f32[1,2,2]{2,1,0:T(2,128)} %fraction_ref) | copy-start | bytes 52
  15.3 17.3 %collective-permute-start.2 = (bf16[1,512,512]{2,1,0:T(8,128)(2,1)S(1)}, bf16[1,512,512]{2,1,0:T(8,128)(2,1)S(1)}, u32[]{:S(2)}, u32[]{:S(2)}) collective-permute-start(bf16[1,512,512]{2,1,0:T(8,128)(2,1)S(1)} %get-tuple-element.51), channel_id=1, source_target_pairs={{0,1},{1,2},{2,3},{3,4},{4,5},{5,6},{6,7},{7,8},{8,9},{9,10},{10,1... | collective-permute-start | bytes 1572872 | tf_op jit(solution)/shard_map/ppermute | solution.py:44
  17.3 16.6 %collective-permute-start.3 = (bf16[1,512,512]{2,1,0:T(8,128)(2,1)S(1)}, bf16[1,512,512]{2,1,0:T(8,128)(2,1)S(1)}, u32[]{:S(2)}, u32[]{:S(2)}) collective-permute-start(bf16[1,512,512]{2,1,0:T(8,128)(2,1)S(1)} %get-tuple-element.55), channel_id=1, source_target_pairs={{1,0},{2,1},{3,2},{4,3},{5,4},{6,5},{7,6},{8,7},{9,8},{10,9},{11,1... | collective-permute-start | bytes 1572872 | tf_op jit(solution)/shard_map/ppermute | solution.py:44
  23.6 1.1 copy-start.6
  24.6 1.7 %copy-start.1 = (s32[112,128]{1,0:T(8,128)S(1)}, s32[112,128]{1,0:T(8,128)}, u32[]{:S(2)}) copy-start(s32[112,128]{1,0:T(8,128)} %constant.39.clone.refs_0_) | copy-start | bytes 172036
  24.7 1.7 %copy-start.2 = (s32[96,112]{1,0:T(8,128)S(1)}, s32[96,112]{1,0:T(8,128)}, u32[]{:S(2)}) copy-start(s32[96,112]{1,0:T(8,128)} %constant.40.clone.refs_1_) | copy-start | bytes 129028
  24.7 1.7 %copy-start.8 = (s32[16,32]{1,0:T(8,128)S(1)}, s32[16,32]{1,0:T(8,128)}, u32[]{:S(2)}) copy-start(s32[16,32]{1,0:T(8,128)} %constant.44.clone.refs_5_) | copy-start | bytes 6148
  24.7 1.7 %copy-start.9 = (s32[16,32]{1,0:T(8,128)S(1)}, s32[16,32]{1,0:T(8,128)}, u32[]{:S(2)}) copy-start(s32[16,32]{1,0:T(8,128)} %constant.43.clone.refs_4_) | copy-start | bytes 6148
  24.7 1.7 %copy-start.10 = (s32[16,32]{1,0:T(8,128)S(1)}, s32[16,32]{1,0:T(8,128)}, u32[]{:S(2)}) copy-start(s32[16,32]{1,0:T(8,128)} %constant.42.clone.refs_3_) | copy-start | bytes 6148
  24.7 1.7 %copy-start.11 = (s32[16,32]{1,0:T(8,128)S(1)}, s32[16,32]{1,0:T(8,128)}, u32[]{:S(2)}) copy-start(s32[16,32]{1,0:T(8,128)} %constant.41.clone.refs_2_) | copy-start | bytes 6148
  24.7 1.7 %copy-start.12 = (f32[3,3,3]{2,1,0:T(4,128)S(1)}, f32[3,3,3]{2,1,0:T(4,128)}, u32[]{:S(2)}) copy-start(f32[3,3,3]{2,1,0:T(4,128)} %one_ref) | copy-start | bytes 328
  24.7 1.7 %copy-start.13 = (f32[3,3,3]{2,1,0:T(4,128)S(1)}, f32[3,3,3]{2,1,0:T(4,128)}, u32[]{:S(2)}) copy-start(f32[3,3,3]{2,1,0:T(4,128)} %two_ref) | copy-start | bytes 328
  97.9 20.3 %copy-start.7 = (bf16[32,128]{1,0:T(8,128)(2,1)S(1)}, bf16[32,128]{1,0:T(8,128)(2,1)}, u32[]{:S(2)}) copy-start(bf16[32,128]{1,0:T(8,128)(2,1)} %constant.45.clone.take_ref) | copy-start | bytes 24580
  118.2 4.4 %copy-start.3 = (bf16[128,128]{1,0:T(8,128)(2,1)S(1)}, bf16[128,128]{1,0:T(8,128)(2,1)}, u32[]{:S(2)}) copy-start(bf16[128,128]{1,0:T(8,128)(2,1)} %constant.46.clone.order_ref) | copy-start | bytes 98308
  118.2 11.2 %copy-start.5 = (bf16[64,64]{1,0:T(8,128)(2,1)S(1)}, bf16[64,64]{1,0:T(8,128)(2,1)}, u32[]{:S(2)}) copy-start(bf16[64,64]{1,0:T(8,128)(2,1)} %constant.47.clone.put_ref) | copy-start | bytes 24580
  118.6 10.8 %collective-permute-start.5 = (bf16[16,4224]{1,0:T(8,128)(2,1)S(1)}, bf16[16,4224]{1,0:T(8,128)(2,1)S(1)}, u32[]{:S(2)}, u32[]{:S(2)}) collective-permute-start(bf16[16,4224]{1,0:T(8,128)(2,1)S(1)} %get-tuple-element.68), channel_id=1, source_target_pairs={{0,1},{1,2},{2,3},{3,4},{4,5},{5,6},{6,7},{7,8},{8,9},{9,10},{10,1... | collective-permute-start | bytes 405512 | tf_op jit(solution)/shard_map/ppermute | solution.py:44
  125.4 7.1 %copy-start.4 = (bf16[64,64]{1,0:T(8,128)(2,1)S(1)}, bf16[64,64]{1,0:T(8,128)(2,1)}, u32[]{:S(2)}) copy-start(bf16[64,64]{1,0:T(8,128)(2,1)} %constant.48.clone.put_ref) | copy-start | bytes 24580
  125.4 7.0 %collective-permute-start.4 = (bf16[16,4224]{1,0:T(8,128)(2,1)S(1)}, bf16[16,4224]{1,0:T(8,128)(2,1)S(1)}, u32[]{:S(2)}, u32[]{:S(2)}) collective-permute-start(bf16[16,4224]{1,0:T(8,128)(2,1)S(1)} %get-tuple-element.62), channel_id=1, source_target_pairs={{1,0},{2,1},{3,2},{4,3},{5,4},{6,5},{7,6},{8,7},{9,8},{10,9},{11,1... | collective-permute-start | bytes 405512 | tf_op jit(solution)/shard_map/ppermute | solution.py:44

commit v13 on v11

--- a/solution.py
+++ b/solution.py
@@ -174,9 +174,11 @@
 def edges_body(data_ref, take_ref, first_ref, last_ref):
     sections, chunks, cols, lanes = data_ref.shape
     side = first_ref.shape[0]
-    for chunk in range(chunks):
-        rim = dot(take_ref[...], data_ref[:, chunk].reshape(sections * cols, lanes)).astype(BF16)
-        where = slice(chunk * lanes, (chunk + 1) * lanes)
+    for start in range(0, chunks, 2):
+        taken = range(start, min(start + 2, chunks))
+        blocks = [data_ref[:, chunk].reshape(sections * cols, lanes) for chunk in taken]
+        rim = dot(take_ref[...], jnp.concatenate(blocks, axis=1)).astype(BF16)
+        where = slice(start * lanes, (start + len(blocks)) * lanes)
         first_ref[:, where] = rim[:side]
         last_ref[:, where] = rim[side:]
 

time: 133 us -> 132 us (level)
  transfers between devices with their start and end apart: 6 -> 6, of which waited for: 3 -> 4; matrix products, arithmetic and copies ran while one was open for 0% -> 0% of each run, Pallas kernels for 6% -> 6%
where the time goes in v13:
time: 132 us; the launch traced here: 131 us
  blocking collectives  83.4 us (63%)
  starting transfers between devices  29.7 us (22%)
  Pallas kernels  10.7 us (8%)
  waiting for transfers between devices  5.58 us (4%)
    all_to_all x1, blocking collectives, body(): mine = lax.all_to_all(strip, 'xy', split_axis=0, concat_axis=0, tiled=True)  62.9 us
    ppermute x6, starting transfers between devices, from_behind(): return lax.ppermute(value, axis, shift_pairs(lax.axis_size(axis), steps))  29.7 us
    all_to_all x1, blocking collectives, body(): lax.all_to_all(spread, 'sec', split_axis=0, concat_axis=0, tiled=True)  20.5 us
    ppermute x6, waiting for transfers between devices, from_behind(): return lax.ppermute(value, axis, shift_pairs(lax.axis_size(axis), steps))  5.58 us
    pallas_call x1, Pallas kernels, body(): call(interior_body, (shaped(len(inner_out), per_sec * LANES), shaped(2 *...  2.78 us
  transfers between devices with their start and end apart: 6, of which 4 were waited for; matrix products, arithmetic and copies ran while one was open for 0% of the time, Pallas kernels for 6%

profile of v13, /device:TPU:24, one launch (start us, length us, event | category | flops | bytes accessed | tf_op | source)
XLA Modules:
  0.0 131.2 jit_solution(10213559266914766990)
XLA Ops:
  0.0 3.8 %collective-permute-start.1 = (s32[1,2,2]{2,1,0:T(2,128)}, s32[1,2,2]{2,1,0:T(2,128)S(1)}, u32[]{:S(2)}, u32[]{:S(2)}) collective-permute-start(s32[1,2,2]{2,1,0:T(2,128)} %refs_0_.4), channel_id=1, source_target_pairs={{0,1},{1,2},{2,3},{3,4},{4,5},{5,6},{6,7},{7,8},{8,9},{9,10},{10,1... | collective-permute-start | bytes 56 | tf_op jit(solution)/shard_map/ppermute | solution.py:44
  3.8 9.7 %collective-permute-start = (s32[1,2,2]{2,1,0:T(2,128)}, s32[1,2,2]{2,1,0:T(2,128)S(1)}, u32[]{:S(2)}, u32[]{:S(2)}) collective-permute-start(s32[1,2,2]{2,1,0:T(2,128)} %refs_0_.4), channel_id=1, source_target_pairs={{1,0},{2,1},{3,2},{4,3},{5,4},{6,5},{7,6},{8,7},{9,8},{10,9},{11,1... | collective-permute-start | bytes 56 | tf_op jit(solution)/shard_map/ppermute | solution.py:44
  13.6 0.0 copy-start
  13.6 1.2 copy-done
  14.8 0.1 stage.1.source_ref
  14.9 0.0 copy-start.14
  14.9 0.0 collective-permute-done.1.above_ref
  14.9 0.1 collective-permute-done.below_ref
  15.0 0.3 choose.1
  15.3 1.9 %collective-permute-start.2 = (bf16[1,512,512]{2,1,0:T(8,128)(2,1)S(1)}, bf16[1,512,512]{2,1,0:T(8,128)(2,1)S(1)}, u32[]{:S(2)}, u32[]{:S(2)}) collective-permute-start(bf16[1,512,512]{2,1,0:T(8,128)(2,1)S(1)} %get-tuple-element.49), channel_id=1, source_target_pairs={{0,1},{1,2},{2,3},{3,4},{4,5},{5,6},{6,7},{7,8},{8,9},{9,10},{10,1... | collective-permute-start | bytes 1572872 | tf_op jit(solution)/shard_map/ppermute | solution.py:44
  17.3 6.3 %collective-permute-start.3 = (bf16[1,512,512]{2,1,0:T(8,128)(2,1)S(1)}, bf16[1,512,512]{2,1,0:T(8,128)(2,1)S(1)}, u32[]{:S(2)}, u32[]{:S(2)}) collective-permute-start(bf16[1,512,512]{2,1,0:T(8,128)(2,1)S(1)} %get-tuple-element.53), channel_id=1, source_target_pairs={{1,0},{2,1},{3,2},{4,3},{5,4},{6,5},{7,6},{8,7},{9,8},{10,9},{11,1... | collective-permute-start | bytes 1572872 | tf_op jit(solution)/shard_map/ppermute | solution.py:44
  23.6 0.0 copy-start.6
  23.6 0.1 add_convert_fusion.keep_ref
  23.6 0.0 copy-done.14
  23.7 1.0 matrices.1.matrix_ref.refs_2_
  24.6 0.0 copy-done.6
  24.6 0.0 copy-start.1
  24.7 0.0 copy-start.2
  24.7 0.0 copy-start.8
  24.7 0.0 copy-start.9
  24.7 0.0 copy-start.10
  24.7 0.0 copy-start.11
  24.7 0.0 copy-start.12
  24.7 0.0 copy-start.13
  24.8 1.6 %warp.1.refs_3_ = bf16[64,4,16,128]{3,2,1,0:T(8,128)(2,1)S(1)} custom-call(s32[1,2,2]{2,1,0:T(2,128)S(1)} %copy-done.6, bf16[1,512,1024]{2,1,0:T(8,128)(2,1)S(1)} %stage.1.source_ref, bf16[2,2,512,512]{3,2,1,0:T(8,128)(2,1)S(1)} %matrices.1.matrix_ref.refs_2_), custom_call_target="tpu_custom_call" | custom-call | tf_op jit(solution)/shard_map/warp/pallas_call | solution.py:325
  26.3 0.0 copy-done.1
  26.4 0.0 copy-done.2
  26.4 0.0 copy-done.8
  26.4 0.0 copy-done.9
  26.4 0.0 copy-done.10
  26.4 0.0 copy-done.11
  26.4 0.0 copy-done.12
  26.4 0.0 copy-done.13
  26.4 1.0 stencils.1
  27.5 5.2 %collective-permute-done.2.refs_1_ = bf16[1,512,512]{2,1,0:T(8,128)(2,1)S(1)} collective-permute-done((bf16[1,512,512]{2,1,0:T(8,128)(2,1)S(1)}, bf16[1,512,512]{2,1,0:T(8,128)(2,1)S(1)}, u32[]{:S(2)}, u32[]{:S(2)}) %collective-permute-start.2) | collective-permute-done | bytes 524320 | tf_op jit(solution)/shard_map/ppermute | solution.py:44
  32.6 1.0 warp_above.1.refs_3_
  33.6 0.2 collective-permute-done.3.refs_1_
  33.8 0.1 warp_below.1
  34.0 62.9 %all_to_all.10 = bf16[64,4,16,128]{3,2,1,0:T(8,128)(2,1)S(1)} all-to-all(bf16[64,4,16,128]{3,2,1,0:T(8,128)(2,1)S(1)} %warp_below.1), channel_id=1, replica_groups=mesh['sec'=8,'xy'=64] {'xy'}, dimensions={0} | all-to-all | bytes 2097152 | tf_op jit(solution)/shard_map/all_to_all | solution.py:331
  96.8 0.1 spread.1
  96.9 0.0 copy-start.7
  96.9 20.5 %all_to_all.11.data_ref = bf16[8,33,16,128]{3,2,1,0:T(8,128)(2,1)S(1)} all-to-all(bf16[8,33,16,128]{3,2,1,0:T(8,128)(2,1)S(1)} %spread.1), channel_id=1, replica_groups=mesh['sec'=8,'xy'=64] {'sec'}, dimensions={0} | all-to-all | bytes 2162688 | tf_op jit(solution)/shard_map/all_to_all | solution.py:335
  117.5 0.0 copy-done.7
  117.5 0.0 copy-start.3
  117.5 0.0 copy-start.5
  117.5 0.3 edges.1
  117.8 4.7 %collective-permute-start.5 = (bf16[16,4224]{1,0:T(8,128)(2,1)S(1)}, bf16[16,4224]{1,0:T(8,128)(2,1)S(1)}, u32[]{:S(2)}, u32[]{:S(2)}) collective-permute-start(bf16[16,4224]{1,0:T(8,128)(2,1)S(1)} %get-tuple-element.64), channel_id=1, source_target_pairs={{0,1},{1,2},{2,3},{3,4},{4,5},{5,6},{6,7},{7,8},{8,9},{9,10},{10,1... | collective-permute-start | bytes 405512 | tf_op jit(solution)/shard_map/ppermute | solution.py:44
  122.5 3.3 %collective-permute-start.4 = (bf16[16,4224]{1,0:T(8,128)(2,1)S(1)}, bf16[16,4224]{1,0:T(8,128)(2,1)S(1)}, u32[]{:S(2)}, u32[]{:S(2)}) collective-permute-start(bf16[16,4224]{1,0:T(8,128)(2,1)S(1)} %get-tuple-element.56), channel_id=1, source_target_pairs={{1,0},{2,1},{3,2},{4,3},{5,4},{6,5},{7,6},{8,7},{9,8},{10,9},{11,1... | collective-permute-start | bytes 405512 | tf_op jit(solution)/shard_map/ppermute | solution.py:44
  125.7 0.0 copy-done.3
  125.7 2.8 %interior.1 = (bf16[96,4096]{1,0:T(8,128)(2,1)S(1)}, bf16[32,4224]{1,0:T(8,128)(2,1)S(1)}, bf16[32,4224]{1,0:T(8,128)(2,1)S(1)}) custom-call(f32[3,4224]{1,0:T(4,128)S(1)} %add_convert_fusion.keep_ref, bf16[336,256]{1,0:T(8,128)(2,1)S(1)} %get-tuple-element.57.first_ref, bf16[288,224]{1,0:T(8,128)(2,1)S(1)} %get-tuple-element.58.second_ref, ...), custom_call_target="tpu_custom_call" | custom-call | tf_op jit(solution)/shard_map/interior/pallas_call | solution.py:343
  128.5 0.0 copy-start.4
  128.5 0.0 collective-permute-done.5.halo_ref
  128.6 0.0 copy-done.5
  128.6 0.9 left.1.lower_ref
  129.4 0.1 collective-permute-done.4.halo_ref
  129.5 0.0 copy-done.4
  129.5 1.6 %right.1 = bf16[8,16,4096]{2,1,0:T(8,128)(2,1)} custom-call(f32[3,4224]{1,0:T(4,128)S(1)} %add_convert_fusion.keep_ref, bf16[48,64]{1,0:T(8,128)(2,1)S(1)} %get-tuple-element.51.first_ref, bf16[48,64]{1,0:T(8,128)(2,1)S(1)} %get-tuple-element.52.second_ref, bf16[64,64]{1,0:T(8,128)(2,1)S(1)} %copy-done.4, ...), custom_call_target="tpu_custom_call" | custom-call | tf_op jit(solution)/shard_map/right/pallas_call | solution.py:359
  (2 shorter events, 0.0 us)
Async XLA Ops:
  0.0 14.9 %collective-permute-start.1 = (s32[1,2,2]{2,1,0:T(2,128)}, s32[1,2,2]{2,1,0:T(2,128)S(1)}, u32[]{:S(2)}, u32[]{:S(2)}) collective-permute-start(s32[1,2,2]{2,1,0:T(2,128)} %refs_0_.4), channel_id=1, source_target_pairs={{0,1},{1,2},{2,3},{3,4},{4,5},{5,6},{6,7},{7,8},{8,9},{9,10},{10,1... | collective-permute-start | bytes 56 | tf_op jit(solution)/shard_map/ppermute | solution.py:44
  3.8 11.2 %collective-permute-start = (s32[1,2,2]{2,1,0:T(2,128)}, s32[1,2,2]{2,1,0:T(2,128)S(1)}, u32[]{:S(2)}, u32[]{:S(2)}) collective-permute-start(s32[1,2,2]{2,1,0:T(2,128)} %refs_0_.4), channel_id=1, source_target_pairs={{1,0},{2,1},{3,2},{4,3},{5,4},{6,5},{7,6},{8,7},{9,8},{10,9},{11,1... | collective-permute-start | bytes 56 | tf_op jit(solution)/shard_map/ppermute | solution.py:44
  13.6 1.2 copy-start
  14.9 8.8 %copy-start.14 = (f32[1,2,2]{2,1,0:T(2,128)S(1)}, f32[1,2,2]{2,1,0:T(2,128)}, u32[]{:S(2)}) copy-start(f32[1,2,2]{2,1,0:T(2,128)} %fraction_ref) | copy-start | bytes 52
  15.3 17.3 %collective-permute-start.2 = (bf16[1,512,512]{2,1,0:T(8,128)(2,1)S(1)}, bf16[1,512,512]{2,1,0:T(8,128)(2,1)S(1)}, u32[]{:S(2)}, u32[]{:S(2)}) collective-permute-start(bf16[1,512,512]{2,1,0:T(8,128)(2,1)S(1)} %get-tuple-element.49), channel_id=1, source_target_pairs={{0,1},{1,2},{2,3},{3,4},{4,5},{5,6},{6,7},{7,8},{8,9},{9,10},{10,1... | collective-permute-start | bytes 1572872 | tf_op jit(solution)/shard_map/ppermute | solution.py:44
  17.3 16.6 %collective-permute-start.3 = (bf16[1,512,512]{2,1,0:T(8,128)(2,1)S(1)}, bf16[1,512,512]{2,1,0:T(8,128)(2,1)S(1)}, u32[]{:S(2)}, u32[]{:S(2)}) collective-permute-start(bf16[1,512,512]{2,1,0:T(8,128)(2,1)S(1)} %get-tuple-element.53), channel_id=1, source_target_pairs={{1,0},{2,1},{3,2},{4,3},{5,4},{6,5},{7,6},{8,7},{9,8},{10,9},{11,1... | collective-permute-start | bytes 1572872 | tf_op jit(solution)/shard_map/ppermute | solution.py:44
  23.6 1.1 copy-start.6
  24.6 1.7 %copy-start.1 = (s32[112,128]{1,0:T(8,128)S(1)}, s32[112,128]{1,0:T(8,128)}, u32[]{:S(2)}) copy-start(s32[112,128]{1,0:T(8,128)} %constant.39.clone.refs_0_) | copy-start | bytes 172036
  24.7 1.7 %copy-start.2 = (s32[96,112]{1,0:T(8,128)S(1)}, s32[96,112]{1,0:T(8,128)}, u32[]{:S(2)}) copy-start(s32[96,112]{1,0:T(8,128)} %constant.40.clone.refs_1_) | copy-start | bytes 129028
  24.7 1.7 %copy-start.8 = (s32[16,32]{1,0:T(8,128)S(1)}, s32[16,32]{1,0:T(8,128)}, u32[]{:S(2)}) copy-start(s32[16,32]{1,0:T(8,128)} %constant.44.clone.refs_5_) | copy-start | bytes 6148
  24.7 1.7 %copy-start.9 = (s32[16,32]{1,0:T(8,128)S(1)}, s32[16,32]{1,0:T(8,128)}, u32[]{:S(2)}) copy-start(s32[16,32]{1,0:T(8,128)} %constant.43.clone.refs_4_) | copy-start | bytes 6148
  24.7 1.7 %copy-start.10 = (s32[16,32]{1,0:T(8,128)S(1)}, s32[16,32]{1,0:T(8,128)}, u32[]{:S(2)}) copy-start(s32[16,32]{1,0:T(8,128)} %constant.42.clone.refs_3_) | copy-start | bytes 6148
  24.7 1.7 %copy-start.11 = (s32[16,32]{1,0:T(8,128)S(1)}, s32[16,32]{1,0:T(8,128)}, u32[]{:S(2)}) copy-start(s32[16,32]{1,0:T(8,128)} %constant.41.clone.refs_2_) | copy-start | bytes 6148
  24.7 1.7 %copy-start.12 = (f32[3,3,3]{2,1,0:T(4,128)S(1)}, f32[3,3,3]{2,1,0:T(4,128)}, u32[]{:S(2)}) copy-start(f32[3,3,3]{2,1,0:T(4,128)} %one_ref) | copy-start | bytes 328
  24.7 1.7 %copy-start.13 = (f32[3,3,3]{2,1,0:T(4,128)S(1)}, f32[3,3,3]{2,1,0:T(4,128)}, u32[]{:S(2)}) copy-start(f32[3,3,3]{2,1,0:T(4,128)} %two_ref) | copy-start | bytes 328
  96.9 20.6 %copy-start.7 = (bf16[32,128]{1,0:T(8,128)(2,1)S(1)}, bf16[32,128]{1,0:T(8,128)(2,1)}, u32[]{:S(2)}) copy-start(bf16[32,128]{1,0:T(8,128)(2,1)} %constant.45.clone.take_ref) | copy-start | bytes 24580
  117.5 8.3 %copy-start.3 = (bf16[128,128]{1,0:T(8,128)(2,1)S(1)}, bf16[128,128]{1,0:T(8,128)(2,1)}, u32[]{:S(2)}) copy-start(bf16[128,128]{1,0:T(8,128)(2,1)} %constant.46.clone.order_ref) | copy-start | bytes 98308
  117.5 11.1 %copy-start.5 = (bf16[64,64]{1,0:T(8,128)(2,1)S(1)}, bf16[64,64]{1,0:T(8,128)(2,1)}, u32[]{:S(2)}) copy-start(bf16[64,64]{1,0:T(8,128)(2,1)} %constant.47.clone.put_ref) | copy-start | bytes 24580
  117.8 10.8 %collective-permute-start.5 = (bf16[16,4224]{1,0:T(8,128)(2,1)S(1)}, bf16[16,4224]{1,0:T(8,128)(2,1)S(1)}, u32[]{:S(2)}, u32[]{:S(2)}) collective-permute-start(bf16[16,4224]{1,0:T(8,128)(2,1)S(1)} %get-tuple-element.64), channel_id=1, source_target_pairs={{0,1},{1,2},{2,3},{3,4},{4,5},{5,6},{6,7},{7,8},{8,9},{9,10},{10,1... | collective-permute-start | bytes 405512 | tf_op jit(solution)/shard_map/ppermute | solution.py:44
  122.5 7.0 %collective-permute-start.4 = (bf16[16,4224]{1,0:T(8,128)(2,1)S(1)}, bf16[16,4224]{1,0:T(8,128)(2,1)S(1)}, u32[]{:S(2)}, u32[]{:S(2)}) collective-permute-start(bf16[16,4224]{1,0:T(8,128)(2,1)S(1)} %get-tuple-element.56), channel_id=1, source_target_pairs={{1,0},{2,1},{3,2},{4,3},{5,4},{6,5},{7,6},{8,7},{9,8},{10,9},{11,1... | collective-permute-start | bytes 405512 | tf_op jit(solution)/shard_map/ppermute | solution.py:44
  128.5 1.0 copy-start.4
